TPU v7x, 32 devices: a whole 2x2x4 slice. The times are simulated.
32 devices in a mesh: blk: 16 (over z, y, core), sub: 2 (over x).
Axes of the slice: x: 2, y: 2, z: 4, core: 2. Of those that a mesh axis runs over, the one named last changes fastest.
Arguments:
- correlation: float32 [64, 6, 128, 128], P(('blk', 'sub')), may hold values from -3 to 3, as said below
- factor: float32 [64, 6, 128, 128], P(('blk', 'sub')), may hold values from -2 to 2, as said below
- pattern: int32 [64, 6], replicated, may hold values from 0 to 63, as said below
Outputs:
- refined: float32 [64, 6, 128, 128], P(('blk', 'sub'))
- correction: float32 [64, 6, 128, 128], P(('blk', 'sub'))
Inputs may be any that keep to these rules, and one draw needn't show every extreme that they name: `pattern`: slot 0 of tile row i is i itself; the other 5 slots name all but one of the tile rows i - 3 to i + 3 other than i, taken modulo 64, in increasing offset. `correlation`: slot 0 of each tile row holds the diagonal tile. `factor`: slot 0 of each tile row holds the diagonal tile.
All inputs are finite; a program needn't handle non-finite values.
Results may differ from a plain program's by a relative error of at most 0.0003.
Values sent between devices are 32-bit elements; how exact they have to be, the bound alone decides.
No kernel may reach another device: no remote copies, remote signals or barrier semaphores. Data moves between devices by JAX's collectives and lax.ppermute only.
A program may use at most 64 MiB of HBM per device.

v0:
```python
import jax
import jax.numpy as jnp
from jax import lax
from jax.sharding import PartitionSpec as P

REACH = 3


def passed_along(value, axis, by):
    size = lax.axis_size(axis)
    return lax.ppermute(value, axis, [(i, (i + by) % size) for i in range(size)])


def select_tiles(window_flat, pattern, start_row, rows_wanted, columns_wanted):
    total_rows = pattern.shape[0]
    width_slots = pattern.shape[1]
    zero_index = window_flat.shape[0] - 1
    window_pos = (rows_wanted - start_row + REACH) % total_rows
    matches = pattern[rows_wanted] == columns_wanted[..., None]
    slot_index = jnp.argmax(matches, axis=-1)
    present = jnp.any(matches, axis=-1)
    flat_index = jnp.where(present, window_pos * width_slots + slot_index, zero_index)
    return window_flat[flat_index]


def neighbour_window(tiles):
    rows_here = tiles.shape[0]
    tile_size = tiles.shape[2]
    edge_count = REACH - rows_here
    nearby = [passed_along(tiles, ("blk", "sub"), offset) for offset in (1, -1)]
    sources = ((2, tiles[rows_here - edge_count :]), (-2, tiles[:edge_count]))
    further = [passed_along(source, ("blk", "sub"), offset) for offset, source in sources]
    pieces = [further[0], nearby[0], tiles, nearby[1], further[1]]
    flat_pieces = [piece.reshape((-1, tile_size, tile_size)) for piece in pieces]
    flat_pieces.append(jnp.zeros((1, tile_size, tile_size), tiles.dtype))
    return jnp.concatenate(flat_pieces, axis=0)


def body(correlation, factor, pattern):
    rows_here = correlation.shape[0]
    start_row = lax.axis_index(("blk", "sub")) * rows_here
    total_rows = pattern.shape[0]
    local_rows = start_row + jnp.arange(rows_here, dtype=jnp.int32)
    own_cols = lax.dynamic_slice_in_dim(pattern, start_row, rows_here, 0)
    width_slots = own_cols.shape[1]
    grid_shape = (rows_here, width_slots, width_slots)
    column_rows = jnp.broadcast_to(own_cols[:, None, :], grid_shape)
    column_want = jnp.broadcast_to(own_cols[:, :, None], grid_shape)
    offsets = jnp.arange(-REACH, REACH + 1, dtype=jnp.int32)
    candidates = (local_rows[:, None] + offsets[None, :]) % total_rows
    candidate_shape = (rows_here, width_slots, offsets.shape[0])
    candidate_rows = jnp.broadcast_to(candidates[:, None, :], candidate_shape)
    candidate_want = jnp.broadcast_to(own_cols[:, :, None], candidate_shape)
    diagonal_want = jnp.broadcast_to(local_rows[:, None], candidates.shape)
    identity = jnp.eye(correlation.shape[2], dtype=jnp.float32)
    factor_window = neighbour_window(factor)
    chosen = select_tiles(factor_window, pattern, start_row, column_rows, column_want)
    product = jnp.einsum("tqab,tpqbc->tpac", correlation, chosen, precision=lax.Precision.HIGHEST)
    product_window = neighbour_window(product)
    left_side = select_tiles(factor_window, pattern, start_row, candidates, diagonal_want)
    right_side = select_tiles(product_window, pattern, start_row, candidate_rows, candidate_want)
    gram_tiles = jnp.einsum(
        "toba,tpobc->tpac", left_side, right_side, precision=lax.Precision.HIGHEST
    )
    correction = (-gram_tiles).at[:, 0].add(identity)
    correction_window = neighbour_window(correction)
    picked = select_tiles(correction_window, pattern, start_row, column_rows, column_want)
    update = jnp.einsum("tqab,tpqbc->tpac", factor, picked, precision=lax.Precision.HIGHEST)
    factor = factor + 0.5 * update
    return (factor, correction)


def solution(mesh):
    in_specs = (P(("blk", "sub"), None, None, None), P(("blk", "sub"), None, None, None), P())
    out_specs = (P(("blk", "sub"), None, None, None), P(("blk", "sub"), None, None, None))
    return jax.shard_map(body, mesh=mesh, in_specs=in_specs, out_specs=out_specs, check_vma=False)
```

profile of v0, /device:TPU:1, one launch (start us, length us, event | category | flops | bytes accessed | tf_op | source)
XLA Modules:
  0.0 162.5 jit_solution(10884120070021101743)
XLA Ops:
  0.7 2.7 %collective-permute-start.2 = (f32[2,6,128,128]{3,2,1,0:T(8,128)}, f32[2,6,128,128]{3,2,1,0:T(8,128)S(1)}, u32[]{:S(2)}, u32[]{:S(2)}) collective-permute-start(f32[2,6,128,128]{3,2,1,0:T(8,128)} %param.6), channel_id=1, source_target_pairs={{0,31},{1,0},{2,1},{3,2},{4,3},{5,4},{6,5},{7,6},{8,7},{9,8},{10,9... | collective-permute-start | bytes 2359304 | tf_op jit(solution)/shard_map/ppermute | solution.py:11
  3.3 2.0 %fusion.19 = (f32[1,6,128,128]{3,2,1,0:T(8,128)}, f32[1,6,128,128]{3,2,1,0:T(8,128)}) fusion(f32[2,6,128,128]{3,2,1,0:T(8,128)} %param.6), kind=kLoop, calls=%fused_computation.89 | loop fusion | bytes 1572864 | tf_op jit(solution)/shard_map/slice | solution.py:31
  5.3 3.8 %collective-permute-start.3 = (f32[1,6,128,128]{3,2,1,0:T(8,128)}, f32[1,6,128,128]{3,2,1,0:T(8,128)S(1)}, u32[]{:S(2)}, u32[]{:S(2)}) collective-permute-start(f32[1,6,128,128]{3,2,1,0:T(8,128)} %get-tuple-element.39), channel_id=1, source_target_pairs={{0,30},{1,31},{2,0},{3,1},{4,2},{5,3},{6,4},{7,5},{8,6},{9,7},{10,... | collective-permute-start | bytes 1179656 | tf_op jit(solution)/shard_map/ppermute | solution.py:11
  9.4 0.8 compare_and_fusion
  10.3 0.8 copy.26
  15.1 0.6 gather_fusion.2
  15.9 0.7 fusion.15
  16.7 0.6 iota_reduce_fusion.1
  18.1 0.6 iota_reduce_fusion
  18.7 0.8 bitcast_dynamic-update-slice_fusion.5
  19.5 18.3 %collective-permute-done.1 = f32[2,6,128,128]{3,2,1,0:T(8,128)} collective-permute-done((f32[2,6,128,128]{3,2,1,0:T(8,128)}, f32[2,6,128,128]{3,2,1,0:T(8,128)}, u32[]{:S(2)}, u32[]{:S(2)}) %collective-permute-start.1) | collective-permute-done | bytes 786464 | tf_op jit(solution)/shard_map/ppermute | solution.py:11
  37.8 2.1 %constant_dynamic-update-slice_fusion.3 = f32[49,128,128]{2,1,0:T(8,128)} fusion(f32[49,128,128]{2,1,0:T(8,128)} %bitcast_dynamic-update-slice_fusion.5, f32[12,128,128]{2,1,0:T(8,128)} %bitcast.1), kind=kLoop, calls=%fused_computation.32 | loop fusion | bytes 1572864
  39.9 1.0 constant_dynamic-update-slice_fusion.2
  40.9 0.9 constant_dynamic-update-slice_fusion.1
  41.8 0.8 bitcast_dynamic-update-slice_fusion.4
  43.2 4.9 %gather_fusion.1 = f32[72,128,128]{2,1,0:T(8,128)} fusion(f32[49,128,128]{2,1,0:T(8,128)} %constant_dynamic-update-slice_fusion, s32[1024]{0:T(1024)S(1)} %pad_clamp_fusion.4), kind=kCustom, calls=%fused_computation.1 | custom fusion | bytes 9437472 | tf_op jit(solution)/shard_map/gather | solution.py:23
  48.1 9.4 %fusion.6 = f32[2,6,128,128,1]{3,2,4,1,0:T(8,128)S(1)} fusion(f32[2,6,6,128,128]{4,3,2,1,0:T(8,128)} %bitcast.85, f32[2,6,128,128]{3,2,1,0:T(8,128)S(1)} %copy-done), kind=kOutput, calls=%fused_computation.15 | convolution fusion | flops 1811939328 | bytes 6291456 | tf_op jit(solution)/shard_map/tqab,tpqbc->tpac/dot_general | solution.py:58
  57.5 0.9 fusion.18
  58.4 1.9 %collective-permute-start.5 = (f32[2,6,128,128]{2,3,1,0:T(8,128)S(1)}, f32[2,6,128,128]{2,3,1,0:T(8,128)}, u32[]{:S(2)}, u32[]{:S(2)}) collective-permute-start(f32[2,6,128,128]{2,3,1,0:T(8,128)S(1)} %bitcast.89), channel_id=1, source_target_pairs={{0,1},{1,2},{2,3},{3,4},{4,5},{5,6},{6,7},{7,8},{8,9},{9,10},{10,1... | collective-permute-start | bytes 2359304 | tf_op jit(solution)/shard_map/ppermute | solution.py:11
  60.3 2.0 %collective-permute-start.4 = (f32[1,6,128,128]{2,3,1,0:T(8,128)}, f32[1,6,128,128]{2,3,1,0:T(8,128)}, u32[]{:S(2)}, u32[]{:S(2)}) collective-permute-start(f32[1,6,128,128]{2,3,1,0:T(8,128)} %get-tuple-element.38), channel_id=1, source_target_pairs={{0,2},{1,3},{2,4},{3,5},{4,6},{5,7},{6,8},{7,9},{8,10},{9,11},{10,... | collective-permute-start | bytes 1179656 | tf_op jit(solution)/shard_map/ppermute | solution.py:11
  62.6 2.5 %gather_fusion.5 = f32[14,128,128]{2,1,0:T(8,128)S(1)} fusion(f32[49,128,128]{2,1,0:T(8,128)} %constant_dynamic-update-slice_fusion, s32[1024]{0:T(1024)S(1)} %pad_clamp_fusion), kind=kCustom, calls=%fused_computation.5 | custom fusion | bytes 1835064 | tf_op jit(solution)/shard_map/gather | solution.py:23
  65.1 2.7 %collective-permute-start.7 = (f32[1,6,128,128]{2,3,1,0:T(8,128)}, f32[1,6,128,128]{2,3,1,0:T(8,128)S(1)}, u32[]{:S(2)}, u32[]{:S(2)}) collective-permute-start(f32[1,6,128,128]{2,3,1,0:T(8,128)} %get-tuple-element.37), channel_id=1, source_target_pairs={{0,30},{1,31},{2,0},{3,1},{4,2},{5,3},{6,4},{7,5},{8,6},{9,7},{10,... | collective-permute-start | bytes 1179656 | tf_op jit(solution)/shard_map/ppermute | solution.py:11
  67.7 3.7 %collective-permute-done.4 = f32[1,6,128,128]{2,3,1,0:T(8,128)} collective-permute-done((f32[1,6,128,128]{2,3,1,0:T(8,128)}, f32[1,6,128,128]{2,3,1,0:T(8,128)}, u32[]{:S(2)}, u32[]{:S(2)}) %collective-permute-start.4) | collective-permute-done | bytes 393248 | tf_op jit(solution)/shard_map/ppermute | solution.py:11
  71.4 1.8 %bitcast_dynamic-update-slice_fusion.3 = f32[49,128,128]{1,2,0:T(8,128)} fusion(f32[1,6,128,128]{2,3,1,0:T(8,128)} %collective-permute-done.4), kind=kLoop, calls=%fused_computation.20 | loop fusion | bytes 786432
  73.2 11.3 %collective-permute-done.5 = f32[2,6,128,128]{2,3,1,0:T(8,128)} collective-permute-done((f32[2,6,128,128]{2,3,1,0:T(8,128)S(1)}, f32[2,6,128,128]{2,3,1,0:T(8,128)}, u32[]{:S(2)}, u32[]{:S(2)}) %collective-permute-start.5) | collective-permute-done | bytes 786464 | tf_op jit(solution)/shard_map/ppermute | solution.py:11
  84.5 2.1 %constant_dynamic-update-slice_fusion.7 = f32[49,128,128]{1,2,0:T(8,128)} fusion(f32[49,128,128]{1,2,0:T(8,128)} %bitcast_dynamic-update-slice_fusion.3, f32[12,128,128]{1,2,0:T(8,128)} %bitcast.13), kind=kLoop, calls=%fused_computation.36 | loop fusion | bytes 1572864
  86.6 0.9 constant_dynamic-update-slice_fusion.6
  87.5 7.7 %collective-permute-done.6 = f32[2,6,128,128]{2,3,1,0:T(8,128)} collective-permute-done((f32[2,6,128,128]{2,3,1,0:T(8,128)S(1)}, f32[2,6,128,128]{2,3,1,0:T(8,128)}, u32[]{:S(2)}, u32[]{:S(2)}) %collective-permute-start.6) | collective-permute-done | bytes 786464 | tf_op jit(solution)/shard_map/ppermute | solution.py:11
  95.2 2.1 %constant_dynamic-update-slice_fusion.5 = f32[49,128,128]{1,2,0:T(8,128)} fusion(f32[49,128,128]{1,2,0:T(8,128)} %constant_dynamic-update-slice_fusion.6, f32[12,128,128]{1,2,0:T(8,128)} %bitcast.15), kind=kLoop, calls=%fused_computation.34 | loop fusion | bytes 1572864
  97.3 0.8 bitcast_dynamic-update-slice_fusion.2
  98.7 5.2 %gather_fusion.3 = f32[84,128,128]{1,2,0:T(8,128)} fusion(f32[49,128,128]{1,2,0:T(8,128)} %constant_dynamic-update-slice_fusion.4, s32[1024]{0:T(1024)S(1)} %pad_clamp_fusion.2), kind=kCustom, calls=%fused_computation.3 | custom fusion | bytes 11010384 | tf_op jit(solution)/shard_map/gather | solution.py:23
  103.9 6.5 %fusion.4 = f32[2,6,128,128]{2,3,1,0:T(8,128)S(1)} fusion(f32[2,6,7,128,128]{3,4,2,1,0:T(8,128)} %bitcast.83, f32[2,7,128,128,1]{3,2,1,4,0:T(8,128)S(1)} %bitcast.92), kind=kOutput, calls=%fused_computation.13 | convolution fusion | flops 2114125824 | bytes 7208960 | tf_op jit(solution)/shard_map/toba,tpobc->tpac/dot_general | solution.py:62
  110.4 2.6 %collective-permute-start.9 = (f32[2,6,128,128]{2,3,1,0:T(8,128)S(1)}, f32[2,6,128,128]{2,3,1,0:T(8,128)}, u32[]{:S(2)}, u32[]{:S(2)}) collective-permute-start(f32[2,6,128,128]{2,3,1,0:T(8,128)S(1)} %fusion.8), channel_id=1, source_target_pairs={{0,1},{1,2},{2,3},{3,4},{4,5},{5,6},{6,7},{7,8},{8,9},{9,10},{10,1... | collective-permute-start | bytes 2359304 | tf_op jit(solution)/shard_map/ppermute | solution.py:11
  113.0 0.9 fusion.17
  114.2 1.3 collective-permute-start.10
  115.7 1.1 copy.40
  116.9 2.0 %collective-permute-start.11 = (f32[1,6,128,128]{2,3,1,0:T(8,128)}, f32[1,6,128,128]{2,3,1,0:T(8,128)S(1)}, u32[]{:S(2)}, u32[]{:S(2)}) collective-permute-start(f32[1,6,128,128]{2,3,1,0:T(8,128)} %get-tuple-element.35), channel_id=1, source_target_pairs={{0,30},{1,31},{2,0},{3,1},{4,2},{5,3},{6,4},{7,5},{8,6},{9,7},{10,... | collective-permute-start | bytes 1179656 | tf_op jit(solution)/shard_map/ppermute | solution.py:11
  118.9 4.4 %collective-permute-done.8 = f32[1,6,128,128]{2,3,1,0:T(8,128)S(1)} collective-permute-done((f32[1,6,128,128]{2,3,1,0:T(8,128)}, f32[1,6,128,128]{2,3,1,0:T(8,128)S(1)}, u32[]{:S(2)}, u32[]{:S(2)}) %collective-permute-start.8) | collective-permute-done | bytes 393248 | tf_op jit(solution)/shard_map/ppermute | solution.py:11
  123.3 0.8 bitcast_dynamic-update-slice_fusion.1
  124.1 13.1 %collective-permute-done.9 = f32[2,6,128,128]{2,3,1,0:T(8,128)} collective-permute-done((f32[2,6,128,128]{2,3,1,0:T(8,128)S(1)}, f32[2,6,128,128]{2,3,1,0:T(8,128)}, u32[]{:S(2)}, u32[]{:S(2)}) %collective-permute-start.9) | collective-permute-done | bytes 786464 | tf_op jit(solution)/shard_map/ppermute | solution.py:11
  137.2 2.1 %constant_dynamic-update-slice_fusion.11 = f32[49,128,128]{1,2,0:T(8,128)} fusion(f32[49,128,128]{1,2,0:T(8,128)} %bitcast_dynamic-update-slice_fusion.1, f32[12,128,128]{1,2,0:T(8,128)} %bitcast.25), kind=kLoop, calls=%fused_computation.40 | loop fusion | bytes 1572864
  139.2 1.0 constant_dynamic-update-slice_fusion.10
  140.2 7.1 %collective-permute-done.10 = f32[2,6,128,128]{2,3,1,0:T(8,128)} collective-permute-done((f32[2,6,128,128]{2,3,1,0:T(8,128)S(1)}, f32[2,6,128,128]{2,3,1,0:T(8,128)}, u32[]{:S(2)}, u32[]{:S(2)}) %collective-permute-start.10) | collective-permute-done | bytes 786464 | tf_op jit(solution)/shard_map/ppermute | solution.py:11
  147.3 2.1 %constant_dynamic-update-slice_fusion.9 = f32[49,128,128]{1,2,0:T(8,128)} fusion(f32[49,128,128]{1,2,0:T(8,128)} %constant_dynamic-update-slice_fusion.10, f32[12,128,128]{1,2,0:T(8,128)} %bitcast.27), kind=kLoop, calls=%fused_computation.38 | loop fusion | bytes 1572864
  149.4 0.8 bitcast_dynamic-update-slice_fusion
  150.8 4.9 %gather_fusion.6 = f32[72,128,128]{1,2,0:T(8,128)} fusion(f32[49,128,128]{1,2,0:T(8,128)} %constant_dynamic-update-slice_fusion.8, s32[1024]{0:T(1024)S(1)} %pad_clamp_fusion.4), kind=kCustom, calls=%fused_computation.6 | custom fusion | bytes 9437472 | tf_op jit(solution)/shard_map/gather | solution.py:23
  155.7 5.7 %fusion.2 = f32[2,6,128,128]{2,3,1,0:T(8,128)S(1)} fusion(f32[2,6,128,128]{2,3,1,0:T(8,128)S(1)} %copy.38, f32[2,6,6,128,128]{3,4,2,1,0:T(8,128)} %bitcast.84, f32[2,6,128,128]{3,2,1,0:T(8,128)S(1)} %copy-done.1), kind=kOutput, calls=%fused_computation.10 | convolution fusion | flops 1812332544 | bytes 7077888 | tf_op jit(solution)/shard_map/tqab,tpqbc->tpac/dot_general | solution.py:68
  161.4 1.1 copy.39
  (69 shorter events, 8.0 us)
Async XLA Ops:
  0.6 47.5 %copy-start = (f32[2,6,128,128]{3,2,1,0:T(8,128)S(1)}, f32[2,6,128,128]{3,2,1,0:T(8,128)}, u32[]{:S(2)}) copy-start(f32[2,6,128,128]{3,2,1,0:T(8,128)} %param.5) | copy-start | bytes 2359300
  0.6 39.3 %copy-start.1 = (f32[2,6,128,128]{3,2,1,0:T(8,128)S(1)}, f32[2,6,128,128]{3,2,1,0:T(8,128)}, u32[]{:S(2)}) copy-start(f32[2,6,128,128]{3,2,1,0:T(8,128)} %param.6) | copy-start | bytes 2359300
  0.7 40.2 %collective-permute-start.2 = (f32[2,6,128,128]{3,2,1,0:T(8,128)}, f32[2,6,128,128]{3,2,1,0:T(8,128)S(1)}, u32[]{:S(2)}, u32[]{:S(2)}) collective-permute-start(f32[2,6,128,128]{3,2,1,0:T(8,128)} %param.6), channel_id=1, source_target_pairs={{0,31},{1,0},{2,1},{3,2},{4,3},{5,4},{6,5},{7,6},{8,7},{9,8},{10,9... | collective-permute-start | bytes 2359304 | tf_op jit(solution)/shard_map/ppermute | solution.py:11
  3.3 34.5 %collective-permute-start.1 = (f32[2,6,128,128]{3,2,1,0:T(8,128)}, f32[2,6,128,128]{3,2,1,0:T(8,128)}, u32[]{:S(2)}, u32[]{:S(2)}) collective-permute-start(f32[2,6,128,128]{3,2,1,0:T(8,128)} %param.6), channel_id=1, source_target_pairs={{0,1},{1,2},{2,3},{3,4},{4,5},{5,6},{6,7},{7,8},{8,9},{9,10},{10,1... | collective-permute-start | bytes 2359304 | tf_op jit(solution)/shard_map/ppermute | solution.py:11
  5.3 36.5 %collective-permute-start.3 = (f32[1,6,128,128]{3,2,1,0:T(8,128)}, f32[1,6,128,128]{3,2,1,0:T(8,128)S(1)}, u32[]{:S(2)}, u32[]{:S(2)}) collective-permute-start(f32[1,6,128,128]{3,2,1,0:T(8,128)} %get-tuple-element.39), channel_id=1, source_target_pairs={{0,30},{1,31},{2,0},{3,1},{4,2},{5,3},{6,4},{7,5},{8,6},{9,7},{10,... | collective-permute-start | bytes 1179656 | tf_op jit(solution)/shard_map/ppermute | solution.py:11
  9.2 9.5 %collective-permute-start = (f32[1,6,128,128]{3,2,1,0:T(8,128)}, f32[1,6,128,128]{3,2,1,0:T(8,128)S(1)}, u32[]{:S(2)}, u32[]{:S(2)}) collective-permute-start(f32[1,6,128,128]{3,2,1,0:T(8,128)} %get-tuple-element.40), channel_id=1, source_target_pairs={{0,2},{1,3},{2,4},{3,5},{4,6},{5,7},{6,8},{7,9},{8,10},{9,11},{10,... | collective-permute-start | bytes 1179656 | tf_op jit(solution)/shard_map/ppermute | solution.py:11
  48.1 14.2 %copy-start.2 = (pred[2,6,7]{2,1,0:T(8,128)(4,1)S(1)}, pred[2,6,7]{2,1,0:T(8,128)(4,1)}, u32[]{:S(2)}) copy-start(pred[2,6,7]{2,1,0:T(8,128)(4,1)} %get-tuple-element.28) | copy-start | bytes 256
  48.1 14.2 %copy-start.3 = (s32[2,7]{1,0:T(2,128)S(1)}, s32[2,7]{1,0:T(2,128)}, u32[]{:S(2)}) copy-start(s32[2,7]{1,0:T(2,128)} %broadcast_add_fusion.2) | copy-start | bytes 172
  48.1 14.2 %copy-start.5 = (pred[2,7]{1,0:T(4,128)(4,1)S(1)}, pred[2,7]{1,0:T(4,128)(4,1)}, u32[]{:S(2)}) copy-start(pred[2,7]{1,0:T(4,128)(4,1)} %compare_and_fusion.1) | copy-start | bytes 46
  48.1 14.2 %copy-start.4 = (s32[2,7]{1,0:T(2,128)S(1)}, s32[2,7]{1,0:T(2,128)}, u32[]{:S(2)}) copy-start(s32[2,7]{1,0:T(2,128)} %get-tuple-element.24) | copy-start | bytes 172
  58.4 26.1 %collective-permute-start.5 = (f32[2,6,128,128]{2,3,1,0:T(8,128)S(1)}, f32[2,6,128,128]{2,3,1,0:T(8,128)}, u32[]{:S(2)}, u32[]{:S(2)}) collective-permute-start(f32[2,6,128,128]{2,3,1,0:T(8,128)S(1)} %bitcast.89), channel_id=1, source_target_pairs={{0,1},{1,2},{2,3},{3,4},{4,5},{5,6},{6,7},{7,8},{8,9},{9,10},{10,1... | collective-permute-start | bytes 2359304 | tf_op jit(solution)/shard_map/ppermute | solution.py:11
  60.3 11.1 %collective-permute-start.4 = (f32[1,6,128,128]{2,3,1,0:T(8,128)}, f32[1,6,128,128]{2,3,1,0:T(8,128)}, u32[]{:S(2)}, u32[]{:S(2)}) collective-permute-start(f32[1,6,128,128]{2,3,1,0:T(8,128)} %get-tuple-element.38), channel_id=1, source_target_pairs={{0,2},{1,3},{2,4},{3,5},{4,6},{5,7},{6,8},{7,9},{8,10},{9,11},{10,... | collective-permute-start | bytes 1179656 | tf_op jit(solution)/shard_map/ppermute | solution.py:11
  62.4 32.8 %collective-permute-start.6 = (f32[2,6,128,128]{2,3,1,0:T(8,128)S(1)}, f32[2,6,128,128]{2,3,1,0:T(8,128)}, u32[]{:S(2)}, u32[]{:S(2)}) collective-permute-start(f32[2,6,128,128]{2,3,1,0:T(8,128)S(1)} %bitcast.90), channel_id=1, source_target_pairs={{0,31},{1,0},{2,1},{3,2},{4,3},{5,4},{6,5},{7,6},{8,7},{9,8},{10,9... | collective-permute-start | bytes 2359304 | tf_op jit(solution)/shard_map/ppermute | solution.py:11
  65.1 32.2 %collective-permute-start.7 = (f32[1,6,128,128]{2,3,1,0:T(8,128)}, f32[1,6,128,128]{2,3,1,0:T(8,128)S(1)}, u32[]{:S(2)}, u32[]{:S(2)}) collective-permute-start(f32[1,6,128,128]{2,3,1,0:T(8,128)} %get-tuple-element.37), channel_id=1, source_target_pairs={{0,30},{1,31},{2,0},{3,1},{4,2},{5,3},{6,4},{7,5},{8,6},{9,7},{10,... | collective-permute-start | bytes 1179656 | tf_op jit(solution)/shard_map/ppermute | solution.py:11
  110.4 26.7 %collective-permute-start.9 = (f32[2,6,128,128]{2,3,1,0:T(8,128)S(1)}, f32[2,6,128,128]{2,3,1,0:T(8,128)}, u32[]{:S(2)}, u32[]{:S(2)}) collective-permute-start(f32[2,6,128,128]{2,3,1,0:T(8,128)S(1)} %fusion.8), channel_id=1, source_target_pairs={{0,1},{1,2},{2,3},{3,4},{4,5},{5,6},{6,7},{7,8},{8,9},{9,10},{10,1... | collective-permute-start | bytes 2359304 | tf_op jit(solution)/shard_map/ppermute | solution.py:11
  113.9 9.4 %collective-permute-start.8 = (f32[1,6,128,128]{2,3,1,0:T(8,128)}, f32[1,6,128,128]{2,3,1,0:T(8,128)S(1)}, u32[]{:S(2)}, u32[]{:S(2)}) collective-permute-start(f32[1,6,128,128]{2,3,1,0:T(8,128)} %get-tuple-element.36), channel_id=1, source_target_pairs={{0,2},{1,3},{2,4},{3,5},{4,6},{5,7},{6,8},{7,9},{8,10},{9,11},{10,... | collective-permute-start | bytes 1179656 | tf_op jit(solution)/shard_map/ppermute | solution.py:11
  114.2 33.1 %collective-permute-start.10 = (f32[2,6,128,128]{2,3,1,0:T(8,128)S(1)}, f32[2,6,128,128]{2,3,1,0:T(8,128)}, u32[]{:S(2)}, u32[]{:S(2)}) collective-permute-start(f32[2,6,128,128]{2,3,1,0:T(8,128)S(1)} %fusion.8), channel_id=1, source_target_pairs={{0,31},{1,0},{2,1},{3,2},{4,3},{5,4},{6,5},{7,6},{8,7},{9,8},{10,9... | collective-permute-start | bytes 2359304 | tf_op jit(solution)/shard_map/ppermute | solution.py:11
  116.9 32.5 %collective-permute-start.11 = (f32[1,6,128,128]{2,3,1,0:T(8,128)}, f32[1,6,128,128]{2,3,1,0:T(8,128)S(1)}, u32[]{:S(2)}, u32[]{:S(2)}) collective-permute-start(f32[1,6,128,128]{2,3,1,0:T(8,128)} %get-tuple-element.35), channel_id=1, source_target_pairs={{0,30},{1,31},{2,0},{3,1},{4,2},{5,3},{6,4},{7,5},{8,6},{9,7},{10,... | collective-permute-start | bytes 1179656 | tf_op jit(solution)/shard_map/ppermute | solution.py:11
where the time goes:
time: 163 us
  waiting for transfers between devices  65.6 us (40%)
  local copies, waits for them, and re-layouts  49.8 us (31%)
  matrix products  21.5 us (13%)
  starting transfers between devices  19.1 us (12%)
  other arithmetic  5.58 us (3%)
    ppermute x12, waiting for transfers between devices, passed_along(): lax.ppermute(value, axis, [(i, (i + by) % size) for i in range(size)])  65.6 us
    unnamed x31, local copies, waits for them, and re-layouts  23.3 us
    ppermute x12, starting transfers between devices, passed_along(): lax.ppermute(value, axis, [(i, (i + by) % size) for i in range(size)])  19.1 us
    gather x4, local copies, waits for them, and re-layouts, select_tiles(): return window_flat[flat_index]  17.5 us
    dot_general x1, matrix products, body(): jnp.einsum('tqab,tpqbc->tpac', correlation, chosen, precision=lax.Precisi...  9.36 us
    dot_general x1, matrix products, body(): jnp.einsum('toba,tpobc->tpac', left_side, right_side, precision=lax.Preci...  6.49 us
    dot_general x1, matrix products, body(): jnp.einsum('tqab,tpqbc->tpac', factor, picked, precision=lax.Precision.HI...  5.7 us
    slice x3, local copies, waits for them, and re-layouts, neighbour_window(): sources = ((2, tiles[rows_here - edge_count:]), (-2, tiles[:edge_count]))  3.88 us
  transfers between devices with their start and end apart: 12, of which 7 were waited for; matrix products, arithmetic and copies ran while one was open for 21% of the time, Pallas kernels for 0%

commit v1 on v0

v1 whole, which is shorter than its diff:
```python
import jax
import jax.numpy as jnp
from jax import lax
from jax.experimental import pallas as pl
from jax.experimental.pallas import tpu as pltpu
from jax.sharding import PartitionSpec as P


REACH = 3
AXES = ("blk", "sub")
OWN = 2
LEFT = -2 * REACH
WIDE = OWN + 4 * REACH
COL0 = -REACH
COLS = OWN + 2 * REACH
PAIRS = COLS // 2
SIDE = 3
F32 = jnp.float32
BF16 = jnp.bfloat16

UP = ((0, 3), (0, 4), (0, 5), (1, 0), (1, 3), (1, 4), (1, 5))
DOWN = ((0, 0), (0, 1), (0, 2), (0, 3), (1, 1), (1, 2), (1, 3))
FAR_UP = ((0, 5), (1, 4), (1, 5))
FAR_DOWN = ((0, 1), (0, 2), (1, 1))


def send(value, to):
    count = lax.axis_size(AXES)
    return lax.ppermute(value, AXES, [(i, to(i) % count) for i in range(count)])


def swap(i):
    return i ^ 1


def up(i):
    return i + 2


def down(i):
    return i - 2


def near(i):
    return i + 2 if i % 2 == 0 else i - 2


def far_up(i):
    return i + 4 if i % 2 == 0 else i + 2


def far_down(i):
    return i - 2 if i % 2 == 0 else i - 4


def split(value):
    high = value.astype(BF16)
    low = (value - high.astype(F32)).astype(BF16)
    return high, low


def dot3(a_high, a_low, b_high, b_low):
    left = jnp.concatenate([a_high, a_low, a_high], axis=1)
    right = jnp.concatenate([b_high, b_high, b_low], axis=0)
    return jnp.dot(left, right, preferred_element_type=F32)


def slot_of(offset, dropped):
    pos = offset + REACH - jnp.where(offset > 0, 1, 0)
    slot = jnp.where(offset == 0, 0, pos + 1 - jnp.where(pos > dropped, 1, 0))
    there = (jnp.abs(offset) <= REACH) & ((offset == 0) | (pos != dropped))
    return jnp.clip(slot, 0, 2 * REACH - 1), there


class Rows:
    def __init__(self, meta):
        self.meta = meta
        self.parity = meta[WIDE]

    def dropped(self, row):
        return self.meta[row - LEFT]

    def side_row(self, side):
        return 2 - 4 * jnp.bitwise_xor(self.parity, side)

    def side_pair(self, side):
        return 1 - jnp.bitwise_xor(self.parity, side)

    def present(self, row, col):
        return slot_of(jnp.int32(col - row), self.dropped(row))[1]

    def own(self, refs, row, col):
        slot, there = slot_of(jnp.int32(col - row), self.dropped(row))
        tile = refs[row][0, slot] if isinstance(refs, tuple) else refs[row, slot]
        return jnp.where(there, tile, 0.0)

    def packed(self, ref, layout, row0, r, col):
        slots = [s for rr, s in layout if rr == r]
        base = [j for j, (rr, _) in enumerate(layout) if rr == r][0]
        row = row0 + r
        if col == row:
            return ref[base + slots.index(0)]
        slot, there = slot_of(jnp.int32(col - row), self.dropped(row))
        rest = [s for s in slots if s]
        index = base + slots.index(rest[0]) + jnp.clip(slot - rest[0], 0, len(rest) - 1)
        return jnp.where(there, ref[index], 0.0)

    def side(self, refs, side, r, col):
        row = self.side_row(side) + r
        slot, there = slot_of(col - row, self.dropped(row))
        return jnp.where(there, refs[r][0, slot], 0.0)

    def dense_slot(self, row, slot):
        if slot == 0:
            return row - COL0
        pos = slot - 1 + jnp.where(slot - 1 >= self.dropped(row), 1, 0)
        return row - COL0 - REACH + pos + jnp.where(pos >= REACH, 1, 0)


def zero(tile):
    return jnp.zeros((tile, tile), F32)


def put(high, low, r, c, tile, value):
    h, l = split(value)
    high[r, :, c * tile : (c + 1) * tile] = h
    low[r, :, c * tile : (c + 1) * tile] = l


def flat(ref, rows, cols):
    value = ref[rows, :, cols]
    return value.reshape(value.shape[0] * value.shape[1], value.shape[2])


def row_matmul(left_high, left_low, right_high, right_low, out, tile):
    for c in range(0, COLS, 2):
        lo, hi = max(c - REACH, 0), min(c + 1 + REACH, COLS - 1) + 1
        k = slice(lo * tile, hi * tile)
        n = slice(c * tile, (c + 2) * tile)
        block = dot3(
            flat(left_high, slice(None), k),
            flat(left_low, slice(None), k),
            flat(right_high, slice(lo, hi), n),
            flat(right_low, slice(lo, hi), n),
        )
        for i in range(OWN):
            for j in range(2):
                out[i, c + j] = block[i * tile : (i + 1) * tile, j * tile : (j + 1) * tile]


def pack_kernel(z, zu, zd):
    for out, layout in ((zu, UP), (zd, DOWN)):
        for j, (i, slot) in enumerate(layout):
            out[j] = z[i, slot]


def product_kernel(meta, s, z, x0, x1, n0, n1, zu, zd, p0, p1, pu, pd, z_high, z_low, s_high, s_low, dense):
    tile = s.shape[-1]
    rows = Rows(meta)
    for c in range(COLS):
        col = c + COL0
        for i in range(OWN):
            near_by = abs(col - i) <= REACH
            put(s_high, s_low, i, c, tile, rows.own(s, i, col) if near_by else zero(tile))
            put(z_high, z_low, i - COL0, c, tile, rows.own(z, i, col) if near_by else zero(tile))
        for side, refs in enumerate(((x0, x1), (n0, n1))):
            for r in range(2):
                where = rows.side_row(side) + r - COL0
                put(z_high, z_low, where, c, tile, rows.side(refs, side, r, col))
        row = -REACH
        put(z_high, z_low, 0, c, tile, rows.packed(zu, UP, -4, 1, col) if abs(col - row) <= REACH else zero(tile))
        row = OWN - 1 + REACH
        put(z_high, z_low, COLS - 1, c, tile, rows.packed(zd, DOWN, 4, 0, col) if abs(col - row) <= REACH else zero(tile))
    row_matmul(s_high, s_low, z_high, z_low, dense, tile)
    for i, ref in enumerate((p0, p1)):
        for slot in range(2 * REACH):
            ref[0, slot] = dense[i, rows.dense_slot(i, slot)]
    for ref, layout in ((pu, UP), (pd, DOWN)):
        for j, (i, slot) in enumerate(layout):
            ref[j] = dense[i, rows.dense_slot(i, slot)]


def turn_kernel(meta, z, x0, x1, n0, n1, zu, zd, fu, fd, t_own, t_up, t_down, t_swap, t_near, t_far, z_own):
    tile = z.shape[-1]
    rows = Rows(meta)

    def store(out, c, r, value):
        high, low = split(value.T)
        out[c * tile : (c + 1) * tile, r * tile : (r + 1) * tile] = high
        out[c * tile : (c + 1) * tile, (2 + r) * tile : (3 + r) * tile] = low

    for r in range(2):
        for c in range(COLS):
            col = c + COL0
            value = rows.own(z, r, col) if abs(col - r) <= REACH else zero(tile)
            store(t_own, c, r, value)
            high, low = split(value)
            z_own[r, :, c * tile : (c + 1) * tile] = high
            z_own[r, :, (COLS + c) * tile : (COLS + c + 1) * tile] = low
        for c in range(4):
            col = c + COL0
            store(t_up, c, r, rows.packed(zu, UP, -4, r, col) if abs(col - (r - 4)) <= REACH else zero(tile))
            col = c + COL0 + 4
            store(t_down, c, r, rows.packed(zd, DOWN, 4, r, col) if abs(col - (r + 4)) <= REACH else zero(tile))
        for c in range(2):
            col = c + COL0
            store(t_far, c, r, rows.packed(fu, FAR_UP, -6, r, col) if abs(col - (r - 6)) <= REACH else zero(tile))
            col = c + COL0 + 6
            store(t_far, 2 + c, r, rows.packed(fd, FAR_DOWN, 6, r, col) if abs(col - (r + 6)) <= REACH else zero(tile))
        for side, (out, refs) in enumerate(((t_swap, (x0, x1)), (t_near, (n0, n1)))):
            first = 2 * rows.side_pair(side) + COL0
            for c in range(2 * SIDE):
                store(out, c, r, rows.side(refs, side, r, first + c))


def halves(turned, first, last, tile):
    part = turned[2 * first * tile : 2 * last * tile]
    return part[:, : 2 * tile], part[:, 2 * tile :]


def side_gram(rows, side, refs, turned, high, low, add, tile):
    first = 2 * rows.side_pair(side) + COL0
    for r in range(2):
        for c in range(2 * SIDE):
            put(high, low, r, c, tile, rows.side(refs, side, r, first + c))
    left = halves(turned, 0, SIDE, tile)
    for b in range(SIDE):
        n = slice(2 * b * tile, (2 * b + 2) * tile)
        block = dot3(*left, flat(high, slice(0, 2), n), flat(low, slice(0, 2), n))
        for a in range(SIDE):
            add(a, b, block[2 * a * tile : (2 * a + 2) * tile])


def gram_kernel(meta, t_own, t_up, t_down, t_swap, p0, p1, pu, pd, x0, x1, gram, high, low, side_high, side_low):
    tile = p0.shape[-1]
    rows = Rows(meta)
    for r in range(2):
        for c in range(COLS):
            col = c + COL0
            put(high, low, r, c, tile, rows.own((p0, p1), r, col) if abs(col - r) <= REACH else zero(tile))
        for c in range(4):
            col = c + COL0
            value = rows.packed(pu, UP, -4, r, col) if abs(col - (r - 4)) <= REACH else zero(tile)
            put(high, low, 2 + r, c, tile, value)
            col = c + COL0 + 4
            value = rows.packed(pd, DOWN, 4, r, col) if abs(col - (r + 4)) <= REACH else zero(tile)
            put(high, low, 2 + r, 4 + c, tile, value)
    for b in range(PAIRS):
        n = slice(2 * b * tile, (2 * b + 2) * tile)
        first, last = max(0, b - 2), min(PAIRS, b + 3)
        block = dot3(*halves(t_own, first, last, tile), flat(high, slice(0, 2), n), flat(low, slice(0, 2), n))
        edge = dot3(
            *halves(t_up if b < 2 else t_down, 0, 2, tile), flat(high, slice(2, 4), n), flat(low, slice(2, 4), n)
        )
        for a in range(first, last):
            value = block[2 * (a - first) * tile : 2 * (a - first + 1) * tile]
            e = a if b < 2 else a - 2
            if 0 <= e < 2:
                value = value + edge[2 * e * tile : (2 * e + 2) * tile]
            gram[PAIRS * a + b] = value

    def add(a, b, value):
        index = PAIRS * a + b + (PAIRS + 1) * rows.side_pair(0)
        gram[index] = gram[index] + value

    side_gram(rows, 0, (x0, x1), t_swap, side_high, side_low, add, tile)


def refine_kernel(
    meta, z, z_own, t_near, t_far, early, n0, n1, fu, fd, refined, correction,
    high, low, far_high, far_low, late, d_high, d_low, dense, z_high, z_low,
):
    tile = z.shape[-1]
    rows = Rows(meta)

    def add(a, b, value):
        late[SIDE * a + b] = value

    side_gram(rows, 1, (n0, n1), t_near, high, low, add, tile)
    for r in range(2):
        for c in range(2):
            col = c + COL0
            value = rows.packed(fu, FAR_UP, -6, r, col) if abs(col - (r - 6)) <= REACH else zero(tile)
            put(far_high, far_low, r, c, tile, value)
            col = c + COL0 + 6
            value = rows.packed(fd, FAR_DOWN, 6, r, col) if abs(col - (r + 6)) <= REACH else zero(tile)
            put(far_high, far_low, r, 2 + c, tile, value)
    far = []
    for e in range(2):
        n = slice(2 * e * tile, (2 * e + 2) * tile)
        far.append(
            dot3(*halves(t_far, e, e + 1, tile), flat(far_high, slice(0, 2), n), flat(far_low, slice(0, 2), n))
        )
    eye = (
        lax.broadcasted_iota(jnp.int32, (tile, tile), 0) == lax.broadcasted_iota(jnp.int32, (tile, tile), 1)
    ).astype(F32)
    shift = rows.side_pair(1)
    for a in range(PAIRS):
        for b in range(PAIRS):
            if abs(a - b) > 2:
                continue
            gram = early[PAIRS * a + b]
            ia, ib = a - shift, b - shift
            there = (ia >= 0) & (ia < SIDE) & (ib >= 0) & (ib < SIDE)
            gram = gram + jnp.where(there, late[jnp.clip(SIDE * ia + ib, 0, SIDE * SIDE - 1)], 0.0)
            if a == b and a in (0, PAIRS - 1):
                gram = gram + far[0 if a == 0 else 1]
            for i in range(2):
                for j in range(2):
                    k, c = 2 * a + i, 2 * b + j
                    value = -gram[i * tile : (i + 1) * tile, j * tile : (j + 1) * tile]
                    if k == c:
                        value = value + eye
                    elif abs(k - c) <= REACH:
                        value = jnp.where(rows.present(k + COL0, c + COL0), value, 0.0)
                    else:
                        value = zero(tile)
                    put(d_high, d_low, k, c, tile, value)
                    if k + COL0 in (0, 1):
                        dense[k + COL0, c] = value
    for i in range(OWN):
        for slot in range(2 * REACH):
            correction[i, slot] = dense[i, rows.dense_slot(i, slot)]
    half = COLS * tile
    z_high[...] = z_own[:, :, :half]
    z_low[...] = z_own[:, :, half:]
    row_matmul(z_high, z_low, d_high, d_low, dense, tile)
    for i in range(OWN):
        for slot in range(2 * REACH):
            refined[i, slot] = z[i, slot] + 0.5 * dense[i, rows.dense_slot(i, slot)]


def pick(rows, layout):
    return jnp.concatenate([rows[r][0, s : s + 1] for r, s in layout], axis=0)


def body(correlation, factor, pattern):
    rows_here, slots, tile = correlation.shape[:3]
    total = pattern.shape[0]
    assert rows_here == OWN and slots == 2 * REACH and total >= WIDE
    device = lax.axis_index(AXES)
    rows = (device * OWN + jnp.arange(LEFT, LEFT + WIDE, dtype=jnp.int32)) % total
    offsets = (pattern[rows][:, 1:] - rows[:, None] + total // 2) % total - total // 2
    expected = jnp.array([-3, -2, -1, 1, 2], jnp.int32)
    dropped = jnp.sum((offsets == expected).astype(jnp.int32), axis=1)
    meta = jnp.concatenate([dropped, (device % 2)[None]]).astype(jnp.int32)

    vmem = pl.BlockSpec(memory_space=pltpu.VMEM)
    smem = pl.BlockSpec(memory_space=pltpu.SMEM)

    def call(kernel, ins, outs, scratch, flops, scalars=1):
        return pl.pallas_call(
            kernel,
            in_specs=[smem] * scalars + [vmem] * (len(ins) - scalars),
            out_specs=jax.tree.map(lambda _: vmem, outs),
            out_shape=outs,
            scratch_shapes=scratch,
            cost_estimate=pl.CostEstimate(flops=flops, bytes_accessed=4 << 20, transcendentals=0),
        )(*ins)

    def shape(*dims, dtype=F32):
        return jax.ShapeDtypeStruct(dims, dtype)

    def halves_of(n, m):
        return [pltpu.VMEM((n, tile, m * tile), BF16)] * 2

    row = shape(1, slots, tile, tile)
    seven = shape(len(UP), tile, tile)
    dense = pltpu.VMEM((OWN, COLS, tile, tile), F32)

    x = [send(factor[r : r + 1], swap) for r in range(OWN)]
    zu, zd = call(pack_kernel, (factor,), (seven, seven), [], 1000, 0)
    zu, zd = send(zu, up), send(zd, down)
    n = [send(x[r], near) for r in range(OWN)]
    zfu = send(pick(x, FAR_UP), far_up)
    zfd = send(pick(x, FAR_DOWN), far_down)
    p0, p1, pu, pd = call(
        product_kernel,
        (meta, correlation, factor, *x, *n, zu, zd),
        (row, row, seven, seven),
        halves_of(COLS, COLS) + halves_of(OWN, COLS) + [dense],
        int(2e9),
    )
    px = [send(v, swap) for v in (p0, p1)]
    pu, pd = send(pu, up), send(pd, down)
    pn = [send(v, near) for v in px]
    pfu = send(pick(px, FAR_UP), far_up)
    pfd = send(pick(px, FAR_DOWN), far_down)

    def turned(columns):
        return shape(columns * tile, 4 * tile, dtype=BF16)

    t_own, t_up, t_down, t_swap, t_near, t_far, z_own = call(
        turn_kernel,
        (meta, factor, *x, *n, zu, zd, zfu, zfd),
        (turned(COLS), turned(4), turned(4), turned(2 * SIDE), turned(2 * SIDE), turned(4),
         shape(OWN, tile, 2 * COLS * tile, dtype=BF16)),
        [],
        int(2e9),
    )
    early = call(
        gram_kernel,
        (meta, t_own, t_up, t_down, t_swap, p0, p1, pu, pd, *px),
        shape(PAIRS * PAIRS, 2 * tile, 2 * tile),
        halves_of(4, COLS) + halves_of(2, 2 * SIDE),
        int(4e9),
    )
    return call(
        refine_kernel,
        (meta, factor, z_own, t_near, t_far, early, *pn, pfu, pfd),
        (shape(*factor.shape), shape(*factor.shape)),
        halves_of(2, 2 * SIDE)
        + halves_of(2, 4)
        + [pltpu.VMEM((SIDE * SIDE, 2 * tile, 2 * tile), F32)]
        + halves_of(COLS, COLS)
        + [dense]
        + halves_of(OWN, COLS),
        int(4e9),
    )


def solution(mesh):
    tiles = P(AXES, None, None, None)

    return jax.shard_map(body, mesh=mesh, in_specs=(tiles, tiles, P()), out_specs=(tiles, tiles), check_vma=False)
```

time: 163 us -> 86 us (0.53)
  waiting for transfers between devices: 65.6 us -> 20.5 us
  local copies, waits for them, and re-layouts: 49.8 us -> 5.79 us
  Pallas kernels: 0 us -> 29.7 us
  matrix products: 21.5 us -> 0 us
  starting transfers between devices: 19.1 us -> 27.3 us
  other arithmetic: 5.58 us -> 1.57 us
    ppermute x12 -> x16, waiting for transfers between devices: 65.6 us -> 20.5 us  [send(): return lax.ppermute(value, AXES, [(i, to(i) % count) for i in range(count)])]
    pallas_call x0 -> x5, Pallas kernels: none -> 29.7 us  [call(): pl.pallas_call(kernel, in_specs=[smem] * scalars + [vmem] * (len(ins) - s...]
    dot_general x3 -> x0, matrix products: 21.5 us -> none  [the longest x1 9.36 us: body(): jnp.einsum('tqab,tpqbc->tpac', correlation, chosen, precision=lax.Precisi...]
    unnamed x31 -> x33, local copies, waits for them, and re-layouts: 23.3 us -> 4.01 us
    gather x13 -> x1, local copies, waits for them, and re-layouts: 19.7 us -> 0.56 us  [body(): pattern[rows][:, 1:] - rows[:, None] + total // 2]
    ppermute x12 -> x16, starting transfers between devices: 19.1 us -> 27.3 us  [send(): return lax.ppermute(value, AXES, [(i, to(i) % count) for i in range(count)])]
    slice x3 -> x1, local copies, waits for them, and re-layouts: 3.88 us -> 1.17 us  [body(): x = [send(factor[r:r + 1], swap) for r in range(OWN)]]
    another operation x3 -> x0, other arithmetic: 1.88 us -> none  [select_tiles(): slot_index = jnp.argmax(matches, axis=-1)]
  transfers between devices with their start and end apart: 12 -> 16, of which waited for: 7 -> 6; matrix products, arithmetic and copies ran while one was open for 21% -> 3% of each run, Pallas kernels for 0% -> 25%
where the time goes in v1:
time: 86 us; the launch traced here: 85.7 us
  Pallas kernels  29.7 us (35%)
  starting transfers between devices  27.3 us (32%)
  waiting for transfers between devices  20.5 us (24%)
  local copies, waits for them, and re-layouts  5.79 us (7%)
  other arithmetic  1.57 us (2%)
    pallas_call x5, Pallas kernels, call(): pl.pallas_call(kernel, in_specs=[smem] * scalars + [vmem] * (len(ins) - s...  29.7 us
    ppermute x16, starting transfers between devices, send(): return lax.ppermute(value, AXES, [(i, to(i) % count) for i in range(count)])  27.3 us
    ppermute x16, waiting for transfers between devices, send(): return lax.ppermute(value, AXES, [(i, to(i) % count) for i in range(count)])  20.5 us
    unnamed x33, local copies, waits for them, and re-layouts  4.01 us
  transfers between devices with their start and end apart: 16, of which 6 were waited for; matrix products, arithmetic and copies ran while one was open for 3% of the time, Pallas kernels for 25%

profile of v1, /device:TPU:1, one launch (start us, length us, event | category | flops | bytes accessed | tf_op | source)
XLA Modules:
  0.0 85.7 jit_solution(7189479742329193455)
XLA Ops:
  0.6 1.2 %fusion.7 = (f32[1,6,128,128]{3,2,1,0:T(8,128)S(1)}, f32[1,6,128,128]{3,2,1,0:T(8,128)S(1)}) fusion(f32[2,6,128,128]{3,2,1,0:T(8,128)} %z.7), kind=kLoop, calls=%fused_computation.38 | loop fusion | bytes 1572864 | tf_op jit(solution)/shard_map/slice | solution.py:371
  1.8 2.1 %collective-permute-start = (f32[1,6,128,128]{3,2,1,0:T(8,128)S(1)}, f32[1,6,128,128]{3,2,1,0:T(8,128)S(1)}, u32[]{:S(2)}, u32[]{:S(2)}) collective-permute-start(f32[1,6,128,128]{3,2,1,0:T(8,128)S(1)} %get-tuple-element.29), channel_id=1, source_target_pairs={{0,1},{1,0},{2,3},{3,2},{4,5},{5,4},{6,7},{7,6},{8,9},{9,8},{10,11... | collective-permute-start | bytes 1179656 | tf_op jit(solution)/shard_map/ppermute | solution.py:29
  3.9 0.1 collective-permute-start.1
  4.0 2.1 %shard_map.59 = (f32[7,128,128]{2,1,0:T(8,128)}, f32[7,128,128]{2,1,0:T(8,128)}) custom-call(f32[2,6,128,128]{3,2,1,0:T(8,128)} %z.7), custom_call_target="tpu_custom_call" | custom-call | flops 1000 | bytes 4194304 | tf_op jit(solution)/shard_map/pallas_call | solution.py:352
  6.1 2.5 %collective-permute-start.4 = (f32[7,128,128]{2,1,0:T(8,128)}, f32[7,128,128]{2,1,0:T(8,128)S(1)}, u32[]{:S(2)}, u32[]{:S(2)}) collective-permute-start(f32[7,128,128]{2,1,0:T(8,128)} %get-tuple-element.15), channel_id=1, source_target_pairs={{0,2},{1,3},{2,4},{3,5},{4,6},{5,7},{6,8},{7,9},{8,10},{9,11},{10,... | collective-permute-start | bytes 1376264 | tf_op jit(solution)/shard_map/ppermute | solution.py:29
  8.6 0.0 collective-permute-start.5
  8.6 0.8 copy.6
  9.4 0.6 gather_fusion
  10.0 0.9 convert_reduce_fusion
  10.8 0.6 pad_add_fusion.meta
  11.5 1.2 %collective-permute-done.x0 = f32[1,6,128,128]{3,2,1,0:T(8,128)S(1)} collective-permute-done((f32[1,6,128,128]{3,2,1,0:T(8,128)S(1)}, f32[1,6,128,128]{3,2,1,0:T(8,128)S(1)}, u32[]{:S(2)}, u32[]{:S(2)}) %collective-permute-start) | collective-permute-done | bytes 393248 | tf_op jit(solution)/shard_map/ppermute | solution.py:29
  12.7 3.8 %collective-permute-start.2 = (f32[1,6,128,128]{3,2,1,0:T(8,128)S(1)}, f32[1,6,128,128]{3,2,1,0:T(8,128)S(1)}, u32[]{:S(2)}, u32[]{:S(2)}) collective-permute-start(f32[1,6,128,128]{3,2,1,0:T(8,128)S(1)} %collective-permute-done.x0), channel_id=1, source_target_pairs={{0,2},{1,31},{2,4},{3,1},{4,6},{5,3},{6,8},{7,5},{8,10},{9,7},{10,... | collective-permute-start | bytes 1179656 | tf_op jit(solution)/shard_map/ppermute | solution.py:29
  16.5 4.7 %collective-permute-done.1.x1 = f32[1,6,128,128]{3,2,1,0:T(8,128)S(1)} collective-permute-done((f32[1,6,128,128]{3,2,1,0:T(8,128)S(1)}, f32[1,6,128,128]{3,2,1,0:T(8,128)S(1)}, u32[]{:S(2)}, u32[]{:S(2)}) %collective-permute-start.1) | collective-permute-done | bytes 393248 | tf_op jit(solution)/shard_map/ppermute | solution.py:29
  21.1 2.6 %collective-permute-start.3 = (f32[1,6,128,128]{3,2,1,0:T(8,128)S(1)}, f32[1,6,128,128]{3,2,1,0:T(8,128)S(1)}, u32[]{:S(2)}, u32[]{:S(2)}) collective-permute-start(f32[1,6,128,128]{3,2,1,0:T(8,128)S(1)} %collective-permute-done.1.x1), channel_id=1, source_target_pairs={{0,2},{1,31},{2,4},{3,1},{4,6},{5,3},{6,8},{7,5},{8,10},{9,7},{10,... | collective-permute-start | bytes 1179656 | tf_op jit(solution)/shard_map/ppermute | solution.py:29
  23.8 1.3 %collective-permute-start.6 = (f32[3,128,128]{2,1,0:T(8,128)S(1)}, f32[3,128,128]{2,1,0:T(8,128)S(1)}, u32[]{:S(2)}, u32[]{:S(2)}) collective-permute-start(f32[3,128,128]{2,1,0:T(8,128)S(1)} %pad_maximum_fusion), channel_id=1, source_target_pairs={{0,4},{1,3},{2,6},{3,5},{4,8},{5,7},{6,10},{7,9},{8,12},{9,11},{10... | collective-permute-start | bytes 589832 | tf_op jit(solution)/shard_map/ppermute | solution.py:29
  25.1 0.0 collective-permute-done.4.zu
  25.1 0.7 collective-permute-done.5.zd
  25.8 0.0 collective-permute-done.2.n0
  25.9 4.7 %collective-permute-done.3.n1 = f32[1,6,128,128]{3,2,1,0:T(8,128)S(1)} collective-permute-done((f32[1,6,128,128]{3,2,1,0:T(8,128)S(1)}, f32[1,6,128,128]{3,2,1,0:T(8,128)S(1)}, u32[]{:S(2)}, u32[]{:S(2)}) %collective-permute-start.3) | collective-permute-done | bytes 393248 | tf_op jit(solution)/shard_map/ppermute | solution.py:29
  30.6 0.8 copy-done.9
  31.4 6.0 %shard_map.61 = (f32[1,6,128,128]{3,2,1,0:T(8,128)}, f32[1,6,128,128]{3,2,1,0:T(8,128)}, f32[7,128,128]{2,1,0:T(8,128)}, f32[7,128,128]{2,1,0:T(8,128)}) custom-call(s32[15]{0:T(128)} %pad_add_fusion.meta, f32[2,6,128,128]{3,2,1,0:T(8,128)} %s.1, f32[2,6,128,128]{3,2,1,0:T(8,128)} %z.7, f32[1,6,128,128]{3,2,1,0:T(8,128)} %copy-done, ...), custom_call_target="tpu_custom_call" | custom-call | flops 2000000000 | bytes 4194304 | tf_op jit(solution)/shard_map/pallas_call | solution.py:352
  37.4 0.7 collective-permute-start.11
  38.1 3.2 %collective-permute-start.7 = (f32[3,128,128]{2,1,0:T(8,128)S(1)}, f32[3,128,128]{2,1,0:T(8,128)S(1)}, u32[]{:S(2)}, u32[]{:S(2)}) collective-permute-start(f32[3,128,128]{2,1,0:T(8,128)S(1)} %pad_maximum_fusion.1), channel_id=1, source_target_pairs={{0,30},{1,29},{2,0},{3,31},{4,2},{5,1},{6,4},{7,3},{8,6},{9,5},{10... | collective-permute-start | bytes 589832 | tf_op jit(solution)/shard_map/ppermute | solution.py:29
  41.3 0.0 collective-permute-start.8
  41.3 2.6 %collective-permute-start.9 = (f32[7,128,128]{2,1,0:T(8,128)}, f32[7,128,128]{2,1,0:T(8,128)S(1)}, u32[]{:S(2)}, u32[]{:S(2)}) collective-permute-start(f32[7,128,128]{2,1,0:T(8,128)} %get-tuple-element.27), channel_id=1, source_target_pairs={{0,30},{1,31},{2,0},{3,1},{4,2},{5,3},{6,4},{7,5},{8,6},{9,7},{10,... | collective-permute-start | bytes 1376264 | tf_op jit(solution)/shard_map/ppermute | solution.py:29
  43.9 0.0 collective-permute-done.6.fu
  43.9 1.3 %collective-permute-start.10 = (f32[1,6,128,128]{3,2,1,0:T(8,128)}, f32[1,6,128,128]{3,2,1,0:T(8,128)S(1)}, u32[]{:S(2)}, u32[]{:S(2)}) collective-permute-start(f32[1,6,128,128]{3,2,1,0:T(8,128)} %get-tuple-element.24.p0), channel_id=1, source_target_pairs={{0,1},{1,0},{2,3},{3,2},{4,5},{5,4},{6,7},{7,6},{8,9},{9,8},{10,11... | collective-permute-start | bytes 1179656 | tf_op jit(solution)/shard_map/ppermute | solution.py:29
  45.2 0.0 collective-permute-done.7.fd
  45.2 0.7 copy-done.15
  45.9 5.3 %shard_map.60 = (bf16[1024,512]{1,0:T(8,128)(2,1)}, bf16[512,512]{1,0:T(8,128)(2,1)}, bf16[512,512]{1,0:T(8,128)(2,1)}, bf16[768,512]{1,0:T(8,128)(2,1)}, bf16[7...) custom-call(s32[15]{0:T(128)} %pad_add_fusion.meta, f32[2,6,128,128]{3,2,1,0:T(8,128)} %z.7, ...), custom_call_target="tpu_custom_call" | custom-call | flops 2000000000 | bytes 4194304 | tf_op jit(solution)/shard_map/pallas_call | solution.py:352
  51.2 0.0 collective-permute-done.11.x1
  51.3 3.1 %collective-permute-done.10.x0 = f32[1,6,128,128]{3,2,1,0:T(8,128)S(1)} collective-permute-done((f32[1,6,128,128]{3,2,1,0:T(8,128)}, f32[1,6,128,128]{3,2,1,0:T(8,128)S(1)}, u32[]{:S(2)}, u32[]{:S(2)}) %collective-permute-start.10) | collective-permute-done | bytes 393248 | tf_op jit(solution)/shard_map/ppermute | solution.py:29
  54.4 2.3 %collective-permute-start.14 = (f32[3,128,128]{2,1,0:T(8,128)S(1)}, f32[3,128,128]{2,1,0:T(8,128)S(1)}, u32[]{:S(2)}, u32[]{:S(2)}) collective-permute-start(f32[3,128,128]{2,1,0:T(8,128)S(1)} %pad_maximum_fusion.2), channel_id=1, source_target_pairs={{0,4},{1,3},{2,6},{3,5},{4,8},{5,7},{6,10},{7,9},{8,12},{9,11},{10... | collective-permute-start | bytes 589832 | tf_op jit(solution)/shard_map/ppermute | solution.py:29
  56.7 4.1 %collective-permute-start.12 = (f32[1,6,128,128]{3,2,1,0:T(8,128)S(1)}, f32[1,6,128,128]{3,2,1,0:T(8,128)S(1)}, u32[]{:S(2)}, u32[]{:S(2)}) collective-permute-start(f32[1,6,128,128]{3,2,1,0:T(8,128)S(1)} %collective-permute-done.10.x0), channel_id=1, source_target_pairs={{0,2},{1,31},{2,4},{3,1},{4,6},{5,3},{6,8},{7,5},{8,10},{9,7},{10,... | collective-permute-start | bytes 1179656 | tf_op jit(solution)/shard_map/ppermute | solution.py:29
  60.8 0.0 collective-permute-start.13
  60.9 0.0 collective-permute-done.8.pu
  60.9 0.7 collective-permute-start.15
  61.6 0.0 collective-permute-done.9.pd
  61.6 0.1 copy-done.6
  61.7 0.7 copy-done.7
  62.4 8.3 %shard_map.62.early = f32[16,256,256]{2,1,0:T(8,128)} custom-call(s32[15]{0:T(128)} %pad_add_fusion.meta, bf16[1024,512]{1,0:T(8,128)(2,1)} %get-tuple-element.20.t_own, bf16[512,512]{1,0:T(8,128)(2,1)} %get-tuple-element.21.t_up, bf16[512,512]{1,0:T(8,128)(2,1)} %get-tuple-element.22.t_down, bf16[768,512]{1,0:T(8,128)(2,1)} %get-tuple-element.23.t_swap, ...), custom_call_target="tpu_custom_call" | custom-call | flops 4000000000 | bytes 4194304 | tf_op jit(solution)/shard_map/pallas_call | solution.py:352
  70.7 0.0 collective-permute-done.14.fu
  70.7 6.0 %collective-permute-done.15.fd = f32[3,128,128]{2,1,0:T(8,128)S(1)} collective-permute-done((f32[3,128,128]{2,1,0:T(8,128)S(1)}, f32[3,128,128]{2,1,0:T(8,128)S(1)}, u32[]{:S(2)}, u32[]{:S(2)}) %collective-permute-start.15) | collective-permute-done | bytes 196640 | tf_op jit(solution)/shard_map/ppermute | solution.py:29
  76.7 0.0 collective-permute-done.13.n1
  76.8 0.7 copy-done.14
  77.4 0.1 copy-done.10
  77.6 0.1 copy-done.11
  77.7 8.0 %shard_map.63 = (f32[2,6,128,128]{3,2,1,0:T(8,128)}, f32[2,6,128,128]{3,2,1,0:T(8,128)}) custom-call(s32[15]{0:T(128)} %pad_add_fusion.meta, f32[2,6,128,128]{3,2,1,0:T(8,128)} %z.7, bf16[2,128,2048]{2,1,0:T(8,128)(2,1)} %get-tuple-element.17.z_own, bf16[768,512]{1,0:T(8,128)(2,1)} %get-tuple-element.18.t_near, bf16[512,512]{1,0:T(8,128)(2,1)} %get-tuple-element.19.t_far, ...), custom_call_target="tpu_custom_call" | custom-call | flops 4000000000 | bytes 4194304 | tf_op jit(solution)/shard_map/pallas_call | solution.py:352
  (37 shorter events, 0.2 us)
Async XLA Ops:
  1.8 10.9 %collective-permute-start = (f32[1,6,128,128]{3,2,1,0:T(8,128)S(1)}, f32[1,6,128,128]{3,2,1,0:T(8,128)S(1)}, u32[]{:S(2)}, u32[]{:S(2)}) collective-permute-start(f32[1,6,128,128]{3,2,1,0:T(8,128)S(1)} %get-tuple-element.29), channel_id=1, source_target_pairs={{0,1},{1,0},{2,3},{3,2},{4,5},{5,4},{6,7},{7,6},{8,9},{9,8},{10,11... | collective-permute-start | bytes 1179656 | tf_op jit(solution)/shard_map/ppermute | solution.py:29
  3.9 17.2 %collective-permute-start.1 = (f32[1,6,128,128]{3,2,1,0:T(8,128)S(1)}, f32[1,6,128,128]{3,2,1,0:T(8,128)S(1)}, u32[]{:S(2)}, u32[]{:S(2)}) collective-permute-start(f32[1,6,128,128]{3,2,1,0:T(8,128)S(1)} %get-tuple-element.28), channel_id=1, source_target_pairs={{0,1},{1,0},{2,3},{3,2},{4,5},{5,4},{6,7},{7,6},{8,9},{9,8},{10,11... | collective-permute-start | bytes 1179656 | tf_op jit(solution)/shard_map/ppermute | solution.py:29
  6.1 19.1 %collective-permute-start.4 = (f32[7,128,128]{2,1,0:T(8,128)}, f32[7,128,128]{2,1,0:T(8,128)S(1)}, u32[]{:S(2)}, u32[]{:S(2)}) collective-permute-start(f32[7,128,128]{2,1,0:T(8,128)} %get-tuple-element.15), channel_id=1, source_target_pairs={{0,2},{1,3},{2,4},{3,5},{4,6},{5,7},{6,8},{7,9},{8,10},{9,11},{10,... | collective-permute-start | bytes 1376264 | tf_op jit(solution)/shard_map/ppermute | solution.py:29
  8.6 17.2 %collective-permute-start.5 = (f32[7,128,128]{2,1,0:T(8,128)}, f32[7,128,128]{2,1,0:T(8,128)S(1)}, u32[]{:S(2)}, u32[]{:S(2)}) collective-permute-start(f32[7,128,128]{2,1,0:T(8,128)} %get-tuple-element.16), channel_id=1, source_target_pairs={{0,30},{1,31},{2,0},{3,1},{4,2},{5,3},{6,4},{7,5},{8,6},{9,7},{10,... | collective-permute-start | bytes 1376264 | tf_op jit(solution)/shard_map/ppermute | solution.py:29
  12.7 17.9 %copy-start = (f32[1,6,128,128]{3,2,1,0:T(8,128)}, f32[1,6,128,128]{3,2,1,0:T(8,128)S(1)}, u32[]{:S(2)}) copy-start(f32[1,6,128,128]{3,2,1,0:T(8,128)S(1)} %collective-permute-done.x0) | copy-start | bytes 1179652
  12.7 13.1 %collective-permute-start.2 = (f32[1,6,128,128]{3,2,1,0:T(8,128)S(1)}, f32[1,6,128,128]{3,2,1,0:T(8,128)S(1)}, u32[]{:S(2)}, u32[]{:S(2)}) collective-permute-start(f32[1,6,128,128]{3,2,1,0:T(8,128)S(1)} %collective-permute-done.x0), channel_id=1, source_target_pairs={{0,2},{1,31},{2,4},{3,1},{4,6},{5,3},{6,8},{7,5},{8,10},{9,7},{10,... | collective-permute-start | bytes 1179656 | tf_op jit(solution)/shard_map/ppermute | solution.py:29
  21.1 9.5 %copy-start.1 = (f32[1,6,128,128]{3,2,1,0:T(8,128)}, f32[1,6,128,128]{3,2,1,0:T(8,128)S(1)}, u32[]{:S(2)}) copy-start(f32[1,6,128,128]{3,2,1,0:T(8,128)S(1)} %collective-permute-done.1.x1) | copy-start | bytes 1179652
  21.1 9.5 %collective-permute-start.3 = (f32[1,6,128,128]{3,2,1,0:T(8,128)S(1)}, f32[1,6,128,128]{3,2,1,0:T(8,128)S(1)}, u32[]{:S(2)}, u32[]{:S(2)}) collective-permute-start(f32[1,6,128,128]{3,2,1,0:T(8,128)S(1)} %collective-permute-done.1.x1), channel_id=1, source_target_pairs={{0,2},{1,31},{2,4},{3,1},{4,6},{5,3},{6,8},{7,5},{8,10},{9,7},{10,... | collective-permute-start | bytes 1179656 | tf_op jit(solution)/shard_map/ppermute | solution.py:29
  23.8 20.1 %collective-permute-start.6 = (f32[3,128,128]{2,1,0:T(8,128)S(1)}, f32[3,128,128]{2,1,0:T(8,128)S(1)}, u32[]{:S(2)}, u32[]{:S(2)}) collective-permute-start(f32[3,128,128]{2,1,0:T(8,128)S(1)} %pad_maximum_fusion), channel_id=1, source_target_pairs={{0,4},{1,3},{2,6},{3,5},{4,8},{5,7},{6,10},{7,9},{8,12},{9,11},{10... | collective-permute-start | bytes 589832 | tf_op jit(solution)/shard_map/ppermute | solution.py:29
  25.1 5.5 %copy-start.4 = (f32[7,128,128]{2,1,0:T(8,128)}, f32[7,128,128]{2,1,0:T(8,128)S(1)}, u32[]{:S(2)}) copy-start(f32[7,128,128]{2,1,0:T(8,128)S(1)} %collective-permute-done.4.zu) | copy-start | bytes 1376260
  25.8 4.8 %copy-start.5 = (f32[7,128,128]{2,1,0:T(8,128)}, f32[7,128,128]{2,1,0:T(8,128)S(1)}, u32[]{:S(2)}) copy-start(f32[7,128,128]{2,1,0:T(8,128)S(1)} %collective-permute-done.5.zd) | copy-start | bytes 1376260
  25.9 4.8 %copy-start.8 = (f32[1,6,128,128]{3,2,1,0:T(8,128)}, f32[1,6,128,128]{3,2,1,0:T(8,128)S(1)}, u32[]{:S(2)}) copy-start(f32[1,6,128,128]{3,2,1,0:T(8,128)S(1)} %collective-permute-done.2.n0) | copy-start | bytes 1179652
  30.6 0.8 copy-start.9
  37.4 13.8 %collective-permute-start.11 = (f32[1,6,128,128]{3,2,1,0:T(8,128)}, f32[1,6,128,128]{3,2,1,0:T(8,128)S(1)}, u32[]{:S(2)}, u32[]{:S(2)}) collective-permute-start(f32[1,6,128,128]{3,2,1,0:T(8,128)} %get-tuple-element.25.p1), channel_id=1, source_target_pairs={{0,1},{1,0},{2,3},{3,2},{4,5},{5,4},{6,7},{7,6},{8,9},{9,8},{10,11... | collective-permute-start | bytes 1179656 | tf_op jit(solution)/shard_map/ppermute | solution.py:29
  38.1 7.1 %collective-permute-start.7 = (f32[3,128,128]{2,1,0:T(8,128)S(1)}, f32[3,128,128]{2,1,0:T(8,128)S(1)}, u32[]{:S(2)}, u32[]{:S(2)}) collective-permute-start(f32[3,128,128]{2,1,0:T(8,128)S(1)} %pad_maximum_fusion.1), channel_id=1, source_target_pairs={{0,30},{1,29},{2,0},{3,31},{4,2},{5,1},{6,4},{7,3},{8,6},{9,5},{10... | collective-permute-start | bytes 589832 | tf_op jit(solution)/shard_map/ppermute | solution.py:29
  41.3 19.6 %collective-permute-start.8 = (f32[7,128,128]{2,1,0:T(8,128)}, f32[7,128,128]{2,1,0:T(8,128)S(1)}, u32[]{:S(2)}, u32[]{:S(2)}) collective-permute-start(f32[7,128,128]{2,1,0:T(8,128)} %get-tuple-element.26), channel_id=1, source_target_pairs={{0,2},{1,3},{2,4},{3,5},{4,6},{5,7},{6,8},{7,9},{8,10},{9,11},{10,... | collective-permute-start | bytes 1376264 | tf_op jit(solution)/shard_map/ppermute | solution.py:29
  41.3 20.3 %collective-permute-start.9 = (f32[7,128,128]{2,1,0:T(8,128)}, f32[7,128,128]{2,1,0:T(8,128)S(1)}, u32[]{:S(2)}, u32[]{:S(2)}) collective-permute-start(f32[7,128,128]{2,1,0:T(8,128)} %get-tuple-element.27), channel_id=1, source_target_pairs={{0,30},{1,31},{2,0},{3,1},{4,2},{5,3},{6,4},{7,5},{8,6},{9,7},{10,... | collective-permute-start | bytes 1376264 | tf_op jit(solution)/shard_map/ppermute | solution.py:29
  43.9 1.3 %copy-start.12 = (f32[3,128,128]{2,1,0:T(8,128)}, f32[3,128,128]{2,1,0:T(8,128)S(1)}, u32[]{:S(2)}) copy-start(f32[3,128,128]{2,1,0:T(8,128)S(1)} %collective-permute-done.6.fu) | copy-start | bytes 589828
  43.9 10.4 %collective-permute-start.10 = (f32[1,6,128,128]{3,2,1,0:T(8,128)}, f32[1,6,128,128]{3,2,1,0:T(8,128)S(1)}, u32[]{:S(2)}, u32[]{:S(2)}) collective-permute-start(f32[1,6,128,128]{3,2,1,0:T(8,128)} %get-tuple-element.24.p0), channel_id=1, source_target_pairs={{0,1},{1,0},{2,3},{3,2},{4,5},{5,4},{6,7},{7,6},{8,9},{9,8},{10,11... | collective-permute-start | bytes 1179656 | tf_op jit(solution)/shard_map/ppermute | solution.py:29
  45.2 0.7 copy-start.15
  51.2 10.4 %copy-start.2 = (f32[1,6,128,128]{3,2,1,0:T(8,128)}, f32[1,6,128,128]{3,2,1,0:T(8,128)S(1)}, u32[]{:S(2)}) copy-start(f32[1,6,128,128]{3,2,1,0:T(8,128)S(1)} %collective-permute-done.11.x1) | copy-start | bytes 1179652
  54.4 7.3 %copy-start.3 = (f32[1,6,128,128]{3,2,1,0:T(8,128)}, f32[1,6,128,128]{3,2,1,0:T(8,128)S(1)}, u32[]{:S(2)}) copy-start(f32[1,6,128,128]{3,2,1,0:T(8,128)S(1)} %collective-permute-done.10.x0) | copy-start | bytes 1179652
  54.4 16.3 %collective-permute-start.14 = (f32[3,128,128]{2,1,0:T(8,128)S(1)}, f32[3,128,128]{2,1,0:T(8,128)S(1)}, u32[]{:S(2)}, u32[]{:S(2)}) collective-permute-start(f32[3,128,128]{2,1,0:T(8,128)S(1)} %pad_maximum_fusion.2), channel_id=1, source_target_pairs={{0,4},{1,3},{2,6},{3,5},{4,8},{5,7},{6,10},{7,9},{8,12},{9,11},{10... | collective-permute-start | bytes 589832 | tf_op jit(solution)/shard_map/ppermute | solution.py:29
  56.7 20.0 %collective-permute-start.12 = (f32[1,6,128,128]{3,2,1,0:T(8,128)S(1)}, f32[1,6,128,128]{3,2,1,0:T(8,128)S(1)}, u32[]{:S(2)}, u32[]{:S(2)}) collective-permute-start(f32[1,6,128,128]{3,2,1,0:T(8,128)S(1)} %collective-permute-done.10.x0), channel_id=1, source_target_pairs={{0,2},{1,31},{2,4},{3,1},{4,6},{5,3},{6,8},{7,5},{8,10},{9,7},{10,... | collective-permute-start | bytes 1179656 | tf_op jit(solution)/shard_map/ppermute | solution.py:29
  60.8 15.9 %collective-permute-start.13 = (f32[1,6,128,128]{3,2,1,0:T(8,128)S(1)}, f32[1,6,128,128]{3,2,1,0:T(8,128)S(1)}, u32[]{:S(2)}, u32[]{:S(2)}) collective-permute-start(f32[1,6,128,128]{3,2,1,0:T(8,128)S(1)} %collective-permute-done.11.x1), channel_id=1, source_target_pairs={{0,2},{1,31},{2,4},{3,1},{4,6},{5,3},{6,8},{7,5},{8,10},{9,7},{10,... | collective-permute-start | bytes 1179656 | tf_op jit(solution)/shard_map/ppermute | solution.py:29
  60.9 0.8 copy-start.6
  60.9 15.8 %collective-permute-start.15 = (f32[3,128,128]{2,1,0:T(8,128)S(1)}, f32[3,128,128]{2,1,0:T(8,128)S(1)}, u32[]{:S(2)}, u32[]{:S(2)}) collective-permute-start(f32[3,128,128]{2,1,0:T(8,128)S(1)} %pad_maximum_fusion.3), channel_id=1, source_target_pairs={{0,30},{1,29},{2,0},{3,31},{4,2},{5,1},{6,4},{7,3},{8,6},{9,5},{10... | collective-permute-start | bytes 589832 | tf_op jit(solution)/shard_map/ppermute | solution.py:29
  61.6 0.8 copy-start.7
  70.7 6.1 %copy-start.13 = (f32[3,128,128]{2,1,0:T(8,128)}, f32[3,128,128]{2,1,0:T(8,128)S(1)}, u32[]{:S(2)}) copy-start(f32[3,128,128]{2,1,0:T(8,128)S(1)} %collective-permute-done.14.fu) | copy-start | bytes 589828
  76.7 0.7 copy-start.14
  76.7 0.8 copy-start.10
  76.8 1.0 %copy-start.11 = (f32[1,6,128,128]{3,2,1,0:T(8,128)}, f32[1,6,128,128]{3,2,1,0:T(8,128)S(1)}, u32[]{:S(2)}) copy-start(f32[1,6,128,128]{3,2,1,0:T(8,128)S(1)} %collective-permute-done.13.n1) | copy-start | bytes 1179652

commit v2 on v1

--- a/solution.py
+++ b/solution.py
@@ -15,6 +15,7 @@
 COLS = OWN + 2 * REACH
 PAIRS = COLS // 2
 SIDE = 3
+VMEM_LIMIT = 24 << 20
 F32 = jnp.float32
 BF16 = jnp.bfloat16
 
@@ -330,8 +331,12 @@
             refined[i, slot] = z[i, slot] + 0.5 * dense[i, rows.dense_slot(i, slot)]
 
 
-def pick(rows, layout):
-    return jnp.concatenate([rows[r][0, s : s + 1] for r, s in layout], axis=0)
+def far(rows):
+    first = lax.optimization_barrier(
+        jnp.concatenate([rows[0][0, s : s + 1] for r, s in FAR_UP + FAR_DOWN if r == 0], axis=0)
+    )
+    last = [rows[1][0, s : s + 1] for r, s in FAR_UP + FAR_DOWN if r == 1]
+    return jnp.concatenate([first[:1], *last[:2]], axis=0), jnp.concatenate([first[1:], last[2]], axis=0)
 
 
 def body(correlation, factor, pattern):
@@ -355,8 +360,9 @@
             out_specs=jax.tree.map(lambda _: vmem, outs),
             out_shape=outs,
             scratch_shapes=scratch,
+            compiler_params=pltpu.CompilerParams(vmem_limit_bytes=VMEM_LIMIT),
             cost_estimate=pl.CostEstimate(flops=flops, bytes_accessed=4 << 20, transcendentals=0),
-        )(*ins)
+        )(*ins[:scalars], *(pltpu.with_memory_space_constraint(v, pltpu.VMEM) for v in ins[scalars:]))
 
     def shape(*dims, dtype=F32):
         return jax.ShapeDtypeStruct(dims, dtype)
@@ -372,8 +378,8 @@
     zu, zd = call(pack_kernel, (factor,), (seven, seven), [], 1000, 0)
     zu, zd = send(zu, up), send(zd, down)
     n = [send(x[r], near) for r in range(OWN)]
-    zfu = send(pick(x, FAR_UP), far_up)
-    zfd = send(pick(x, FAR_DOWN), far_down)
+    zfu, zfd = far(x)
+    zfu, zfd = send(zfu, far_up), send(zfd, far_down)
     p0, p1, pu, pd = call(
         product_kernel,
         (meta, correlation, factor, *x, *n, zu, zd),
@@ -384,8 +390,8 @@
     px = [send(v, swap) for v in (p0, p1)]
     pu, pd = send(pu, up), send(pd, down)
     pn = [send(v, near) for v in px]
-    pfu = send(pick(px, FAR_UP), far_up)
-    pfd = send(pick(px, FAR_DOWN), far_down)
+    pfu, pfd = far(px)
+    pfu, pfd = send(pfu, far_up), send(pfd, far_down)
 
     def turned(columns):
         return shape(columns * tile, 4 * tile, dtype=BF16)

time: 86 us -> 79.8 us (0.928)
  Pallas kernels: 29.7 us -> 15.8 us
  waiting for transfers between devices: 20.5 us -> 29.9 us
  local copies, waits for them, and re-layouts: 5.79 us -> 4.73 us
    pallas_call x5, Pallas kernels: 29.7 us -> 15.8 us  [call(): pl.pallas_call(kernel, in_specs=[smem] * scalars + [vmem] * (len(ins) - s...]
    ppermute x16, waiting for transfers between devices: 20.5 us -> 29.9 us  [send(): return lax.ppermute(value, AXES, [(i, to(i) % count) for i in range(count)])]
    unnamed x33 -> x7, local copies, waits for them, and re-layouts: 4.01 us -> 1.92 us
    slice x1, local copies, waits for them, and re-layouts: 1.17 us -> 2.16 us  [body(): x = [send(factor[r:r + 1], swap) for r in range(OWN)]]
  transfers between devices with their start and end apart: 16 -> 16, of which waited for: 6 -> 6; matrix products, arithmetic and copies ran while one was open for 3% -> 3% of each run, Pallas kernels for 25% -> 13%
where the time goes in v2:
time: 79.8 us; the launch traced here: 79.5 us
  waiting for transfers between devices  29.9 us (37%)
  starting transfers between devices  27.3 us (34%)
  Pallas kernels  15.8 us (20%)
  local copies, waits for them, and re-layouts  4.73 us (6%)
  other arithmetic  1.05 us (1%)
  between operations  0.82 us (1%)
    ppermute x16, waiting for transfers between devices, send(): return lax.ppermute(value, AXES, [(i, to(i) % count) for i in range(count)])  29.9 us
    ppermute x16, starting transfers between devices, send(): return lax.ppermute(value, AXES, [(i, to(i) % count) for i in range(count)])  27.3 us
    pallas_call x5, Pallas kernels, call(): pl.pallas_call(kernel, in_specs=[smem] * scalars + [vmem] * (len(ins) - s...  15.8 us
    slice x1, local copies, waits for them, and re-layouts, body(): x = [send(factor[r:r + 1], swap) for r in range(OWN)]  2.16 us
    unnamed x7, local copies, waits for them, and re-layouts  1.92 us
  transfers between devices with their start and end apart: 16, of which 6 were waited for; matrix products, arithmetic and copies ran while one was open for 3% of the time, Pallas kernels for 13%

profile of v2, /device:TPU:1, one launch (start us, length us, event | category | flops | bytes accessed | tf_op | source)
XLA Modules:
  0.0 79.5 jit_solution(15939009884327500039)
XLA Ops:
  0.6 0.0 copy-start.1
  0.6 0.0 copy-start.2
  0.7 2.2 %fusion.7 = (f32[1,6,128,128]{3,2,1,0:T(8,128)}, f32[1,6,128,128]{3,2,1,0:T(8,128)}) fusion(f32[2,6,128,128]{3,2,1,0:T(8,128)} %z.7), kind=kLoop, calls=%fused_computation.40 | loop fusion | bytes 1572864 | tf_op jit(solution)/shard_map/slice | solution.py:377
  2.8 2.0 %collective-permute-start = (f32[1,6,128,128]{3,2,1,0:T(8,128)}, f32[1,6,128,128]{3,2,1,0:T(8,128)S(1)}, u32[]{:S(2)}, u32[]{:S(2)}) collective-permute-start(f32[1,6,128,128]{3,2,1,0:T(8,128)} %get-tuple-element.29), channel_id=1, source_target_pairs={{0,1},{1,0},{2,3},{3,2},{4,5},{5,4},{6,7},{7,6},{8,9},{9,8},{10,11... | collective-permute-start | bytes 1179656 | tf_op jit(solution)/shard_map/ppermute | solution.py:30
  4.8 0.0 collective-permute-start.1
  4.9 0.0 copy-start
  4.9 1.1 %copy-done = f32[2,6,128,128]{3,2,1,0:T(8,128)S(1)} copy-done((f32[2,6,128,128]{3,2,1,0:T(8,128)S(1)}, f32[2,6,128,128]{3,2,1,0:T(8,128)}, u32[]{:S(2)}) %copy-start) | copy-done | bytes 786456
  6.0 1.0 %shard_map.59 = (f32[7,128,128]{2,1,0:T(8,128)}, f32[7,128,128]{2,1,0:T(8,128)}) custom-call(f32[2,6,128,128]{3,2,1,0:T(8,128)S(1)} %copy-done), custom_call_target="tpu_custom_call" | custom-call | flops 1000 | bytes 4194304 | tf_op jit(solution)/shard_map/pallas_call | solution.py:357
  7.0 2.6 %collective-permute-start.4 = (f32[7,128,128]{2,1,0:T(8,128)}, f32[7,128,128]{2,1,0:T(8,128)S(1)}, u32[]{:S(2)}, u32[]{:S(2)}) collective-permute-start(f32[7,128,128]{2,1,0:T(8,128)} %get-tuple-element.15), channel_id=1, source_target_pairs={{0,2},{1,3},{2,4},{3,5},{4,6},{5,7},{6,8},{7,9},{8,10},{9,11},{10,... | collective-permute-start | bytes 1376264 | tf_op jit(solution)/shard_map/ppermute | solution.py:30
  9.6 0.0 collective-permute-start.5
  9.6 0.8 copy.6
  10.4 0.6 gather_fusion
  11.0 0.9 %convert_reduce_fusion = s32[14]{0:T(128)S(1)} fusion(s32[14,6]{1,0:T(8,128)S(1)} %gather_fusion, s32[5]{0:T(128)} %constant.54.clone, s32[14]{0:T(128)S(1)} %and_select_fusion), kind=kLoop, calls=%fused_computation.27 | loop fusion | flops 1176 | bytes 412 | tf_op jit(solution)/shard_map/reduce_sum | solution.py:350
  11.8 0.1 pad_add_fusion.meta
  11.9 2.0 %collective-permute-done.x0 = f32[1,6,128,128]{3,2,1,0:T(8,128)S(1)} collective-permute-done((f32[1,6,128,128]{3,2,1,0:T(8,128)}, f32[1,6,128,128]{3,2,1,0:T(8,128)S(1)}, u32[]{:S(2)}, u32[]{:S(2)}) %collective-permute-start) | collective-permute-done | bytes 393248 | tf_op jit(solution)/shard_map/ppermute | solution.py:30
  13.9 3.8 %collective-permute-start.2 = (f32[1,6,128,128]{3,2,1,0:T(8,128)S(1)}, f32[1,6,128,128]{3,2,1,0:T(8,128)S(1)}, u32[]{:S(2)}, u32[]{:S(2)}) collective-permute-start(f32[1,6,128,128]{3,2,1,0:T(8,128)S(1)} %collective-permute-done.x0), channel_id=1, source_target_pairs={{0,2},{1,31},{2,4},{3,1},{4,6},{5,3},{6,8},{7,5},{8,10},{9,7},{10,... | collective-permute-start | bytes 1179656 | tf_op jit(solution)/shard_map/ppermute | solution.py:30
  17.6 4.7 %collective-permute-done.1.x1 = f32[1,6,128,128]{3,2,1,0:T(8,128)S(1)} collective-permute-done((f32[1,6,128,128]{3,2,1,0:T(8,128)}, f32[1,6,128,128]{3,2,1,0:T(8,128)S(1)}, u32[]{:S(2)}, u32[]{:S(2)}) %collective-permute-start.1) | collective-permute-done | bytes 393248 | tf_op jit(solution)/shard_map/ppermute | solution.py:30
  22.3 2.6 %collective-permute-start.3 = (f32[1,6,128,128]{3,2,1,0:T(8,128)S(1)}, f32[1,6,128,128]{3,2,1,0:T(8,128)S(1)}, u32[]{:S(2)}, u32[]{:S(2)}) collective-permute-start(f32[1,6,128,128]{3,2,1,0:T(8,128)S(1)} %collective-permute-done.1.x1), channel_id=1, source_target_pairs={{0,2},{1,31},{2,4},{3,1},{4,6},{5,3},{6,8},{7,5},{8,10},{9,7},{10,... | collective-permute-start | bytes 1179656 | tf_op jit(solution)/shard_map/ppermute | solution.py:30
  25.0 1.3 %collective-permute-start.6 = (f32[3,128,128]{2,1,0:T(8,128)S(1)}, f32[3,128,128]{2,1,0:T(8,128)S(1)}, u32[]{:S(2)}, u32[]{:S(2)}) collective-permute-start(f32[3,128,128]{2,1,0:T(8,128)S(1)} %pad_maximum_fusion.1), channel_id=1, source_target_pairs={{0,4},{1,3},{2,6},{3,5},{4,8},{5,7},{6,10},{7,9},{8,12},{9,11},{10... | collective-permute-start | bytes 589832 | tf_op jit(solution)/shard_map/ppermute | solution.py:30
  26.3 0.0 collective-permute-done.4.zu
  26.3 0.5 collective-permute-done.5.zd
  26.8 0.0 collective-permute-done.2.n0
  26.8 4.9 %collective-permute-done.3.n1 = f32[1,6,128,128]{3,2,1,0:T(8,128)S(1)} collective-permute-done((f32[1,6,128,128]{3,2,1,0:T(8,128)S(1)}, f32[1,6,128,128]{3,2,1,0:T(8,128)S(1)}, u32[]{:S(2)}, u32[]{:S(2)}) %collective-permute-start.3) | collective-permute-done | bytes 393248 | tf_op jit(solution)/shard_map/ppermute | solution.py:30
  31.8 0.0 copy-done.1
  31.8 0.0 copy-done.2
  31.8 3.4 %shard_map.61 = (f32[1,6,128,128]{3,2,1,0:T(8,128)S(1)}, f32[1,6,128,128]{3,2,1,0:T(8,128)S(1)}, f32[7,128,128]{2,1,0:T(8,128)S(1)}, f32[7,128,128]{2,1,0:T(8,128)S(1)}) custom-call(s32[15]{0:T(128)S(1)} %pad_add_fusion.meta, f32[2,6,128,128]{3,2,1,0:T(8,128)S(1)} %copy-done.2, f32[2,6,128,128]{3,2,1,0:T(8,128)S(1)} %copy-done.1, ...), custom_call_target="tpu_custom_call" | custom-call | flops 2000000000 | bytes 4194304 | tf_op jit(solution)/shard_map/pallas_call | solution.py:357
  35.1 0.5 collective-permute-start.10
  35.7 3.4 %collective-permute-start.7 = (f32[3,128,128]{2,1,0:T(8,128)S(1)}, f32[3,128,128]{2,1,0:T(8,128)S(1)}, u32[]{:S(2)}, u32[]{:S(2)}) collective-permute-start(f32[3,128,128]{2,1,0:T(8,128)S(1)} %pad_maximum_fusion.2), channel_id=1, source_target_pairs={{0,30},{1,29},{2,0},{3,31},{4,2},{5,1},{6,4},{7,3},{8,6},{9,5},{10... | collective-permute-start | bytes 589832 | tf_op jit(solution)/shard_map/ppermute | solution.py:30
  39.1 0.0 collective-permute-start.8
  39.1 2.6 %collective-permute-start.9 = (f32[7,128,128]{2,1,0:T(8,128)S(1)}, f32[7,128,128]{2,1,0:T(8,128)S(1)}, u32[]{:S(2)}, u32[]{:S(2)}) collective-permute-start(f32[7,128,128]{2,1,0:T(8,128)S(1)} %get-tuple-element.27), channel_id=1, source_target_pairs={{0,30},{1,31},{2,0},{3,1},{4,2},{5,3},{6,4},{7,5},{8,6},{9,7},{10,... | collective-permute-start | bytes 1376264 | tf_op jit(solution)/shard_map/ppermute | solution.py:30
  41.7 0.0 collective-permute-done.6.fu
  41.7 1.3 %collective-permute-start.11 = (f32[1,6,128,128]{3,2,1,0:T(8,128)S(1)}, f32[1,6,128,128]{3,2,1,0:T(8,128)S(1)}, u32[]{:S(2)}, u32[]{:S(2)}) collective-permute-start(f32[1,6,128,128]{3,2,1,0:T(8,128)S(1)} %get-tuple-element.25.p1), channel_id=1, source_target_pairs={{0,1},{1,0},{2,3},{3,2},{4,5},{5,4},{6,7},{7,6},{8,9},{9,8},{10,11... | collective-permute-start | bytes 1179656 | tf_op jit(solution)/shard_map/ppermute | solution.py:30
  43.0 0.0 collective-permute-done.7.fd
  43.0 1.7 %shard_map.60 = (bf16[1024,512]{1,0:T(8,128)(2,1)S(1)}, bf16[512,512]{1,0:T(8,128)(2,1)S(1)}, bf16[512,512]{1,0:T(8,128)(2,1)S(1)}, bf16[768,512]{1,0:T(8,128)(2...) custom-call(s32[15]{0:T(128)S(1)} %pad_add_fusion.meta, ...), custom_call_target="tpu_custom_call" | custom-call | flops 2000000000 | bytes 4194304 | tf_op jit(solution)/shard_map/pallas_call | solution.py:357
  44.7 0.0 collective-permute-done.10.x0
  44.8 7.1 %collective-permute-done.11.x1 = f32[1,6,128,128]{3,2,1,0:T(8,128)S(1)} collective-permute-done((f32[1,6,128,128]{3,2,1,0:T(8,128)S(1)}, f32[1,6,128,128]{3,2,1,0:T(8,128)S(1)}, u32[]{:S(2)}, u32[]{:S(2)}) %collective-permute-start.11) | collective-permute-done | bytes 393248 | tf_op jit(solution)/shard_map/ppermute | solution.py:30
  52.0 2.3 %collective-permute-start.14 = (f32[3,128,128]{2,1,0:T(8,128)S(1)}, f32[3,128,128]{2,1,0:T(8,128)S(1)}, u32[]{:S(2)}, u32[]{:S(2)}) collective-permute-start(f32[3,128,128]{2,1,0:T(8,128)S(1)} %pad_maximum_fusion.4), channel_id=1, source_target_pairs={{0,4},{1,3},{2,6},{3,5},{4,8},{5,7},{6,10},{7,9},{8,12},{9,11},{10... | collective-permute-start | bytes 589832 | tf_op jit(solution)/shard_map/ppermute | solution.py:30
  54.3 4.1 %collective-permute-start.12 = (f32[1,6,128,128]{3,2,1,0:T(8,128)S(1)}, f32[1,6,128,128]{3,2,1,0:T(8,128)S(1)}, u32[]{:S(2)}, u32[]{:S(2)}) collective-permute-start(f32[1,6,128,128]{3,2,1,0:T(8,128)S(1)} %collective-permute-done.10.x0), channel_id=1, source_target_pairs={{0,2},{1,31},{2,4},{3,1},{4,6},{5,3},{6,8},{7,5},{8,10},{9,7},{10,... | collective-permute-start | bytes 1179656 | tf_op jit(solution)/shard_map/ppermute | solution.py:30
  58.4 0.0 collective-permute-start.13
  58.4 0.0 collective-permute-done.8.pu
  58.4 0.7 collective-permute-start.15
  59.2 0.0 collective-permute-done.9.pd
  59.2 4.4 %shard_map.62.early = f32[16,256,256]{2,1,0:T(8,128)S(1)} custom-call(s32[15]{0:T(128)S(1)} %pad_add_fusion.meta, bf16[1024,512]{1,0:T(8,128)(2,1)S(1)} %get-tuple-element.20.t_own, bf16[512,512]{1,0:T(8,128)(2,1)S(1)} %get-tuple-element.21.t_up, bf16[512,512]{1,0:T(8,128)(2,1)S(1)} %get-tuple-element.22.t_down, ...), custom_call_target="tpu_custom_call" | custom-call | flops 4000000000 | bytes 4194304 | tf_op jit(solution)/shard_map/pallas_call | solution.py:357
  63.6 0.0 collective-permute-done.14.fu
  63.6 10.6 %collective-permute-done.15.fd = f32[3,128,128]{2,1,0:T(8,128)S(1)} collective-permute-done((f32[3,128,128]{2,1,0:T(8,128)S(1)}, f32[3,128,128]{2,1,0:T(8,128)S(1)}, u32[]{:S(2)}, u32[]{:S(2)}) %collective-permute-start.15) | collective-permute-done | bytes 196640 | tf_op jit(solution)/shard_map/ppermute | solution.py:30
  74.2 0.0 collective-permute-done.12.n0
  74.2 0.0 collective-permute-done.13.n1
  74.2 5.3 %shard_map.63 = (f32[2,6,128,128]{3,2,1,0:T(8,128)}, f32[2,6,128,128]{3,2,1,0:T(8,128)}) custom-call(s32[15]{0:T(128)S(1)} %pad_add_fusion.meta, f32[2,6,128,128]{3,2,1,0:T(8,128)S(1)} %copy-done.1, bf16[2,128,2048]{2,1,0:T(8,128)(2,1)S(1)} %get-tuple-element.17.z_own, bf16[768,512]{1,0:T(8,128)(2,1)S(1)} %get-tuple-element.18.t_near, ...), custom_call_target="tpu_custom_call" | custom-call | flops 4000000000 | bytes 4194304 | tf_op jit(solution)/shard_map/pallas_call | solution.py:357
  (17 shorter events, 0.2 us)
Async XLA Ops:
  0.6 31.1 %copy-start.1 = (f32[2,6,128,128]{3,2,1,0:T(8,128)S(1)}, f32[2,6,128,128]{3,2,1,0:T(8,128)}, u32[]{:S(2)}) copy-start(f32[2,6,128,128]{3,2,1,0:T(8,128)} %z.7) | copy-start | bytes 2359300
  0.6 31.1 %copy-start.2 = (f32[2,6,128,128]{3,2,1,0:T(8,128)S(1)}, f32[2,6,128,128]{3,2,1,0:T(8,128)}, u32[]{:S(2)}) copy-start(f32[2,6,128,128]{3,2,1,0:T(8,128)} %s.1) | copy-start | bytes 2359300
  2.8 11.1 %collective-permute-start = (f32[1,6,128,128]{3,2,1,0:T(8,128)}, f32[1,6,128,128]{3,2,1,0:T(8,128)S(1)}, u32[]{:S(2)}, u32[]{:S(2)}) collective-permute-start(f32[1,6,128,128]{3,2,1,0:T(8,128)} %get-tuple-element.29), channel_id=1, source_target_pairs={{0,1},{1,0},{2,3},{3,2},{4,5},{5,4},{6,7},{7,6},{8,9},{9,8},{10,11... | collective-permute-start | bytes 1179656 | tf_op jit(solution)/shard_map/ppermute | solution.py:30
  4.8 17.5 %collective-permute-start.1 = (f32[1,6,128,128]{3,2,1,0:T(8,128)}, f32[1,6,128,128]{3,2,1,0:T(8,128)S(1)}, u32[]{:S(2)}, u32[]{:S(2)}) collective-permute-start(f32[1,6,128,128]{3,2,1,0:T(8,128)} %get-tuple-element.28), channel_id=1, source_target_pairs={{0,1},{1,0},{2,3},{3,2},{4,5},{5,4},{6,7},{7,6},{8,9},{9,8},{10,11... | collective-permute-start | bytes 1179656 | tf_op jit(solution)/shard_map/ppermute | solution.py:30
  4.9 1.1 %copy-start = (f32[2,6,128,128]{3,2,1,0:T(8,128)S(1)}, f32[2,6,128,128]{3,2,1,0:T(8,128)}, u32[]{:S(2)}) copy-start(f32[2,6,128,128]{3,2,1,0:T(8,128)} %z.7) | copy-start | bytes 2359300
  7.0 19.3 %collective-permute-start.4 = (f32[7,128,128]{2,1,0:T(8,128)}, f32[7,128,128]{2,1,0:T(8,128)S(1)}, u32[]{:S(2)}, u32[]{:S(2)}) collective-permute-start(f32[7,128,128]{2,1,0:T(8,128)} %get-tuple-element.15), channel_id=1, source_target_pairs={{0,2},{1,3},{2,4},{3,5},{4,6},{5,7},{6,8},{7,9},{8,10},{9,11},{10,... | collective-permute-start | bytes 1376264 | tf_op jit(solution)/shard_map/ppermute | solution.py:30
  9.6 17.2 %collective-permute-start.5 = (f32[7,128,128]{2,1,0:T(8,128)}, f32[7,128,128]{2,1,0:T(8,128)S(1)}, u32[]{:S(2)}, u32[]{:S(2)}) collective-permute-start(f32[7,128,128]{2,1,0:T(8,128)} %get-tuple-element.16), channel_id=1, source_target_pairs={{0,30},{1,31},{2,0},{3,1},{4,2},{5,3},{6,4},{7,5},{8,6},{9,7},{10,... | collective-permute-start | bytes 1376264 | tf_op jit(solution)/shard_map/ppermute | solution.py:30
  13.9 12.9 %collective-permute-start.2 = (f32[1,6,128,128]{3,2,1,0:T(8,128)S(1)}, f32[1,6,128,128]{3,2,1,0:T(8,128)S(1)}, u32[]{:S(2)}, u32[]{:S(2)}) collective-permute-start(f32[1,6,128,128]{3,2,1,0:T(8,128)S(1)} %collective-permute-done.x0), channel_id=1, source_target_pairs={{0,2},{1,31},{2,4},{3,1},{4,6},{5,3},{6,8},{7,5},{8,10},{9,7},{10,... | collective-permute-start | bytes 1179656 | tf_op jit(solution)/shard_map/ppermute | solution.py:30
  22.3 9.5 %collective-permute-start.3 = (f32[1,6,128,128]{3,2,1,0:T(8,128)S(1)}, f32[1,6,128,128]{3,2,1,0:T(8,128)S(1)}, u32[]{:S(2)}, u32[]{:S(2)}) collective-permute-start(f32[1,6,128,128]{3,2,1,0:T(8,128)S(1)} %collective-permute-done.1.x1), channel_id=1, source_target_pairs={{0,2},{1,31},{2,4},{3,1},{4,6},{5,3},{6,8},{7,5},{8,10},{9,7},{10,... | collective-permute-start | bytes 1179656 | tf_op jit(solution)/shard_map/ppermute | solution.py:30
  25.0 16.7 %collective-permute-start.6 = (f32[3,128,128]{2,1,0:T(8,128)S(1)}, f32[3,128,128]{2,1,0:T(8,128)S(1)}, u32[]{:S(2)}, u32[]{:S(2)}) collective-permute-start(f32[3,128,128]{2,1,0:T(8,128)S(1)} %pad_maximum_fusion.1), channel_id=1, source_target_pairs={{0,4},{1,3},{2,6},{3,5},{4,8},{5,7},{6,10},{7,9},{8,12},{9,11},{10... | collective-permute-start | bytes 589832 | tf_op jit(solution)/shard_map/ppermute | solution.py:30
  35.1 9.5 %collective-permute-start.10 = (f32[1,6,128,128]{3,2,1,0:T(8,128)S(1)}, f32[1,6,128,128]{3,2,1,0:T(8,128)S(1)}, u32[]{:S(2)}, u32[]{:S(2)}) collective-permute-start(f32[1,6,128,128]{3,2,1,0:T(8,128)S(1)} %get-tuple-element.24.p0), channel_id=1, source_target_pairs={{0,1},{1,0},{2,3},{3,2},{4,5},{5,4},{6,7},{7,6},{8,9},{9,8},{10,11... | collective-permute-start | bytes 1179656 | tf_op jit(solution)/shard_map/ppermute | solution.py:30
  35.7 7.3 %collective-permute-start.7 = (f32[3,128,128]{2,1,0:T(8,128)S(1)}, f32[3,128,128]{2,1,0:T(8,128)S(1)}, u32[]{:S(2)}, u32[]{:S(2)}) collective-permute-start(f32[3,128,128]{2,1,0:T(8,128)S(1)} %pad_maximum_fusion.2), channel_id=1, source_target_pairs={{0,30},{1,29},{2,0},{3,31},{4,2},{5,1},{6,4},{7,3},{8,6},{9,5},{10... | collective-permute-start | bytes 589832 | tf_op jit(solution)/shard_map/ppermute | solution.py:30
  39.1 19.3 %collective-permute-start.8 = (f32[7,128,128]{2,1,0:T(8,128)S(1)}, f32[7,128,128]{2,1,0:T(8,128)S(1)}, u32[]{:S(2)}, u32[]{:S(2)}) collective-permute-start(f32[7,128,128]{2,1,0:T(8,128)S(1)} %get-tuple-element.26), channel_id=1, source_target_pairs={{0,2},{1,3},{2,4},{3,5},{4,6},{5,7},{6,8},{7,9},{8,10},{9,11},{10,... | collective-permute-start | bytes 1376264 | tf_op jit(solution)/shard_map/ppermute | solution.py:30
  39.1 20.1 %collective-permute-start.9 = (f32[7,128,128]{2,1,0:T(8,128)S(1)}, f32[7,128,128]{2,1,0:T(8,128)S(1)}, u32[]{:S(2)}, u32[]{:S(2)}) collective-permute-start(f32[7,128,128]{2,1,0:T(8,128)S(1)} %get-tuple-element.27), channel_id=1, source_target_pairs={{0,30},{1,31},{2,0},{3,1},{4,2},{5,3},{6,4},{7,5},{8,6},{9,7},{10,... | collective-permute-start | bytes 1376264 | tf_op jit(solution)/shard_map/ppermute | solution.py:30
  41.7 10.2 %collective-permute-start.11 = (f32[1,6,128,128]{3,2,1,0:T(8,128)S(1)}, f32[1,6,128,128]{3,2,1,0:T(8,128)S(1)}, u32[]{:S(2)}, u32[]{:S(2)}) collective-permute-start(f32[1,6,128,128]{3,2,1,0:T(8,128)S(1)} %get-tuple-element.25.p1), channel_id=1, source_target_pairs={{0,1},{1,0},{2,3},{3,2},{4,5},{5,4},{6,7},{7,6},{8,9},{9,8},{10,11... | collective-permute-start | bytes 1179656 | tf_op jit(solution)/shard_map/ppermute | solution.py:30
  52.0 11.6 %collective-permute-start.14 = (f32[3,128,128]{2,1,0:T(8,128)S(1)}, f32[3,128,128]{2,1,0:T(8,128)S(1)}, u32[]{:S(2)}, u32[]{:S(2)}) collective-permute-start(f32[3,128,128]{2,1,0:T(8,128)S(1)} %pad_maximum_fusion.4), channel_id=1, source_target_pairs={{0,4},{1,3},{2,6},{3,5},{4,8},{5,7},{6,10},{7,9},{8,12},{9,11},{10... | collective-permute-start | bytes 589832 | tf_op jit(solution)/shard_map/ppermute | solution.py:30
  54.3 19.9 %collective-permute-start.12 = (f32[1,6,128,128]{3,2,1,0:T(8,128)S(1)}, f32[1,6,128,128]{3,2,1,0:T(8,128)S(1)}, u32[]{:S(2)}, u32[]{:S(2)}) collective-permute-start(f32[1,6,128,128]{3,2,1,0:T(8,128)S(1)} %collective-permute-done.10.x0), channel_id=1, source_target_pairs={{0,2},{1,31},{2,4},{3,1},{4,6},{5,3},{6,8},{7,5},{8,10},{9,7},{10,... | collective-permute-start | bytes 1179656 | tf_op jit(solution)/shard_map/ppermute | solution.py:30
  58.4 15.8 %collective-permute-start.13 = (f32[1,6,128,128]{3,2,1,0:T(8,128)S(1)}, f32[1,6,128,128]{3,2,1,0:T(8,128)S(1)}, u32[]{:S(2)}, u32[]{:S(2)}) collective-permute-start(f32[1,6,128,128]{3,2,1,0:T(8,128)S(1)} %collective-permute-done.11.x1), channel_id=1, source_target_pairs={{0,2},{1,31},{2,4},{3,1},{4,6},{5,3},{6,8},{7,5},{8,10},{9,7},{10,... | collective-permute-start | bytes 1179656 | tf_op jit(solution)/shard_map/ppermute | solution.py:30
  58.4 15.8 %collective-permute-start.15 = (f32[3,128,128]{2,1,0:T(8,128)S(1)}, f32[3,128,128]{2,1,0:T(8,128)S(1)}, u32[]{:S(2)}, u32[]{:S(2)}) collective-permute-start(f32[3,128,128]{2,1,0:T(8,128)S(1)} %pad_maximum_fusion.5), channel_id=1, source_target_pairs={{0,30},{1,29},{2,0},{3,31},{4,2},{5,1},{6,4},{7,3},{8,6},{9,5},{10... | collective-permute-start | bytes 589832 | tf_op jit(solution)/shard_map/ppermute | solution.py:30

commit v3 on v2

--- a/solution.py
+++ b/solution.py
@@ -21,6 +21,8 @@
 
 UP = ((0, 3), (0, 4), (0, 5), (1, 0), (1, 3), (1, 4), (1, 5))
 DOWN = ((0, 0), (0, 1), (0, 2), (0, 3), (1, 1), (1, 2), (1, 3))
+Z_UP = ((0, 0), (0, 3), (0, 4), (0, 5), (1, 0), (1, 2), (1, 3), (1, 4), (1, 5))
+Z_DOWN = ((0, 0), (0, 1), (0, 2), (0, 3), (0, 4), (1, 0), (1, 1), (1, 2), (1, 3))
 FAR_UP = ((0, 5), (1, 4), (1, 5))
 FAR_DOWN = ((0, 1), (0, 2), (1, 1))
 
@@ -106,10 +108,13 @@
         index = base + slots.index(rest[0]) + jnp.clip(slot - rest[0], 0, len(rest) - 1)
         return jnp.where(there, ref[index], 0.0)
 
-    def side(self, refs, side, r, col):
+    def side(self, ref, side, r, col):
         row = self.side_row(side) + r
         slot, there = slot_of(col - row, self.dropped(row))
-        return jnp.where(there, refs[r][0, slot], 0.0)
+        return jnp.where(there, ref[0, slot], 0.0)
+
+    def by_distance(self, refs):
+        return tuple(zip(refs, (self.parity, 1 - self.parity)))
 
     def dense_slot(self, row, slot):
         if slot == 0:
@@ -150,12 +155,20 @@
 
 
 def pack_kernel(z, zu, zd):
-    for out, layout in ((zu, UP), (zd, DOWN)):
+    for out, layout in ((zu, Z_UP), (zd, Z_DOWN)):
         for j, (i, slot) in enumerate(layout):
             out[j] = z[i, slot]
 
 
-def product_kernel(meta, s, z, x0, x1, n0, n1, zu, zd, p0, p1, pu, pd, z_high, z_low, s_high, s_low, dense):
+def far_kernel(meta, nearer, farther, fu, fd):
+    even = meta[WIDE] == 0
+    for out, layout in ((fu, FAR_UP), (fd, FAR_DOWN)):
+        for j, (r, slot) in enumerate(layout):
+            a, b = (nearer, farther) if r == 0 else (farther, nearer)
+            out[j] = jnp.where(even, a[0, slot], b[0, slot])
+
+
+def product_kernel(meta, s, z, x0, x1, n0, n1, zu, zd, p0, p1, pf, pu, pd, z_high, z_low, s_high, s_low, dense):
     tile = s.shape[-1]
     rows = Rows(meta)
     for c in range(COLS):
@@ -167,18 +180,76 @@
         for side, refs in enumerate(((x0, x1), (n0, n1))):
             for r in range(2):
                 where = rows.side_row(side) + r - COL0
-                put(z_high, z_low, where, c, tile, rows.side(refs, side, r, col))
+                put(z_high, z_low, where, c, tile, rows.side(refs[r], side, r, col))
         row = -REACH
-        put(z_high, z_low, 0, c, tile, rows.packed(zu, UP, -4, 1, col) if abs(col - row) <= REACH else zero(tile))
+        put(z_high, z_low, 0, c, tile, rows.packed(zu, Z_UP, -4, 1, col) if abs(col - row) <= REACH else zero(tile))
         row = OWN - 1 + REACH
-        put(z_high, z_low, COLS - 1, c, tile, rows.packed(zd, DOWN, 4, 0, col) if abs(col - row) <= REACH else zero(tile))
+        put(z_high, z_low, COLS - 1, c, tile, rows.packed(zd, Z_DOWN, 4, 0, col) if abs(col - row) <= REACH else zero(tile))
     row_matmul(s_high, s_low, z_high, z_low, dense, tile)
     for i, ref in enumerate((p0, p1)):
         for slot in range(2 * REACH):
             ref[0, slot] = dense[i, rows.dense_slot(i, slot)]
+    for slot in range(2 * REACH):
+        pf[0, slot] = dense[rows.parity, rows.dense_slot(rows.parity, slot)]
     for ref, layout in ((pu, UP), (pd, DOWN)):
         for j, (i, slot) in enumerate(layout):
             ref[j] = dense[i, rows.dense_slot(i, slot)]
+
+
+def side_kernel(meta, s, z, x0, x1, n0, n1, zu, zd, out, z_high, z_low, s_high, s_low, dense):
+    tile = s.shape[-1]
+    rows = Rows(meta)
+    width = 2 * REACH + 1
+
+    def own():
+        return lambda row, col: rows.own(z, row, col)
+
+    def swapped(r):
+        return lambda row, col: rows.side((x0, x1)[r], 0, r, col)
+
+    def relayed(r):
+        return lambda row, col: rows.side((n0, n1)[r], 1, r, col)
+
+    def from_down(r):
+        return lambda row, col: rows.packed(zu, Z_UP, -4, r, col)
+
+    def from_up(r):
+        return lambda row, col: rows.packed(zd, Z_DOWN, 4, r, col)
+
+    even = (relayed(1), own(), own(), swapped(0), swapped(1), from_up(0), from_up(1))
+    odd = (from_down(0), from_down(1), swapped(0), swapped(1), own(), own(), relayed(0))
+    for parity, sources in ((0, even), (1, odd)):
+
+        @pl.when(rows.parity == parity)
+        def _():
+            centre = OWN if parity == 0 else -1
+            first = centre - REACH
+            for k in range(width):
+                for c in range(width):
+                    there = abs(k - c) <= REACH
+                    put(z_high, z_low, k, c, tile, sources[k](first + k, first + c) if there else zero(tile))
+
+    centre = jnp.where(rows.parity == 0, OWN, -1)
+    dropped = rows.dropped(centre)
+    for c in range(width):
+        slot, there = slot_of(jnp.int32(c - REACH), dropped)
+        put(s_high, s_low, 0, c, tile, jnp.where(there, s[0, slot], 0.0))
+    for c in range(0, width, 2):
+        last = min(c + 2, width)
+        lo, hi = max(c - REACH, 0), min(last - 1 + REACH, width - 1) + 1
+        n = slice(c * tile, last * tile)
+        k = slice(lo * tile, hi * tile)
+        block = dot3(
+            flat(s_high, slice(None), k),
+            flat(s_low, slice(None), k),
+            flat(z_high, slice(lo, hi), n),
+            flat(z_low, slice(lo, hi), n),
+        )
+        for j in range(last - c):
+            dense[c + j] = block[:, j * tile : (j + 1) * tile]
+    for slot in range(2 * REACH):
+        pos = slot - 1 + jnp.where(slot - 1 >= dropped, 1, 0)
+        out[0, slot] = dense[REACH if slot == 0 else pos + jnp.where(pos >= REACH, 1, 0)]
 
 
 def turn_kernel(meta, z, x0, x1, n0, n1, zu, zd, fu, fd, t_own, t_up, t_down, t_swap, t_near, t_far, z_own):
@@ -200,9 +271,9 @@
             z_own[r, :, (COLS + c) * tile : (COLS + c + 1) * tile] = low
         for c in range(4):
             col = c + COL0
-            store(t_up, c, r, rows.packed(zu, UP, -4, r, col) if abs(col - (r - 4)) <= REACH else zero(tile))
+            store(t_up, c, r, rows.packed(zu, Z_UP, -4, r, col) if abs(col - (r - 4)) <= REACH else zero(tile))
             col = c + COL0 + 4
-            store(t_down, c, r, rows.packed(zd, DOWN, 4, r, col) if abs(col - (r + 4)) <= REACH else zero(tile))
+            store(t_down, c, r, rows.packed(zd, Z_DOWN, 4, r, col) if abs(col - (r + 4)) <= REACH else zero(tile))
         for c in range(2):
             col = c + COL0
             store(t_far, c, r, rows.packed(fu, FAR_UP, -6, r, col) if abs(col - (r - 6)) <= REACH else zero(tile))
@@ -211,7 +282,7 @@
         for side, (out, refs) in enumerate(((t_swap, (x0, x1)), (t_near, (n0, n1)))):
             first = 2 * rows.side_pair(side) + COL0
             for c in range(2 * SIDE):
-                store(out, c, r, rows.side(refs, side, r, first + c))
+                store(out, c, r, rows.side(refs[r], side, r, first + c))
 
 
 def halves(turned, first, last, tile):
@@ -221,9 +292,9 @@
 
 def side_gram(rows, side, refs, turned, high, low, add, tile):
     first = 2 * rows.side_pair(side) + COL0
-    for r in range(2):
+    for ref, r in rows.by_distance(refs):
         for c in range(2 * SIDE):
-            put(high, low, r, c, tile, rows.side(refs, side, r, first + c))
+            put(high, low, r, c, tile, rows.side(ref, side, r, first + c))
     left = halves(turned, 0, SIDE, tile)
     for b in range(SIDE):
         n = slice(2 * b * tile, (2 * b + 2) * tile)
@@ -232,7 +303,7 @@
             add(a, b, block[2 * a * tile : (2 * a + 2) * tile])
 
 
-def gram_kernel(meta, t_own, t_up, t_down, t_swap, p0, p1, pu, pd, x0, x1, gram, high, low, side_high, side_low):
+def gram_kernel(meta, t_own, t_up, t_down, t_swap, p0, p1, pu, pd, nearer, farther, gram, high, low, side_high, side_low):
     tile = p0.shape[-1]
     rows = Rows(meta)
     for r in range(2):
@@ -264,11 +335,11 @@
         index = PAIRS * a + b + (PAIRS + 1) * rows.side_pair(0)
         gram[index] = gram[index] + value
 
-    side_gram(rows, 0, (x0, x1), t_swap, side_high, side_low, add, tile)
+    side_gram(rows, 0, (nearer, farther), t_swap, side_high, side_low, add, tile)
 
 
 def refine_kernel(
-    meta, z, z_own, t_near, t_far, early, n0, n1, fu, fd, refined, correction,
+    meta, z, z_own, t_near, t_far, early, nearer, farther, fu, fd, refined, correction,
     high, low, far_high, far_low, late, d_high, d_low, dense, z_high, z_low,
 ):
     tile = z.shape[-1]
@@ -277,7 +348,7 @@
     def add(a, b, value):
         late[SIDE * a + b] = value
 
-    side_gram(rows, 1, (n0, n1), t_near, high, low, add, tile)
+    side_gram(rows, 1, (nearer, farther), t_near, high, low, add, tile)
     for r in range(2):
         for c in range(2):
             col = c + COL0
@@ -372,25 +443,37 @@
 
     row = shape(1, slots, tile, tile)
     seven = shape(len(UP), tile, tile)
+    nine = shape(len(Z_UP), tile, tile)
+    three = shape(len(FAR_UP), tile, tile)
+    parity = device % 2
     dense = pltpu.VMEM((OWN, COLS, tile, tile), F32)
 
     x = [send(factor[r : r + 1], swap) for r in range(OWN)]
-    zu, zd = call(pack_kernel, (factor,), (seven, seven), [], 1000, 0)
+    zu, zd = call(pack_kernel, (factor,), (nine, nine), [], 1000, 0)
     zu, zd = send(zu, up), send(zd, down)
     n = [send(x[r], near) for r in range(OWN)]
+    sx = send(lax.dynamic_slice_in_dim(correlation, 1 - parity, 1, 0), swap)
     zfu, zfd = far(x)
     zfu, zfd = send(zfu, far_up), send(zfd, far_down)
-    p0, p1, pu, pd = call(
+    p0, p1, pf, pu, pd = call(
         product_kernel,
         (meta, correlation, factor, *x, *n, zu, zd),
-        (row, row, seven, seven),
+        (row, row, row, seven, seven),
         halves_of(COLS, COLS) + halves_of(OWN, COLS) + [dense],
         int(2e9),
     )
-    px = [send(v, swap) for v in (p0, p1)]
+    px = send(pf, swap)
     pu, pd = send(pu, up), send(pd, down)
-    pn = [send(v, near) for v in px]
-    pfu, pfd = far(px)
+    width = 2 * REACH + 1
+    ps = call(
+        side_kernel,
+        (meta, sx, factor, *x, *n, zu, zd),
+        row,
+        halves_of(width, width) + halves_of(1, width) + [pltpu.VMEM((width, tile, tile), F32)],
+        int(2e9),
+    )
+    pn = (send(ps, near), send(px, near))
+    pfu, pfd = call(far_kernel, (meta, ps, px), (three, three), [], 1000)
     pfu, pfd = send(pfu, far_up), send(pfd, far_down)
 
     def turned(columns):
@@ -406,7 +489,7 @@
     )
     early = call(
         gram_kernel,
-        (meta, t_own, t_up, t_down, t_swap, p0, p1, pu, pd, *px),
+        (meta, t_own, t_up, t_down, t_swap, p0, p1, pu, pd, ps, px),
         shape(PAIRS * PAIRS, 2 * tile, 2 * tile),
         halves_of(4, COLS) + halves_of(2, 2 * SIDE),
         int(4e9),

time: 79.8 us -> 84.1 us (1.054)
  local copies, waits for them, and re-layouts: 4.73 us -> 7.85 us
  Pallas kernels: 15.8 us -> 18.9 us
  starting transfers between devices: 27.3 us -> 24.5 us
    pallas_call x5 -> x7, Pallas kernels: 15.8 us -> 18.9 us  [call(): pl.pallas_call(kernel, in_specs=[smem] * scalars + [vmem] * (len(ins) - s...]
    ppermute x16, starting transfers between devices: 27.3 us -> 24.5 us  [send(): return lax.ppermute(value, AXES, [(i, to(i) % count) for i in range(count)])]
    dynamic_slice x0 -> x1, local copies, waits for them, and re-layouts: none -> 1.79 us  [body(): sx = send(lax.dynamic_slice_in_dim(correlation, 1 - parity, 1, 0), swap)]
  transfers between devices with their start and end apart: 16 -> 16, of which waited for: 6 -> 6; matrix products, arithmetic and copies ran while one was open for 3% -> 7% of each run, Pallas kernels for 13% -> 16%
where the time goes in v3:
time: 84.1 us; the launch traced here: 83.3 us
  waiting for transfers between devices  30.2 us (36%)
  starting transfers between devices  24.5 us (29%)
  Pallas kernels  18.9 us (22%)
  local copies, waits for them, and re-layouts  7.85 us (9%)
  other arithmetic  1.01 us (1%)
    ppermute x16, waiting for transfers between devices, send(): return lax.ppermute(value, AXES, [(i, to(i) % count) for i in range(count)])  30.2 us
    ppermute x16, starting transfers between devices, send(): return lax.ppermute(value, AXES, [(i, to(i) % count) for i in range(count)])  24.5 us
    pallas_call x7, Pallas kernels, call(): pl.pallas_call(kernel, in_specs=[smem] * scalars + [vmem] * (len(ins) - s...  18.9 us
    unnamed x7, local copies, waits for them, and re-layouts  2.52 us
    slice x1, local copies, waits for them, and re-layouts, body(): x = [send(factor[r:r + 1], swap) for r in range(OWN)]  2.17 us
    dynamic_slice x1, local copies, waits for them, and re-layouts, body(): sx = send(lax.dynamic_slice_in_dim(correlation, 1 - parity, 1, 0), swap)  1.79 us
  transfers between devices with their start and end apart: 16, of which 6 were waited for; matrix products, arithmetic and copies ran while one was open for 7% of the time, Pallas kernels for 16%

profile of v3, /device:TPU:1, one launch (start us, length us, event | category | flops | bytes accessed | tf_op | source)
XLA Modules:
  0.0 83.3 jit_solution(13506436393766258191)
XLA Ops:
  0.6 0.0 copy-start.1
  0.6 0.0 copy-start.2
  0.7 2.2 %fusion.7 = (f32[1,6,128,128]{3,2,1,0:T(8,128)}, f32[1,6,128,128]{3,2,1,0:T(8,128)}) fusion(f32[2,6,128,128]{3,2,1,0:T(8,128)} %z.9), kind=kLoop, calls=%fused_computation.32 | loop fusion | bytes 1572864 | tf_op jit(solution)/shard_map/slice | solution.py:451
  2.8 2.0 %collective-permute-start = (f32[1,6,128,128]{3,2,1,0:T(8,128)}, f32[1,6,128,128]{3,2,1,0:T(8,128)S(1)}, u32[]{:S(2)}, u32[]{:S(2)}) collective-permute-start(f32[1,6,128,128]{3,2,1,0:T(8,128)} %get-tuple-element.35), channel_id=1, source_target_pairs={{0,1},{1,0},{2,3},{3,2},{4,5},{5,4},{6,7},{7,6},{8,9},{9,8},{10,11... | collective-permute-start | bytes 1179656 | tf_op jit(solution)/shard_map/ppermute | solution.py:32
  4.9 0.0 collective-permute-start.1
  4.9 1.1 %copy-done = f32[2,6,128,128]{3,2,1,0:T(8,128)S(1)} copy-done((f32[2,6,128,128]{3,2,1,0:T(8,128)S(1)}, f32[2,6,128,128]{3,2,1,0:T(8,128)}, u32[]{:S(2)}) %copy-start) | copy-done | bytes 786456
  6.0 1.1 %shard_map.59 = (f32[9,128,128]{2,1,0:T(8,128)}, f32[9,128,128]{2,1,0:T(8,128)}) custom-call(f32[2,6,128,128]{3,2,1,0:T(8,128)S(1)} %copy-done), custom_call_target="tpu_custom_call" | custom-call | flops 1000 | bytes 4194304 | tf_op jit(solution)/shard_map/pallas_call | solution.py:428
  7.1 2.6 %collective-permute-start.4 = (f32[9,128,128]{2,1,0:T(8,128)}, f32[9,128,128]{2,1,0:T(8,128)S(1)}, u32[]{:S(2)}, u32[]{:S(2)}) collective-permute-start(f32[9,128,128]{2,1,0:T(8,128)} %get-tuple-element.18), channel_id=1, source_target_pairs={{0,2},{1,3},{2,4},{3,5},{4,6},{5,7},{6,8},{7,9},{8,10},{9,11},{10,... | collective-permute-start | bytes 1769480 | tf_op jit(solution)/shard_map/ppermute | solution.py:32
  9.7 0.0 collective-permute-start.5
  9.7 1.8 %constant_dynamic-slice_fusion = f32[1,6,128,128]{3,2,1,0:T(8,128)} fusion(f32[2,6,128,128]{3,2,1,0:T(8,128)} %s.1, s32[]{:T(128)S(6)} %select_n.51), kind=kLoop, calls=%fused_computation.31 | loop fusion | bytes 786436 | tf_op jit(solution)/shard_map/dynamic_slice | solution.py:455
  11.5 1.2 %collective-permute-start.10 = (f32[1,6,128,128]{3,2,1,0:T(8,128)}, f32[1,6,128,128]{3,2,1,0:T(8,128)}, u32[]{:S(2)}, u32[]{:S(2)}) collective-permute-start(f32[1,6,128,128]{3,2,1,0:T(8,128)} %constant_dynamic-slice_fusion), channel_id=1, source_target_pairs={{0,1},{1,0},{2,3},{3,2},{4,5},{5,4},{6,7},{7,6},{8,9},{9,8},{10,11... | collective-permute-start | bytes 1179656 | tf_op jit(solution)/shard_map/ppermute | solution.py:32
  12.7 1.4 %copy.6 = s32[64,6]{1,0:T(8,128)} copy(s32[64,6]{0,1:T(8,128)} %param.6) | data formatting | bytes 3072 | tf_op args[2]
  14.1 1.3 %gather_fusion = s32[14,6]{1,0:T(8,128)S(1)} fusion(s32[64,6]{1,0:T(8,128)} %copy.6, s32[1024]{0:T(1024)S(1)} %pad_clamp_fusion), kind=kCustom, calls=%fused_computation | custom fusion | bytes 728 | tf_op jit(solution)/shard_map/gather | solution.py:419
  15.4 0.8 %convert_reduce_fusion = s32[14]{0:T(128)S(1)} fusion(s32[14,6]{1,0:T(8,128)S(1)} %gather_fusion, s32[5]{0:T(128)} %constant.59.clone, s32[14]{0:T(128)S(1)} %and_select_fusion), kind=kLoop, calls=%fused_computation.18 | loop fusion | flops 1176 | bytes 412 | tf_op jit(solution)/shard_map/reduce_sum | solution.py:421
  16.3 0.1 pad_add_fusion.meta
  16.4 0.0 collective-permute-done.x0
  16.4 2.0 %collective-permute-start.2 = (f32[1,6,128,128]{3,2,1,0:T(8,128)S(1)}, f32[1,6,128,128]{3,2,1,0:T(8,128)S(1)}, u32[]{:S(2)}, u32[]{:S(2)}) collective-permute-start(f32[1,6,128,128]{3,2,1,0:T(8,128)S(1)} %collective-permute-done.x0), channel_id=1, source_target_pairs={{0,2},{1,31},{2,4},{3,1},{4,6},{5,3},{6,8},{7,5},{8,10},{9,7},{10,... | collective-permute-start | bytes 1179656 | tf_op jit(solution)/shard_map/ppermute | solution.py:32
  18.4 3.9 %collective-permute-done.1.x1 = f32[1,6,128,128]{3,2,1,0:T(8,128)S(1)} collective-permute-done((f32[1,6,128,128]{3,2,1,0:T(8,128)}, f32[1,6,128,128]{3,2,1,0:T(8,128)S(1)}, u32[]{:S(2)}, u32[]{:S(2)}) %collective-permute-start.1) | collective-permute-done | bytes 393248 | tf_op jit(solution)/shard_map/ppermute | solution.py:32
  22.3 3.8 %collective-permute-start.3 = (f32[1,6,128,128]{3,2,1,0:T(8,128)S(1)}, f32[1,6,128,128]{3,2,1,0:T(8,128)S(1)}, u32[]{:S(2)}, u32[]{:S(2)}) collective-permute-start(f32[1,6,128,128]{3,2,1,0:T(8,128)S(1)} %collective-permute-done.1.x1), channel_id=1, source_target_pairs={{0,2},{1,31},{2,4},{3,1},{4,6},{5,3},{6,8},{7,5},{8,10},{9,7},{10,... | collective-permute-start | bytes 1179656 | tf_op jit(solution)/shard_map/ppermute | solution.py:32
  26.2 0.0 collective-permute-done.4.zu
  26.2 7.8 %collective-permute-done.5.zd = f32[9,128,128]{2,1,0:T(8,128)S(1)} collective-permute-done((f32[9,128,128]{2,1,0:T(8,128)}, f32[9,128,128]{2,1,0:T(8,128)S(1)}, u32[]{:S(2)}, u32[]{:S(2)}) %collective-permute-start.5) | collective-permute-done | bytes 589856 | tf_op jit(solution)/shard_map/ppermute | solution.py:32
  33.9 0.0 collective-permute-done.2.n0
  33.9 0.0 collective-permute-done.3.n1
  34.0 3.4 %shard_map.61 = (f32[1,6,128,128]{3,2,1,0:T(8,128)S(1)}, f32[1,6,128,128]{3,2,1,0:T(8,128)S(1)}, f32[1,6,128,128]{3,2,1,0:T(8,128)S(1)}, f32[7,128,128]{2,1,0:T(8,128)S(1)}, f32[7,128,128]{2,1,0:T(8,128)S(1)}) custom-call(s32[15]{0:T(128)S(1)} %pad_add_fusion.meta, f32[2,6,128,128]{3,2,1,0:T(8,128)S(1)} %copy-done.2, f32[2,6,128,128]{3,2,1,0:T(8,128)S(1)} %copy-done.1, ...), custom_call_target="tpu_custom_call" | custom-call | flops 2000000000 | bytes 4194304 | tf_op jit(solution)/shard_map/pallas_call | solution.py:428
  37.4 1.3 %collective-permute-start.11 = (f32[1,6,128,128]{3,2,1,0:T(8,128)S(1)}, f32[1,6,128,128]{3,2,1,0:T(8,128)S(1)}, u32[]{:S(2)}, u32[]{:S(2)}) collective-permute-start(f32[1,6,128,128]{3,2,1,0:T(8,128)S(1)} %get-tuple-element.31), channel_id=1, source_target_pairs={{0,1},{1,0},{2,3},{3,2},{4,5},{5,4},{6,7},{7,6},{8,9},{9,8},{10,11... | collective-permute-start | bytes 1179656 | tf_op jit(solution)/shard_map/ppermute | solution.py:32
  38.7 0.1 collective-permute-start.6
  38.7 0.7 collective-permute-start.8
  39.4 0.0 collective-permute-start.9
  39.4 0.0 collective-permute-done.10.s
  39.4 4.5 %collective-permute-start.7 = (f32[3,128,128]{2,1,0:T(8,128)S(1)}, f32[3,128,128]{2,1,0:T(8,128)S(1)}, u32[]{:S(2)}, u32[]{:S(2)}) collective-permute-start(f32[3,128,128]{2,1,0:T(8,128)S(1)} %pad_maximum_fusion.2), channel_id=1, source_target_pairs={{0,30},{1,29},{2,0},{3,31},{4,2},{5,1},{6,4},{7,3},{8,6},{9,5},{10... | collective-permute-start | bytes 589832 | tf_op jit(solution)/shard_map/ppermute | solution.py:32
  43.9 2.3 %shard_map.62.nearer = f32[1,6,128,128]{3,2,1,0:T(8,128)S(1)} custom-call(s32[15]{0:T(128)S(1)} %pad_add_fusion.meta, f32[1,6,128,128]{3,2,1,0:T(8,128)} %collective-permute-done.10.s, f32[2,6,128,128]{3,2,1,0:T(8,128)S(1)} %copy-done.1, f32[1,6,128,128]{3,2,1,0:T(8,128)S(1)} %collective-permute-done.x0, f32[1,6,128,128]{3,2,1,0:T(8,128)S(1)} %collective-permute-done.1.x1, ...), custom_call_target="tpu_custom_call" | custom-call | flops 2000000000 | bytes 4194304 | tf_op jit(solution)/shard_map/pallas_call | solution.py:428
  46.2 1.5 %collective-permute-done.6.fu = f32[3,128,128]{2,1,0:T(8,128)S(1)} collective-permute-done((f32[3,128,128]{2,1,0:T(8,128)S(1)}, f32[3,128,128]{2,1,0:T(8,128)S(1)}, u32[]{:S(2)}, u32[]{:S(2)}) %collective-permute-start.6) | collective-permute-done | bytes 196640 | tf_op jit(solution)/shard_map/ppermute | solution.py:32
  47.8 6.0 %collective-permute-start.12 = (f32[1,6,128,128]{3,2,1,0:T(8,128)S(1)}, f32[1,6,128,128]{3,2,1,0:T(8,128)S(1)}, u32[]{:S(2)}, u32[]{:S(2)}) collective-permute-start(f32[1,6,128,128]{3,2,1,0:T(8,128)S(1)} %shard_map.62.nearer), channel_id=1, source_target_pairs={{0,2},{1,31},{2,4},{3,1},{4,6},{5,3},{6,8},{7,5},{8,10},{9,7},{10,... | collective-permute-start | bytes 1179656 | tf_op jit(solution)/shard_map/ppermute | solution.py:32
  53.8 0.0 collective-permute-done.11.farther
  53.8 0.0 collective-permute-start.13
  53.8 13.1 %collective-permute-done.7.fd = f32[3,128,128]{2,1,0:T(8,128)S(1)} collective-permute-done((f32[3,128,128]{2,1,0:T(8,128)S(1)}, f32[3,128,128]{2,1,0:T(8,128)S(1)}, u32[]{:S(2)}, u32[]{:S(2)}) %collective-permute-start.7) | collective-permute-done | bytes 196640 | tf_op jit(solution)/shard_map/ppermute | solution.py:32
  67.0 1.7 %shard_map.60 = (bf16[1024,512]{1,0:T(8,128)(2,1)S(1)}, bf16[512,512]{1,0:T(8,128)(2,1)S(1)}, bf16[512,512]{1,0:T(8,128)(2,1)S(1)}, bf16[768,512]{1,0:T(8,128)(2...) custom-call(s32[15]{0:T(128)S(1)} %pad_add_fusion.meta, ...), custom_call_target="tpu_custom_call" | custom-call | flops 2000000000 | bytes 4194304 | tf_op jit(solution)/shard_map/pallas_call | solution.py:428
  68.7 0.6 shard_map.64
  69.3 0.1 collective-permute-start.14
  69.3 0.0 collective-permute-done.8.pu
  69.3 0.2 collective-permute-start.15
  69.6 0.0 collective-permute-done.9.pd
  69.6 4.4 %shard_map.63.early = f32[16,256,256]{2,1,0:T(8,128)S(1)} custom-call(s32[15]{0:T(128)S(1)} %pad_add_fusion.meta, bf16[1024,512]{1,0:T(8,128)(2,1)S(1)} %get-tuple-element.23.t_own, bf16[512,512]{1,0:T(8,128)(2,1)S(1)} %get-tuple-element.24.t_up, bf16[512,512]{1,0:T(8,128)(2,1)S(1)} %get-tuple-element.25.t_down, ...), custom_call_target="tpu_custom_call" | custom-call | flops 4000000000 | bytes 4194304 | tf_op jit(solution)/shard_map/pallas_call | solution.py:428
  74.0 0.0 collective-permute-done.12.nearer
  74.0 2.6 %collective-permute-done.14.fu = f32[3,128,128]{2,1,0:T(8,128)S(1)} collective-permute-done((f32[3,128,128]{2,1,0:T(8,128)S(1)}, f32[3,128,128]{2,1,0:T(8,128)S(1)}, u32[]{:S(2)}, u32[]{:S(2)}) %collective-permute-start.14) | collective-permute-done | bytes 196640 | tf_op jit(solution)/shard_map/ppermute | solution.py:32
  76.6 1.3 %collective-permute-done.15.fd = f32[3,128,128]{2,1,0:T(8,128)S(1)} collective-permute-done((f32[3,128,128]{2,1,0:T(8,128)S(1)}, f32[3,128,128]{2,1,0:T(8,128)S(1)}, u32[]{:S(2)}, u32[]{:S(2)}) %collective-permute-start.15) | collective-permute-done | bytes 196640 | tf_op jit(solution)/shard_map/ppermute | solution.py:32
  77.9 0.0 collective-permute-done.13.farther
  77.9 5.4 %shard_map.65 = (f32[2,6,128,128]{3,2,1,0:T(8,128)}, f32[2,6,128,128]{3,2,1,0:T(8,128)}) custom-call(s32[15]{0:T(128)S(1)} %pad_add_fusion.meta, f32[2,6,128,128]{3,2,1,0:T(8,128)S(1)} %copy-done.1, bf16[2,128,2048]{2,1,0:T(8,128)(2,1)S(1)} %get-tuple-element.20.z_own, bf16[768,512]{1,0:T(8,128)(2,1)S(1)} %get-tuple-element.21.t_near, ...), custom_call_target="tpu_custom_call" | custom-call | flops 4000000000 | bytes 4194304 | tf_op jit(solution)/shard_map/pallas_call | solution.py:428
  (13 shorter events, 0.1 us)
Async XLA Ops:
  0.6 33.3 %copy-start.1 = (f32[2,6,128,128]{3,2,1,0:T(8,128)S(1)}, f32[2,6,128,128]{3,2,1,0:T(8,128)}, u32[]{:S(2)}) copy-start(f32[2,6,128,128]{3,2,1,0:T(8,128)} %z.9) | copy-start | bytes 2359300
  0.6 33.3 %copy-start.2 = (f32[2,6,128,128]{3,2,1,0:T(8,128)S(1)}, f32[2,6,128,128]{3,2,1,0:T(8,128)}, u32[]{:S(2)}) copy-start(f32[2,6,128,128]{3,2,1,0:T(8,128)} %s.1) | copy-start | bytes 2359300
  2.8 13.5 %collective-permute-start = (f32[1,6,128,128]{3,2,1,0:T(8,128)}, f32[1,6,128,128]{3,2,1,0:T(8,128)S(1)}, u32[]{:S(2)}, u32[]{:S(2)}) collective-permute-start(f32[1,6,128,128]{3,2,1,0:T(8,128)} %get-tuple-element.35), channel_id=1, source_target_pairs={{0,1},{1,0},{2,3},{3,2},{4,5},{5,4},{6,7},{7,6},{8,9},{9,8},{10,11... | collective-permute-start | bytes 1179656 | tf_op jit(solution)/shard_map/ppermute | solution.py:32
  4.9 17.5 %collective-permute-start.1 = (f32[1,6,128,128]{3,2,1,0:T(8,128)}, f32[1,6,128,128]{3,2,1,0:T(8,128)S(1)}, u32[]{:S(2)}, u32[]{:S(2)}) collective-permute-start(f32[1,6,128,128]{3,2,1,0:T(8,128)} %get-tuple-element.34), channel_id=1, source_target_pairs={{0,1},{1,0},{2,3},{3,2},{4,5},{5,4},{6,7},{7,6},{8,9},{9,8},{10,11... | collective-permute-start | bytes 1179656 | tf_op jit(solution)/shard_map/ppermute | solution.py:32
  4.9 1.1 %copy-start = (f32[2,6,128,128]{3,2,1,0:T(8,128)S(1)}, f32[2,6,128,128]{3,2,1,0:T(8,128)}, u32[]{:S(2)}) copy-start(f32[2,6,128,128]{3,2,1,0:T(8,128)} %z.9) | copy-start | bytes 2359300
  7.1 19.1 %collective-permute-start.4 = (f32[9,128,128]{2,1,0:T(8,128)}, f32[9,128,128]{2,1,0:T(8,128)S(1)}, u32[]{:S(2)}, u32[]{:S(2)}) collective-permute-start(f32[9,128,128]{2,1,0:T(8,128)} %get-tuple-element.18), channel_id=1, source_target_pairs={{0,2},{1,3},{2,4},{3,5},{4,6},{5,7},{6,8},{7,9},{8,10},{9,11},{10,... | collective-permute-start | bytes 1769480 | tf_op jit(solution)/shard_map/ppermute | solution.py:32
  9.7 24.3 %collective-permute-start.5 = (f32[9,128,128]{2,1,0:T(8,128)}, f32[9,128,128]{2,1,0:T(8,128)S(1)}, u32[]{:S(2)}, u32[]{:S(2)}) collective-permute-start(f32[9,128,128]{2,1,0:T(8,128)} %get-tuple-element.19), channel_id=1, source_target_pairs={{0,30},{1,31},{2,0},{3,1},{4,2},{5,3},{6,4},{7,5},{8,6},{9,7},{10,... | collective-permute-start | bytes 1769480 | tf_op jit(solution)/shard_map/ppermute | solution.py:32
  11.5 28.0 %collective-permute-start.10 = (f32[1,6,128,128]{3,2,1,0:T(8,128)}, f32[1,6,128,128]{3,2,1,0:T(8,128)}, u32[]{:S(2)}, u32[]{:S(2)}) collective-permute-start(f32[1,6,128,128]{3,2,1,0:T(8,128)} %constant_dynamic-slice_fusion), channel_id=1, source_target_pairs={{0,1},{1,0},{2,3},{3,2},{4,5},{5,4},{6,7},{7,6},{8,9},{9,8},{10,11... | collective-permute-start | bytes 1179656 | tf_op jit(solution)/shard_map/ppermute | solution.py:32
  16.4 17.6 %collective-permute-start.2 = (f32[1,6,128,128]{3,2,1,0:T(8,128)S(1)}, f32[1,6,128,128]{3,2,1,0:T(8,128)S(1)}, u32[]{:S(2)}, u32[]{:S(2)}) collective-permute-start(f32[1,6,128,128]{3,2,1,0:T(8,128)S(1)} %collective-permute-done.x0), channel_id=1, source_target_pairs={{0,2},{1,31},{2,4},{3,1},{4,6},{5,3},{6,8},{7,5},{8,10},{9,7},{10,... | collective-permute-start | bytes 1179656 | tf_op jit(solution)/shard_map/ppermute | solution.py:32
  22.3 11.6 %collective-permute-start.3 = (f32[1,6,128,128]{3,2,1,0:T(8,128)S(1)}, f32[1,6,128,128]{3,2,1,0:T(8,128)S(1)}, u32[]{:S(2)}, u32[]{:S(2)}) collective-permute-start(f32[1,6,128,128]{3,2,1,0:T(8,128)S(1)} %collective-permute-done.1.x1), channel_id=1, source_target_pairs={{0,2},{1,31},{2,4},{3,1},{4,6},{5,3},{6,8},{7,5},{8,10},{9,7},{10,... | collective-permute-start | bytes 1179656 | tf_op jit(solution)/shard_map/ppermute | solution.py:32
  37.4 16.4 %collective-permute-start.11 = (f32[1,6,128,128]{3,2,1,0:T(8,128)S(1)}, f32[1,6,128,128]{3,2,1,0:T(8,128)S(1)}, u32[]{:S(2)}, u32[]{:S(2)}) collective-permute-start(f32[1,6,128,128]{3,2,1,0:T(8,128)S(1)} %get-tuple-element.31), channel_id=1, source_target_pairs={{0,1},{1,0},{2,3},{3,2},{4,5},{5,4},{6,7},{7,6},{8,9},{9,8},{10,11... | collective-permute-start | bytes 1179656 | tf_op jit(solution)/shard_map/ppermute | solution.py:32
  38.7 9.1 %collective-permute-start.6 = (f32[3,128,128]{2,1,0:T(8,128)S(1)}, f32[3,128,128]{2,1,0:T(8,128)S(1)}, u32[]{:S(2)}, u32[]{:S(2)}) collective-permute-start(f32[3,128,128]{2,1,0:T(8,128)S(1)} %pad_maximum_fusion.1), channel_id=1, source_target_pairs={{0,4},{1,3},{2,6},{3,5},{4,8},{5,7},{6,10},{7,9},{8,12},{9,11},{10... | collective-permute-start | bytes 589832 | tf_op jit(solution)/shard_map/ppermute | solution.py:32
  38.7 30.6 %collective-permute-start.8 = (f32[7,128,128]{2,1,0:T(8,128)S(1)}, f32[7,128,128]{2,1,0:T(8,128)S(1)}, u32[]{:S(2)}, u32[]{:S(2)}) collective-permute-start(f32[7,128,128]{2,1,0:T(8,128)S(1)} %get-tuple-element.29), channel_id=1, source_target_pairs={{0,2},{1,3},{2,4},{3,5},{4,6},{5,7},{6,8},{7,9},{8,10},{9,11},{10,... | collective-permute-start | bytes 1376264 | tf_op jit(solution)/shard_map/ppermute | solution.py:32
  39.4 30.2 %collective-permute-start.9 = (f32[7,128,128]{2,1,0:T(8,128)S(1)}, f32[7,128,128]{2,1,0:T(8,128)S(1)}, u32[]{:S(2)}, u32[]{:S(2)}) collective-permute-start(f32[7,128,128]{2,1,0:T(8,128)S(1)} %get-tuple-element.30), channel_id=1, source_target_pairs={{0,30},{1,31},{2,0},{3,1},{4,2},{5,3},{6,4},{7,5},{8,6},{9,7},{10,... | collective-permute-start | bytes 1376264 | tf_op jit(solution)/shard_map/ppermute | solution.py:32
  39.4 27.5 %collective-permute-start.7 = (f32[3,128,128]{2,1,0:T(8,128)S(1)}, f32[3,128,128]{2,1,0:T(8,128)S(1)}, u32[]{:S(2)}, u32[]{:S(2)}) collective-permute-start(f32[3,128,128]{2,1,0:T(8,128)S(1)} %pad_maximum_fusion.2), channel_id=1, source_target_pairs={{0,30},{1,29},{2,0},{3,31},{4,2},{5,1},{6,4},{7,3},{8,6},{9,5},{10... | collective-permute-start | bytes 589832 | tf_op jit(solution)/shard_map/ppermute | solution.py:32
  47.8 26.3 %collective-permute-start.12 = (f32[1,6,128,128]{3,2,1,0:T(8,128)S(1)}, f32[1,6,128,128]{3,2,1,0:T(8,128)S(1)}, u32[]{:S(2)}, u32[]{:S(2)}) collective-permute-start(f32[1,6,128,128]{3,2,1,0:T(8,128)S(1)} %shard_map.62.nearer), channel_id=1, source_target_pairs={{0,2},{1,31},{2,4},{3,1},{4,6},{5,3},{6,8},{7,5},{8,10},{9,7},{10,... | collective-permute-start | bytes 1179656 | tf_op jit(solution)/shard_map/ppermute | solution.py:32
  53.8 24.1 %collective-permute-start.13 = (f32[1,6,128,128]{3,2,1,0:T(8,128)S(1)}, f32[1,6,128,128]{3,2,1,0:T(8,128)S(1)}, u32[]{:S(2)}, u32[]{:S(2)}) collective-permute-start(f32[1,6,128,128]{3,2,1,0:T(8,128)S(1)} %collective-permute-done.11.farther), channel_id=1, source_target_pairs={{0,2},{1,31},{2,4},{3,1},{4,6},{5,3},{6,8},{7,5},{8,10},{9,7},{10,... | collective-permute-start | bytes 1179656 | tf_op jit(solution)/shard_map/ppermute | solution.py:32
  69.3 7.4 %collective-permute-start.14 = (f32[3,128,128]{2,1,0:T(8,128)S(1)}, f32[3,128,128]{2,1,0:T(8,128)S(1)}, u32[]{:S(2)}, u32[]{:S(2)}) collective-permute-start(f32[3,128,128]{2,1,0:T(8,128)S(1)} %get-tuple-element.32), channel_id=1, source_target_pairs={{0,4},{1,3},{2,6},{3,5},{4,8},{5,7},{6,10},{7,9},{8,12},{9,11},{10... | collective-permute-start | bytes 589832 | tf_op jit(solution)/shard_map/ppermute | solution.py:32
  69.3 8.6 %collective-permute-start.15 = (f32[3,128,128]{2,1,0:T(8,128)S(1)}, f32[3,128,128]{2,1,0:T(8,128)S(1)}, u32[]{:S(2)}, u32[]{:S(2)}) collective-permute-start(f32[3,128,128]{2,1,0:T(8,128)S(1)} %get-tuple-element.33), channel_id=1, source_target_pairs={{0,30},{1,29},{2,0},{3,31},{4,2},{5,1},{6,4},{7,3},{8,6},{9,5},{10... | collective-permute-start | bytes 589832 | tf_op jit(solution)/shard_map/ppermute | solution.py:32

commit v4 on v3

--- a/solution.py
+++ b/solution.py
@@ -23,8 +23,6 @@
 DOWN = ((0, 0), (0, 1), (0, 2), (0, 3), (1, 1), (1, 2), (1, 3))
 Z_UP = ((0, 0), (0, 3), (0, 4), (0, 5), (1, 0), (1, 2), (1, 3), (1, 4), (1, 5))
 Z_DOWN = ((0, 0), (0, 1), (0, 2), (0, 3), (0, 4), (1, 0), (1, 1), (1, 2), (1, 3))
-FAR_UP = ((0, 5), (1, 4), (1, 5))
-FAR_DOWN = ((0, 1), (0, 2), (1, 1))
 
 
 def send(value, to):
@@ -36,12 +34,12 @@
     return i ^ 1
 
 
-def up(i):
-    return i + 2
-
-
-def down(i):
-    return i - 2
+def inside(i):
+    return i ^ 2
+
+
+def across(i):
+    return i + 2 if i // 2 % 2 else i - 2
 
 
 def near(i):
@@ -79,6 +77,7 @@
     def __init__(self, meta):
         self.meta = meta
         self.parity = meta[WIDE]
+        self.even_pair = meta[WIDE + 1] == 0
 
     def dropped(self, row):
         return self.meta[row - LEFT]
@@ -97,16 +96,17 @@
         tile = refs[row][0, slot] if isinstance(refs, tuple) else refs[row, slot]
         return jnp.where(there, tile, 0.0)
 
-    def packed(self, ref, layout, row0, r, col):
+    def packed(self, refs, layout, row0, r, col):
         slots = [s for rr, s in layout if rr == r]
         base = [j for j, (rr, _) in enumerate(layout) if rr == r][0]
         row = row0 + r
         if col == row:
-            return ref[base + slots.index(0)]
+            index = base + slots.index(0)
+            return jnp.where(self.even_pair, refs[0][index], refs[1][index])
         slot, there = slot_of(jnp.int32(col - row), self.dropped(row))
         rest = [s for s in slots if s]
         index = base + slots.index(rest[0]) + jnp.clip(slot - rest[0], 0, len(rest) - 1)
-        return jnp.where(there, ref[index], 0.0)
+        return jnp.where(there, jnp.where(self.even_pair, refs[0][index], refs[1][index]), 0.0)
 
     def side(self, ref, side, r, col):
         row = self.side_row(side) + r
@@ -154,21 +154,51 @@
                 out[i, c + j] = block[i * tile : (i + 1) * tile, j * tile : (j + 1) * tile]
 
 
-def pack_kernel(z, zu, zd):
-    for out, layout in ((zu, Z_UP), (zd, Z_DOWN)):
-        for j, (i, slot) in enumerate(layout):
-            out[j] = z[i, slot]
-
-
-def far_kernel(meta, nearer, farther, fu, fd):
-    even = meta[WIDE] == 0
-    for out, layout in ((fu, FAR_UP), (fd, FAR_DOWN)):
-        for j, (r, slot) in enumerate(layout):
-            a, b = (nearer, farther) if r == 0 else (farther, nearer)
-            out[j] = jnp.where(even, a[0, slot], b[0, slot])
-
-
-def product_kernel(meta, s, z, x0, x1, n0, n1, zu, zd, p0, p1, pf, pu, pd, z_high, z_low, s_high, s_low, dense):
+def both(layouts, tile_of, rows, chip, link):
+    for j, (first, second) in enumerate(zip(*layouts)):
+        a, b = tile_of(*first), tile_of(*second)
+        chip[j] = jnp.where(rows.even_pair, a, b)
+        link[j] = jnp.where(rows.even_pair, b, a)
+
+
+def pack_kernel(meta, z, z0, z1, chip, link):
+    for r, out in enumerate((z0, z1)):
+        for slot in range(2 * REACH):
+            out[0, slot] = z[r, slot]
+    both((Z_UP, Z_DOWN), lambda i, slot: z[i, slot], Rows(meta), chip, link)
+
+
+def far_tile(rows, refs, sign, r, c, tile):
+    if sign > 0:
+        offset = REACH - c if r == 0 else REACH - 1 + c
+        there = r == 1 or c == 0
+    else:
+        offset = -REACH + c if r == 0 else -REACH + 1 - c
+        there = r == 0 or c == 1
+    if not there:
+        return zero(tile)
+    slot, present = slot_of(jnp.int32(offset), rows.dropped(rows.side_row(0) + r))
+    if len(refs) == 1:
+        value = refs[0][0, slot]
+    else:
+        a, b = refs if r == 0 else refs[::-1]
+        value = jnp.where(rows.parity == 0, a[0, slot], b[0, slot])
+    return jnp.where(present, value, 0.0)
+
+
+def far_kernel(meta, t_up, t_down, nearer, farther, up, down, high, low):
+    tile = nearer.shape[-1]
+    rows = Rows(meta)
+    for turned, sign, out in ((t_up, 1, up), (t_down, -1, down)):
+        c0 = 0 if sign > 0 else 2
+        for r in range(2):
+            for c in range(2):
+                put(high, low, r, c0 + c, tile, far_tile(rows, (nearer, farther), sign, r, c, tile))
+        n = slice(c0 * tile, (c0 + 2) * tile)
+        out[...] = dot3(*halves(turned, 0, 1, tile), flat(high, slice(0, 2), n), flat(low, slice(0, 2), n))
+
+
+def product_kernel(meta, s, z, x0, x1, n0, n1, zi, zc, p0, p1, pf, chip, link, z_high, z_low, s_high, s_low, dense):
     tile = s.shape[-1]
     rows = Rows(meta)
     for c in range(COLS):
@@ -182,21 +212,19 @@
                 where = rows.side_row(side) + r - COL0
                 put(z_high, z_low, where, c, tile, rows.side(refs[r], side, r, col))
         row = -REACH
-        put(z_high, z_low, 0, c, tile, rows.packed(zu, Z_UP, -4, 1, col) if abs(col - row) <= REACH else zero(tile))
+        put(z_high, z_low, 0, c, tile, rows.packed((zc, zi), Z_UP, -4, 1, col) if abs(col - row) <= REACH else zero(tile))
         row = OWN - 1 + REACH
-        put(z_high, z_low, COLS - 1, c, tile, rows.packed(zd, Z_DOWN, 4, 0, col) if abs(col - row) <= REACH else zero(tile))
+        put(z_high, z_low, COLS - 1, c, tile, rows.packed((zi, zc), Z_DOWN, 4, 0, col) if abs(col - row) <= REACH else zero(tile))
     row_matmul(s_high, s_low, z_high, z_low, dense, tile)
     for i, ref in enumerate((p0, p1)):
         for slot in range(2 * REACH):
             ref[0, slot] = dense[i, rows.dense_slot(i, slot)]
     for slot in range(2 * REACH):
         pf[0, slot] = dense[rows.parity, rows.dense_slot(rows.parity, slot)]
-    for ref, layout in ((pu, UP), (pd, DOWN)):
-        for j, (i, slot) in enumerate(layout):
-            ref[j] = dense[i, rows.dense_slot(i, slot)]
-
-
-def side_kernel(meta, s, z, x0, x1, n0, n1, zu, zd, out, z_high, z_low, s_high, s_low, dense):
+    both((UP, DOWN), lambda i, slot: dense[i, rows.dense_slot(i, slot)], rows, chip, link)
+
+
+def side_kernel(meta, s, z, x0, x1, n0, n1, zi, zc, out, z_high, z_low, s_high, s_low, dense):
     tile = s.shape[-1]
     rows = Rows(meta)
     width = 2 * REACH + 1
@@ -211,10 +239,10 @@
         return lambda row, col: rows.side((n0, n1)[r], 1, r, col)
 
     def from_down(r):
-        return lambda row, col: rows.packed(zu, Z_UP, -4, r, col)
+        return lambda row, col: rows.packed((zc, zi), Z_UP, -4, r, col)
 
     def from_up(r):
-        return lambda row, col: rows.packed(zd, Z_DOWN, 4, r, col)
+        return lambda row, col: rows.packed((zi, zc), Z_DOWN, 4, r, col)
 
     even = (relayed(1), own(), own(), swapped(0), swapped(1), from_up(0), from_up(1))
     odd = (from_down(0), from_down(1), swapped(0), swapped(1), own(), own(), relayed(0))
@@ -252,7 +280,7 @@
         out[0, slot] = dense[REACH if slot == 0 else pos + jnp.where(pos >= REACH, 1, 0)]
 
 
-def turn_kernel(meta, z, x0, x1, n0, n1, zu, zd, fu, fd, t_own, t_up, t_down, t_swap, t_near, t_far, z_own):
+def turn_kernel(meta, z, x0, x1, n0, n1, zi, zc, t_own, t_up, t_down, t_swap, t_near, t_far_up, t_far_down, z_own):
     tile = z.shape[-1]
     rows = Rows(meta)
 
@@ -271,14 +299,12 @@
             z_own[r, :, (COLS + c) * tile : (COLS + c + 1) * tile] = low
         for c in range(4):
             col = c + COL0
-            store(t_up, c, r, rows.packed(zu, Z_UP, -4, r, col) if abs(col - (r - 4)) <= REACH else zero(tile))
+            store(t_up, c, r, rows.packed((zc, zi), Z_UP, -4, r, col) if abs(col - (r - 4)) <= REACH else zero(tile))
             col = c + COL0 + 4
-            store(t_down, c, r, rows.packed(zd, Z_DOWN, 4, r, col) if abs(col - (r + 4)) <= REACH else zero(tile))
+            store(t_down, c, r, rows.packed((zi, zc), Z_DOWN, 4, r, col) if abs(col - (r + 4)) <= REACH else zero(tile))
         for c in range(2):
-            col = c + COL0
-            store(t_far, c, r, rows.packed(fu, FAR_UP, -6, r, col) if abs(col - (r - 6)) <= REACH else zero(tile))
-            col = c + COL0 + 6
-            store(t_far, 2 + c, r, rows.packed(fd, FAR_DOWN, 6, r, col) if abs(col - (r + 6)) <= REACH else zero(tile))
+            store(t_far_up, c, r, far_tile(rows, ((x0, x1)[r],), 1, r, c, tile))
+            store(t_far_down, c, r, far_tile(rows, ((x0, x1)[r],), -1, r, c, tile))
         for side, (out, refs) in enumerate(((t_swap, (x0, x1)), (t_near, (n0, n1)))):
             first = 2 * rows.side_pair(side) + COL0
             for c in range(2 * SIDE):
@@ -303,7 +329,7 @@
             add(a, b, block[2 * a * tile : (2 * a + 2) * tile])
 
 
-def gram_kernel(meta, t_own, t_up, t_down, t_swap, p0, p1, pu, pd, nearer, farther, gram, high, low, side_high, side_low):
+def gram_kernel(meta, t_own, t_up, t_down, t_swap, p0, p1, pi, pc, nearer, farther, gram, high, low, side_high, side_low):
     tile = p0.shape[-1]
     rows = Rows(meta)
     for r in range(2):
@@ -312,10 +338,10 @@
             put(high, low, r, c, tile, rows.own((p0, p1), r, col) if abs(col - r) <= REACH else zero(tile))
         for c in range(4):
             col = c + COL0
-            value = rows.packed(pu, UP, -4, r, col) if abs(col - (r - 4)) <= REACH else zero(tile)
+            value = rows.packed((pc, pi), UP, -4, r, col) if abs(col - (r - 4)) <= REACH else zero(tile)
             put(high, low, 2 + r, c, tile, value)
             col = c + COL0 + 4
-            value = rows.packed(pd, DOWN, 4, r, col) if abs(col - (r + 4)) <= REACH else zero(tile)
+            value = rows.packed((pi, pc), DOWN, 4, r, col) if abs(col - (r + 4)) <= REACH else zero(tile)
             put(high, low, 2 + r, 4 + c, tile, value)
     for b in range(PAIRS):
         n = slice(2 * b * tile, (2 * b + 2) * tile)
@@ -339,8 +365,7 @@
 
 
 def refine_kernel(
-    meta, z, z_own, t_near, t_far, early, nearer, farther, fu, fd, refined, correction,
-    high, low, far_high, far_low, late, d_high, d_low, dense, z_high, z_low,
+    meta, z, z_own, t_near, early, nearer, farther, far_up, far_down, refined, correction, high, low, late, d_high, d_low, dense, z_high, z_low,
 ):
     tile = z.shape[-1]
     rows = Rows(meta)
@@ -349,20 +374,6 @@
         late[SIDE * a + b] = value
 
     side_gram(rows, 1, (nearer, farther), t_near, high, low, add, tile)
-    for r in range(2):
-        for c in range(2):
-            col = c + COL0
-            value = rows.packed(fu, FAR_UP, -6, r, col) if abs(col - (r - 6)) <= REACH else zero(tile)
-            put(far_high, far_low, r, c, tile, value)
-            col = c + COL0 + 6
-            value = rows.packed(fd, FAR_DOWN, 6, r, col) if abs(col - (r + 6)) <= REACH else zero(tile)
-            put(far_high, far_low, r, 2 + c, tile, value)
-    far = []
-    for e in range(2):
-        n = slice(2 * e * tile, (2 * e + 2) * tile)
-        far.append(
-            dot3(*halves(t_far, e, e + 1, tile), flat(far_high, slice(0, 2), n), flat(far_low, slice(0, 2), n))
-        )
     eye = (
         lax.broadcasted_iota(jnp.int32, (tile, tile), 0) == lax.broadcasted_iota(jnp.int32, (tile, tile), 1)
     ).astype(F32)
@@ -376,7 +387,7 @@
             there = (ia >= 0) & (ia < SIDE) & (ib >= 0) & (ib < SIDE)
             gram = gram + jnp.where(there, late[jnp.clip(SIDE * ia + ib, 0, SIDE * SIDE - 1)], 0.0)
             if a == b and a in (0, PAIRS - 1):
-                gram = gram + far[0 if a == 0 else 1]
+                gram = gram + (far_up if a == 0 else far_down)[...]
             for i in range(2):
                 for j in range(2):
                     k, c = 2 * a + i, 2 * b + j
@@ -402,14 +413,6 @@
             refined[i, slot] = z[i, slot] + 0.5 * dense[i, rows.dense_slot(i, slot)]
 
 
-def far(rows):
-    first = lax.optimization_barrier(
-        jnp.concatenate([rows[0][0, s : s + 1] for r, s in FAR_UP + FAR_DOWN if r == 0], axis=0)
-    )
-    last = [rows[1][0, s : s + 1] for r, s in FAR_UP + FAR_DOWN if r == 1]
-    return jnp.concatenate([first[:1], *last[:2]], axis=0), jnp.concatenate([first[1:], last[2]], axis=0)
-
-
 def body(correlation, factor, pattern):
     rows_here, slots, tile = correlation.shape[:3]
     total = pattern.shape[0]
@@ -419,7 +422,8 @@
     offsets = (pattern[rows][:, 1:] - rows[:, None] + total // 2) % total - total // 2
     expected = jnp.array([-3, -2, -1, 1, 2], jnp.int32)
     dropped = jnp.sum((offsets == expected).astype(jnp.int32), axis=1)
-    meta = jnp.concatenate([dropped, (device % 2)[None]]).astype(jnp.int32)
+    place = jnp.stack([0] * WIDE + [device % 2, device // 2 % 2]).astype(jnp.int32)
+    meta = jnp.concatenate([dropped, (device % 2)[None], (device // 2 % 2)[None]]).astype(jnp.int32)
 
     vmem = pl.BlockSpec(memory_space=pltpu.VMEM)
     smem = pl.BlockSpec(memory_space=pltpu.SMEM)
@@ -444,62 +448,60 @@
     row = shape(1, slots, tile, tile)
     seven = shape(len(UP), tile, tile)
     nine = shape(len(Z_UP), tile, tile)
-    three = shape(len(FAR_UP), tile, tile)
+    block = shape(2 * tile, 2 * tile)
     parity = device % 2
     dense = pltpu.VMEM((OWN, COLS, tile, tile), F32)
 
-    x = [send(factor[r : r + 1], swap) for r in range(OWN)]
-    zu, zd = call(pack_kernel, (factor,), (nine, nine), [], 1000, 0)
-    zu, zd = send(zu, up), send(zd, down)
+    z0, z1, zi, zc = call(pack_kernel, (place, factor), (row, row, nine, nine), [], 1000)
+    x = [send(v, swap) for v in (z0, z1)]
+    zi, zc = send(zi, inside), send(zc, across)
     n = [send(x[r], near) for r in range(OWN)]
     sx = send(lax.dynamic_slice_in_dim(correlation, 1 - parity, 1, 0), swap)
-    zfu, zfd = far(x)
-    zfu, zfd = send(zfu, far_up), send(zfd, far_down)
-    p0, p1, pf, pu, pd = call(
+    p0, p1, pf, pi, pc = call(
         product_kernel,
-        (meta, correlation, factor, *x, *n, zu, zd),
+        (meta, correlation, factor, *x, *n, zi, zc),
         (row, row, row, seven, seven),
         halves_of(COLS, COLS) + halves_of(OWN, COLS) + [dense],
         int(2e9),
     )
+    pc = send(pc, across)
     px = send(pf, swap)
-    pu, pd = send(pu, up), send(pd, down)
+    pi = send(pi, inside)
     width = 2 * REACH + 1
     ps = call(
         side_kernel,
-        (meta, sx, factor, *x, *n, zu, zd),
+        (meta, sx, factor, *x, *n, zi, zc),
         row,
         halves_of(width, width) + halves_of(1, width) + [pltpu.VMEM((width, tile, tile), F32)],
         int(2e9),
     )
     pn = (send(ps, near), send(px, near))
-    pfu, pfd = call(far_kernel, (meta, ps, px), (three, three), [], 1000)
-    pfu, pfd = send(pfu, far_up), send(pfd, far_down)
 
     def turned(columns):
         return shape(columns * tile, 4 * tile, dtype=BF16)
 
-    t_own, t_up, t_down, t_swap, t_near, t_far, z_own = call(
+    t_own, t_up, t_down, t_swap, t_near, t_far_up, t_far_down, z_own = call(
         turn_kernel,
-        (meta, factor, *x, *n, zu, zd, zfu, zfd),
-        (turned(COLS), turned(4), turned(4), turned(2 * SIDE), turned(2 * SIDE), turned(4),
+        (meta, factor, *x, *n, zi, zc),
+        (turned(COLS), turned(4), turned(4), turned(2 * SIDE), turned(2 * SIDE), turned(2), turned(2),
          shape(OWN, tile, 2 * COLS * tile, dtype=BF16)),
         [],
         int(2e9),
     )
+    gu, gd = call(far_kernel, (meta, t_far_up, t_far_down, ps, px), (block, block), halves_of(2, 4), int(1e8))
+    gu, gd = send(gu, far_up), send(gd, far_down)
     early = call(
         gram_kernel,
-        (meta, t_own, t_up, t_down, t_swap, p0, p1, pu, pd, ps, px),
+        (meta, t_own, t_up, t_down, t_swap, p0, p1, pi, pc, ps, px),
         shape(PAIRS * PAIRS, 2 * tile, 2 * tile),
         halves_of(4, COLS) + halves_of(2, 2 * SIDE),
         int(4e9),
     )
     return call(
         refine_kernel,
-        (meta, factor, z_own, t_near, t_far, early, *pn, pfu, pfd),
+        (meta, factor, z_own, t_near, early, *pn, gu, gd),
         (shape(*factor.shape), shape(*factor.shape)),
         halves_of(2, 2 * SIDE)
-        + halves_of(2, 4)
         + [pltpu.VMEM((SIDE * SIDE, 2 * tile, 2 * tile), F32)]
         + halves_of(COLS, COLS)
         + [dense]

time: 84.1 us -> 79.1 us (0.941)
  waiting for transfers between devices: 30.2 us -> 23.4 us
  Pallas kernels: 18.9 us -> 21.5 us
    ppermute x16 -> x14, waiting for transfers between devices: 30.2 us -> 23.4 us  [send(): return lax.ppermute(value, AXES, [(i, to(i) % count) for i in range(count)])]
    pallas_call x7, Pallas kernels: 18.9 us -> 21.5 us  [call(): pl.pallas_call(kernel, in_specs=[smem] * scalars + [vmem] * (len(ins) - s...]
    unnamed x7 -> x9, local copies, waits for them, and re-layouts: 2.52 us -> 4.79 us
    slice x3 -> x0, local copies, waits for them, and re-layouts: 2.19 us -> none  [the longest x1 2.17 us: body(): x = [send(factor[r:r + 1], swap) for r in range(OWN)]]
    ppermute x16 -> x14, starting transfers between devices: 24.5 us -> 23.9 us  [send(): return lax.ppermute(value, AXES, [(i, to(i) % count) for i in range(count)])]
  transfers between devices with their start and end apart: 16 -> 14, of which waited for: 6 -> 5; matrix products, arithmetic and copies ran while one was open for 7% -> 7% of each run, Pallas kernels for 16% -> 18%
where the time goes in v4:
time: 79.1 us; the launch traced here: 78.6 us
  starting transfers between devices  23.9 us (30%)
  waiting for transfers between devices  23.4 us (30%)
  Pallas kernels  21.5 us (27%)
  local copies, waits for them, and re-layouts  7.97 us (10%)
  other arithmetic  0.96 us (1%)
  between operations  0.8 us (1%)
    ppermute x14, starting transfers between devices, send(): return lax.ppermute(value, AXES, [(i, to(i) % count) for i in range(count)])  23.9 us
    ppermute x14, waiting for transfers between devices, send(): return lax.ppermute(value, AXES, [(i, to(i) % count) for i in range(count)])  23.4 us
    pallas_call x7, Pallas kernels, call(): pl.pallas_call(kernel, in_specs=[smem] * scalars + [vmem] * (len(ins) - s...  21.5 us
    unnamed x9, local copies, waits for them, and re-layouts  4.79 us
    dynamic_slice x1, local copies, waits for them, and re-layouts, body(): sx = send(lax.dynamic_slice_in_dim(correlation, 1 - parity, 1, 0), swap)  1.77 us
  transfers between devices with their start and end apart: 14, of which 5 were waited for; matrix products, arithmetic and copies ran while one was open for 7% of the time, Pallas kernels for 18%

profile of v4, /device:TPU:1, one launch (start us, length us, event | category | flops | bytes accessed | tf_op | source)
XLA Modules:
  0.0 78.6 jit_solution(16176387699068517495)
XLA Ops:
  0.7 0.1 stack.2.meta
  0.8 0.0 copy-start
  0.8 1.1 %copy-done = f32[2,6,128,128]{3,2,1,0:T(8,128)S(1)} copy-done((f32[2,6,128,128]{3,2,1,0:T(8,128)S(1)}, f32[2,6,128,128]{3,2,1,0:T(8,128)}, u32[]{:S(2)}) %copy-start) | copy-done | bytes 786456
  1.9 1.4 %shard_map.59 = (f32[1,6,128,128]{3,2,1,0:T(8,128)S(1)}, f32[1,6,128,128]{3,2,1,0:T(8,128)}, f32[9,128,128]{2,1,0:T(8,128)S(1)}, f32[9,128,128]{2,1,0:T(8,128)S(1)}) custom-call(s32[16]{0:T(128)S(1)} %stack.2.meta, f32[2,6,128,128]{3,2,1,0:T(8,128)S(1)} %copy-done), custom_call_target="tpu_custom_call" | custom-call | flops 1000 | bytes 4194304 | tf_op jit(solution)/shard_map/pallas_call | solution.py:432
  3.3 2.0 %collective-permute-start = (f32[1,6,128,128]{3,2,1,0:T(8,128)S(1)}, f32[1,6,128,128]{3,2,1,0:T(8,128)S(1)}, u32[]{:S(2)}, u32[]{:S(2)}) collective-permute-start(f32[1,6,128,128]{3,2,1,0:T(8,128)S(1)} %get-tuple-element.21), channel_id=1, source_target_pairs={{0,1},{1,0},{2,3},{3,2},{4,5},{5,4},{6,7},{7,6},{8,9},{9,8},{10,11... | collective-permute-start | bytes 1179656 | tf_op jit(solution)/shard_map/ppermute | solution.py:30
  5.3 0.0 collective-permute-start.1
  5.4 1.0 %collective-permute-start.4 = (f32[9,128,128]{2,1,0:T(8,128)S(1)}, f32[9,128,128]{2,1,0:T(8,128)S(1)}, u32[]{:S(2)}, u32[]{:S(2)}) collective-permute-start(f32[9,128,128]{2,1,0:T(8,128)S(1)} %get-tuple-element.23), channel_id=1, source_target_pairs={{0,2},{1,3},{2,0},{3,1},{4,6},{5,7},{6,4},{7,5},{8,10},{9,11},{10,... | collective-permute-start | bytes 1769480 | tf_op jit(solution)/shard_map/ppermute | solution.py:30
  6.3 1.6 %collective-permute-start.5 = (f32[9,128,128]{2,1,0:T(8,128)S(1)}, f32[9,128,128]{2,1,0:T(8,128)S(1)}, u32[]{:S(2)}, u32[]{:S(2)}) collective-permute-start(f32[9,128,128]{2,1,0:T(8,128)S(1)} %get-tuple-element.24), channel_id=1, source_target_pairs={{0,30},{1,31},{2,4},{3,5},{4,2},{5,3},{6,8},{7,9},{8,6},{9,7},{10,... | collective-permute-start | bytes 1769480 | tf_op jit(solution)/shard_map/ppermute | solution.py:30
  8.0 1.8 %constant_dynamic-slice_fusion = f32[1,6,128,128]{3,2,1,0:T(8,128)} fusion(f32[2,6,128,128]{3,2,1,0:T(8,128)} %s.1, s32[]{:T(128)S(6)} %select_n.66), kind=kLoop, calls=%fused_computation.22 | loop fusion | bytes 786436 | tf_op jit(solution)/shard_map/dynamic_slice | solution.py:459
  9.7 1.2 %collective-permute-start.8 = (f32[1,6,128,128]{3,2,1,0:T(8,128)}, f32[1,6,128,128]{3,2,1,0:T(8,128)}, u32[]{:S(2)}, u32[]{:S(2)}) collective-permute-start(f32[1,6,128,128]{3,2,1,0:T(8,128)} %constant_dynamic-slice_fusion), channel_id=1, source_target_pairs={{0,1},{1,0},{2,3},{3,2},{4,5},{5,4},{6,7},{7,6},{8,9},{9,8},{10,11... | collective-permute-start | bytes 1179656 | tf_op jit(solution)/shard_map/ppermute | solution.py:30
  11.0 3.2 %collective-permute-done.x0 = f32[1,6,128,128]{3,2,1,0:T(8,128)S(1)} collective-permute-done((f32[1,6,128,128]{3,2,1,0:T(8,128)S(1)}, f32[1,6,128,128]{3,2,1,0:T(8,128)S(1)}, u32[]{:S(2)}, u32[]{:S(2)}) %collective-permute-start) | collective-permute-done | bytes 393248 | tf_op jit(solution)/shard_map/ppermute | solution.py:30
  14.2 3.8 %collective-permute-start.2 = (f32[1,6,128,128]{3,2,1,0:T(8,128)S(1)}, f32[1,6,128,128]{3,2,1,0:T(8,128)S(1)}, u32[]{:S(2)}, u32[]{:S(2)}) collective-permute-start(f32[1,6,128,128]{3,2,1,0:T(8,128)S(1)} %collective-permute-done.x0), channel_id=1, source_target_pairs={{0,2},{1,31},{2,4},{3,1},{4,6},{5,3},{6,8},{7,5},{8,10},{9,7},{10,... | collective-permute-start | bytes 1179656 | tf_op jit(solution)/shard_map/ppermute | solution.py:30
  17.9 4.7 %collective-permute-done.1.x1 = f32[1,6,128,128]{3,2,1,0:T(8,128)S(1)} collective-permute-done((f32[1,6,128,128]{3,2,1,0:T(8,128)}, f32[1,6,128,128]{3,2,1,0:T(8,128)S(1)}, u32[]{:S(2)}, u32[]{:S(2)}) %collective-permute-start.1) | collective-permute-done | bytes 393248 | tf_op jit(solution)/shard_map/ppermute | solution.py:30
  22.6 3.8 %collective-permute-start.3 = (f32[1,6,128,128]{3,2,1,0:T(8,128)S(1)}, f32[1,6,128,128]{3,2,1,0:T(8,128)}, u32[]{:S(2)}, u32[]{:S(2)}) collective-permute-start(f32[1,6,128,128]{3,2,1,0:T(8,128)S(1)} %collective-permute-done.1.x1), channel_id=1, source_target_pairs={{0,2},{1,31},{2,4},{3,1},{4,6},{5,3},{6,8},{7,5},{8,10},{9,7},{10,... | collective-permute-start | bytes 1179656 | tf_op jit(solution)/shard_map/ppermute | solution.py:30
  26.3 1.4 %copy.6 = s32[64,6]{1,0:T(8,128)} copy(s32[64,6]{0,1:T(8,128)} %param.6) | data formatting | bytes 3072 | tf_op args[2]
  27.7 1.3 %gather_fusion = s32[14,6]{1,0:T(8,128)S(1)} fusion(s32[64,6]{1,0:T(8,128)} %copy.6, s32[1024]{0:T(1024)S(1)} %pad_clamp_fusion), kind=kCustom, calls=%fused_computation | custom fusion | bytes 728 | tf_op jit(solution)/shard_map/gather | solution.py:422
  29.1 0.8 %convert_reduce_fusion = s32[14]{0:T(128)S(1)} fusion(s32[14,6]{1,0:T(8,128)S(1)} %gather_fusion, s32[5]{0:T(128)} %constant.83.clone, s32[14]{0:T(128)S(1)} %and_select_fusion), kind=kLoop, calls=%fused_computation.9 | loop fusion | flops 1176 | bytes 412 | tf_op jit(solution)/shard_map/reduce_sum | solution.py:424
  29.9 0.1 pad_add_fusion.meta
  30.0 0.0 collective-permute-done.4.zi
  30.0 0.0 collective-permute-done.5.zc
  30.0 0.0 collective-permute-done.2.n0
  30.0 1.0 %collective-permute-done.3.n1 = f32[1,6,128,128]{3,2,1,0:T(8,128)} collective-permute-done((f32[1,6,128,128]{3,2,1,0:T(8,128)S(1)}, f32[1,6,128,128]{3,2,1,0:T(8,128)}, u32[]{:S(2)}, u32[]{:S(2)}) %collective-permute-start.3) | collective-permute-done | bytes 393248 | tf_op jit(solution)/shard_map/ppermute | solution.py:30
  31.1 0.0 copy-start.1
  31.1 1.1 %copy-done.1 = f32[2,6,128,128]{3,2,1,0:T(8,128)S(1)} copy-done((f32[2,6,128,128]{3,2,1,0:T(8,128)S(1)}, f32[2,6,128,128]{3,2,1,0:T(8,128)}, u32[]{:S(2)}) %copy-start.1) | copy-done | bytes 786456
  32.2 1.1 %copy-done.3 = f32[2,6,128,128]{3,2,1,0:T(8,128)S(1)} copy-done((f32[2,6,128,128]{3,2,1,0:T(8,128)S(1)}, f32[2,6,128,128]{3,2,1,0:T(8,128)}, u32[]{:S(2)}) %copy-start.3) | copy-done | bytes 786456
  33.3 3.9 %shard_map.61 = (f32[1,6,128,128]{3,2,1,0:T(8,128)S(1)}, f32[1,6,128,128]{3,2,1,0:T(8,128)S(1)}, f32[1,6,128,128]{3,2,1,0:T(8,128)S(1)}, f32[7,128,128]{2,1,0:T(8,128)S(1)}, f32[7,128,128]{2,1,0:T(8,128)S(1)}) custom-call(s32[16]{0:T(128)S(1)} %pad_add_fusion.meta, f32[2,6,128,128]{3,2,1,0:T(8,128)S(1)} %copy-done.3, f32[2,6,128,128]{3,2,1,0:T(8,128)S(1)} %copy-done.1, ...), custom_call_target="tpu_custom_call" | custom-call | flops 2000000000 | bytes 4194304 | tf_op jit(solution)/shard_map/pallas_call | solution.py:432
  37.3 2.4 %collective-permute-start.9 = (f32[1,6,128,128]{3,2,1,0:T(8,128)S(1)}, f32[1,6,128,128]{3,2,1,0:T(8,128)S(1)}, u32[]{:S(2)}, u32[]{:S(2)}) collective-permute-start(f32[1,6,128,128]{3,2,1,0:T(8,128)S(1)} %get-tuple-element.35), channel_id=1, source_target_pairs={{0,1},{1,0},{2,3},{3,2},{4,5},{5,4},{6,7},{7,6},{8,9},{9,8},{10,11... | collective-permute-start | bytes 1179656 | tf_op jit(solution)/shard_map/ppermute | solution.py:30
  39.7 1.3 %collective-permute-start.6 = (f32[7,128,128]{2,1,0:T(8,128)S(1)}, f32[7,128,128]{2,1,0:T(8,128)S(1)}, u32[]{:S(2)}, u32[]{:S(2)}) collective-permute-start(f32[7,128,128]{2,1,0:T(8,128)S(1)} %get-tuple-element.33), channel_id=1, source_target_pairs={{0,2},{1,3},{2,0},{3,1},{4,6},{5,7},{6,4},{7,5},{8,10},{9,11},{10,... | collective-permute-start | bytes 1376264 | tf_op jit(solution)/shard_map/ppermute | solution.py:30
  41.0 0.0 collective-permute-start.7
  41.0 0.0 collective-permute-done.8.s
  41.1 2.4 %shard_map.62.nearer = f32[1,6,128,128]{3,2,1,0:T(8,128)S(1)} custom-call(s32[16]{0:T(128)S(1)} %pad_add_fusion.meta, f32[1,6,128,128]{3,2,1,0:T(8,128)} %collective-permute-done.8.s, f32[2,6,128,128]{3,2,1,0:T(8,128)S(1)} %copy-done.1, f32[1,6,128,128]{3,2,1,0:T(8,128)S(1)} %collective-permute-done.x0, f32[1,6,128,128]{3,2,1,0:T(8,128)S(1)} %collective-permute-done.1.x1, ...), custom_call_target="tpu_custom_call" | custom-call | flops 2000000000 | bytes 4194304 | tf_op jit(solution)/shard_map/pallas_call | solution.py:432
  43.5 1.8 %collective-permute-start.10 = (f32[1,6,128,128]{3,2,1,0:T(8,128)S(1)}, f32[1,6,128,128]{3,2,1,0:T(8,128)S(1)}, u32[]{:S(2)}, u32[]{:S(2)}) collective-permute-start(f32[1,6,128,128]{3,2,1,0:T(8,128)S(1)} %shard_map.62.nearer), channel_id=1, source_target_pairs={{0,2},{1,31},{2,4},{3,1},{4,6},{5,3},{6,8},{7,5},{8,10},{9,7},{10,... | collective-permute-start | bytes 1179656 | tf_op jit(solution)/shard_map/ppermute | solution.py:30
  45.3 1.9 %collective-permute-done.9.farther = f32[1,6,128,128]{3,2,1,0:T(8,128)S(1)} collective-permute-done((f32[1,6,128,128]{3,2,1,0:T(8,128)S(1)}, f32[1,6,128,128]{3,2,1,0:T(8,128)S(1)}, u32[]{:S(2)}, u32[]{:S(2)}) %collective-permute-start.9) | collective-permute-done | bytes 393248 | tf_op jit(solution)/shard_map/ppermute | solution.py:30
  47.2 3.4 %collective-permute-start.11 = (f32[1,6,128,128]{3,2,1,0:T(8,128)S(1)}, f32[1,6,128,128]{3,2,1,0:T(8,128)S(1)}, u32[]{:S(2)}, u32[]{:S(2)}) collective-permute-start(f32[1,6,128,128]{3,2,1,0:T(8,128)S(1)} %collective-permute-done.9.farther), channel_id=1, source_target_pairs={{0,2},{1,31},{2,4},{3,1},{4,6},{5,3},{6,8},{7,5},{8,10},{9,7},{10,... | collective-permute-start | bytes 1179656 | tf_op jit(solution)/shard_map/ppermute | solution.py:30
  50.6 2.2 %shard_map.60 = (bf16[1024,512]{1,0:T(8,128)(2,1)S(1)}, bf16[512,512]{1,0:T(8,128)(2,1)S(1)}, bf16[512,512]{1,0:T(8,128)(2,1)S(1)}, bf16[768,512]{1,0:T(8,128)(2...) custom-call(s32[16]{0:T(128)S(1)} %pad_add_fusion.meta, ...), custom_call_target="tpu_custom_call" | custom-call | flops 2000000000 | bytes 4194304 | tf_op jit(solution)/shard_map/pallas_call | solution.py:432
  52.7 1.0 %shard_map.64 = (f32[256,256]{1,0:T(8,128)S(1)}, f32[256,256]{1,0:T(8,128)S(1)}) custom-call(s32[16]{0:T(128)S(1)} %pad_add_fusion.meta, bf16[256,512]{1,0:T(8,128)(2,1)S(1)} %get-tuple-element.36.t_up, bf16[256,512]{1,0:T(8,128)(2,1)S(1)} %get-tuple-element.37.t_down, f32[1,6,128,128]{3,2,1,0:T(8,128)S(1)} %shard_map.62.nearer, ...), custom_call_target="tpu_custom_call" | custom-call | flops 100000000 | bytes 4194304 | tf_op jit(solution)/shard_map/pallas_call | solution.py:432
  53.7 1.6 %collective-permute-start.12 = (f32[256,256]{1,0:T(8,128)S(1)}, f32[256,256]{1,0:T(8,128)S(1)}, u32[]{:S(2)}, u32[]{:S(2)}) collective-permute-start(f32[256,256]{1,0:T(8,128)S(1)} %get-tuple-element.38), channel_id=1, source_target_pairs={{0,4},{1,3},{2,6},{3,5},{4,8},{5,7},{6,10},{7,9},{8,12},{9,11},{10... | collective-permute-start | bytes 786440 | tf_op jit(solution)/shard_map/ppermute | solution.py:30
  55.3 0.0 collective-permute-done.6.pi
  55.3 0.0 collective-permute-start.13
  55.3 12.6 %collective-permute-done.7.pc = f32[7,128,128]{2,1,0:T(8,128)S(1)} collective-permute-done((f32[7,128,128]{2,1,0:T(8,128)S(1)}, f32[7,128,128]{2,1,0:T(8,128)S(1)}, u32[]{:S(2)}, u32[]{:S(2)}) %collective-permute-start.7) | collective-permute-done | bytes 458784 | tf_op jit(solution)/shard_map/ppermute | solution.py:30
  67.9 0.0 copy-start.2
  67.9 4.5 %shard_map.63.early = f32[16,256,256]{2,1,0:T(8,128)S(1)} custom-call(s32[16]{0:T(128)S(1)} %pad_add_fusion.meta, bf16[1024,512]{1,0:T(8,128)(2,1)S(1)} %get-tuple-element.27.t_own, bf16[512,512]{1,0:T(8,128)(2,1)S(1)} %get-tuple-element.28.t_up, bf16[512,512]{1,0:T(8,128)(2,1)S(1)} %get-tuple-element.29.t_down, ...), custom_call_target="tpu_custom_call" | custom-call | flops 4000000000 | bytes 4194304 | tf_op jit(solution)/shard_map/pallas_call | solution.py:432
  72.4 0.0 collective-permute-done.10.nearer
  72.4 0.0 collective-permute-done.12.far_up
  72.4 0.0 collective-permute-done.13.far_down
  72.4 0.0 collective-permute-done.11.farther
  72.4 0.0 copy-done.2
  72.5 6.1 %shard_map.65 = (f32[2,6,128,128]{3,2,1,0:T(8,128)}, f32[2,6,128,128]{3,2,1,0:T(8,128)}) custom-call(s32[16]{0:T(128)S(1)} %pad_add_fusion.meta, f32[2,6,128,128]{3,2,1,0:T(8,128)S(1)} %copy-done.2, bf16[2,128,2048]{2,1,0:T(8,128)(2,1)S(1)} %get-tuple-element.25.z_own, bf16[768,512]{1,0:T(8,128)(2,1)S(1)} %get-tuple-element.26.t_near, ...), custom_call_target="tpu_custom_call" | custom-call | flops 4000000000 | bytes 4194304 | tf_op jit(solution)/shard_map/pallas_call | solution.py:432
  (7 shorter events, 0.0 us)
Async XLA Ops:
  0.8 1.1 %copy-start = (f32[2,6,128,128]{3,2,1,0:T(8,128)S(1)}, f32[2,6,128,128]{3,2,1,0:T(8,128)}, u32[]{:S(2)}) copy-start(f32[2,6,128,128]{3,2,1,0:T(8,128)} %z.9) | copy-start | bytes 2359300
  3.3 10.8 %collective-permute-start = (f32[1,6,128,128]{3,2,1,0:T(8,128)S(1)}, f32[1,6,128,128]{3,2,1,0:T(8,128)S(1)}, u32[]{:S(2)}, u32[]{:S(2)}) collective-permute-start(f32[1,6,128,128]{3,2,1,0:T(8,128)S(1)} %get-tuple-element.21), channel_id=1, source_target_pairs={{0,1},{1,0},{2,3},{3,2},{4,5},{5,4},{6,7},{7,6},{8,9},{9,8},{10,11... | collective-permute-start | bytes 1179656 | tf_op jit(solution)/shard_map/ppermute | solution.py:30
  5.3 17.2 %collective-permute-start.1 = (f32[1,6,128,128]{3,2,1,0:T(8,128)}, f32[1,6,128,128]{3,2,1,0:T(8,128)S(1)}, u32[]{:S(2)}, u32[]{:S(2)}) collective-permute-start(f32[1,6,128,128]{3,2,1,0:T(8,128)} %get-tuple-element.22), channel_id=1, source_target_pairs={{0,1},{1,0},{2,3},{3,2},{4,5},{5,4},{6,7},{7,6},{8,9},{9,8},{10,11... | collective-permute-start | bytes 1179656 | tf_op jit(solution)/shard_map/ppermute | solution.py:30
  5.4 24.6 %collective-permute-start.4 = (f32[9,128,128]{2,1,0:T(8,128)S(1)}, f32[9,128,128]{2,1,0:T(8,128)S(1)}, u32[]{:S(2)}, u32[]{:S(2)}) collective-permute-start(f32[9,128,128]{2,1,0:T(8,128)S(1)} %get-tuple-element.23), channel_id=1, source_target_pairs={{0,2},{1,3},{2,0},{3,1},{4,6},{5,7},{6,4},{7,5},{8,10},{9,11},{10,... | collective-permute-start | bytes 1769480 | tf_op jit(solution)/shard_map/ppermute | solution.py:30
  6.3 23.7 %collective-permute-start.5 = (f32[9,128,128]{2,1,0:T(8,128)S(1)}, f32[9,128,128]{2,1,0:T(8,128)S(1)}, u32[]{:S(2)}, u32[]{:S(2)}) collective-permute-start(f32[9,128,128]{2,1,0:T(8,128)S(1)} %get-tuple-element.24), channel_id=1, source_target_pairs={{0,30},{1,31},{2,4},{3,5},{4,2},{5,3},{6,8},{7,9},{8,6},{9,7},{10,... | collective-permute-start | bytes 1769480 | tf_op jit(solution)/shard_map/ppermute | solution.py:30
  9.7 31.3 %collective-permute-start.8 = (f32[1,6,128,128]{3,2,1,0:T(8,128)}, f32[1,6,128,128]{3,2,1,0:T(8,128)}, u32[]{:S(2)}, u32[]{:S(2)}) collective-permute-start(f32[1,6,128,128]{3,2,1,0:T(8,128)} %constant_dynamic-slice_fusion), channel_id=1, source_target_pairs={{0,1},{1,0},{2,3},{3,2},{4,5},{5,4},{6,7},{7,6},{8,9},{9,8},{10,11... | collective-permute-start | bytes 1179656 | tf_op jit(solution)/shard_map/ppermute | solution.py:30
  14.2 15.9 %collective-permute-start.2 = (f32[1,6,128,128]{3,2,1,0:T(8,128)S(1)}, f32[1,6,128,128]{3,2,1,0:T(8,128)S(1)}, u32[]{:S(2)}, u32[]{:S(2)}) collective-permute-start(f32[1,6,128,128]{3,2,1,0:T(8,128)S(1)} %collective-permute-done.x0), channel_id=1, source_target_pairs={{0,2},{1,31},{2,4},{3,1},{4,6},{5,3},{6,8},{7,5},{8,10},{9,7},{10,... | collective-permute-start | bytes 1179656 | tf_op jit(solution)/shard_map/ppermute | solution.py:30
  22.6 8.5 %collective-permute-start.3 = (f32[1,6,128,128]{3,2,1,0:T(8,128)S(1)}, f32[1,6,128,128]{3,2,1,0:T(8,128)}, u32[]{:S(2)}, u32[]{:S(2)}) collective-permute-start(f32[1,6,128,128]{3,2,1,0:T(8,128)S(1)} %collective-permute-done.1.x1), channel_id=1, source_target_pairs={{0,2},{1,31},{2,4},{3,1},{4,6},{5,3},{6,8},{7,5},{8,10},{9,7},{10,... | collective-permute-start | bytes 1179656 | tf_op jit(solution)/shard_map/ppermute | solution.py:30
  31.1 1.1 %copy-start.1 = (f32[2,6,128,128]{3,2,1,0:T(8,128)S(1)}, f32[2,6,128,128]{3,2,1,0:T(8,128)}, u32[]{:S(2)}) copy-start(f32[2,6,128,128]{3,2,1,0:T(8,128)} %z.9) | copy-start | bytes 2359300
  32.2 1.1 %copy-start.3 = (f32[2,6,128,128]{3,2,1,0:T(8,128)S(1)}, f32[2,6,128,128]{3,2,1,0:T(8,128)}, u32[]{:S(2)}) copy-start(f32[2,6,128,128]{3,2,1,0:T(8,128)} %s.1) | copy-start | bytes 2359300
  37.3 9.9 %collective-permute-start.9 = (f32[1,6,128,128]{3,2,1,0:T(8,128)S(1)}, f32[1,6,128,128]{3,2,1,0:T(8,128)S(1)}, u32[]{:S(2)}, u32[]{:S(2)}) collective-permute-start(f32[1,6,128,128]{3,2,1,0:T(8,128)S(1)} %get-tuple-element.35), channel_id=1, source_target_pairs={{0,1},{1,0},{2,3},{3,2},{4,5},{5,4},{6,7},{7,6},{8,9},{9,8},{10,11... | collective-permute-start | bytes 1179656 | tf_op jit(solution)/shard_map/ppermute | solution.py:30
  39.7 15.6 %collective-permute-start.6 = (f32[7,128,128]{2,1,0:T(8,128)S(1)}, f32[7,128,128]{2,1,0:T(8,128)S(1)}, u32[]{:S(2)}, u32[]{:S(2)}) collective-permute-start(f32[7,128,128]{2,1,0:T(8,128)S(1)} %get-tuple-element.33), channel_id=1, source_target_pairs={{0,2},{1,3},{2,0},{3,1},{4,6},{5,7},{6,4},{7,5},{8,10},{9,11},{10,... | collective-permute-start | bytes 1376264 | tf_op jit(solution)/shard_map/ppermute | solution.py:30
  41.0 26.9 %collective-permute-start.7 = (f32[7,128,128]{2,1,0:T(8,128)S(1)}, f32[7,128,128]{2,1,0:T(8,128)S(1)}, u32[]{:S(2)}, u32[]{:S(2)}) collective-permute-start(f32[7,128,128]{2,1,0:T(8,128)S(1)} %get-tuple-element.34), channel_id=1, source_target_pairs={{0,30},{1,31},{2,4},{3,5},{4,2},{5,3},{6,8},{7,9},{8,6},{9,7},{10,... | collective-permute-start | bytes 1376264 | tf_op jit(solution)/shard_map/ppermute | solution.py:30
  43.5 28.9 %collective-permute-start.10 = (f32[1,6,128,128]{3,2,1,0:T(8,128)S(1)}, f32[1,6,128,128]{3,2,1,0:T(8,128)S(1)}, u32[]{:S(2)}, u32[]{:S(2)}) collective-permute-start(f32[1,6,128,128]{3,2,1,0:T(8,128)S(1)} %shard_map.62.nearer), channel_id=1, source_target_pairs={{0,2},{1,31},{2,4},{3,1},{4,6},{5,3},{6,8},{7,5},{8,10},{9,7},{10,... | collective-permute-start | bytes 1179656 | tf_op jit(solution)/shard_map/ppermute | solution.py:30
  47.2 25.3 %collective-permute-start.11 = (f32[1,6,128,128]{3,2,1,0:T(8,128)S(1)}, f32[1,6,128,128]{3,2,1,0:T(8,128)S(1)}, u32[]{:S(2)}, u32[]{:S(2)}) collective-permute-start(f32[1,6,128,128]{3,2,1,0:T(8,128)S(1)} %collective-permute-done.9.farther), channel_id=1, source_target_pairs={{0,2},{1,31},{2,4},{3,1},{4,6},{5,3},{6,8},{7,5},{8,10},{9,7},{10,... | collective-permute-start | bytes 1179656 | tf_op jit(solution)/shard_map/ppermute | solution.py:30
  53.7 18.7 %collective-permute-start.12 = (f32[256,256]{1,0:T(8,128)S(1)}, f32[256,256]{1,0:T(8,128)S(1)}, u32[]{:S(2)}, u32[]{:S(2)}) collective-permute-start(f32[256,256]{1,0:T(8,128)S(1)} %get-tuple-element.38), channel_id=1, source_target_pairs={{0,4},{1,3},{2,6},{3,5},{4,8},{5,7},{6,10},{7,9},{8,12},{9,11},{10... | collective-permute-start | bytes 786440 | tf_op jit(solution)/shard_map/ppermute | solution.py:30
  55.3 17.1 %collective-permute-start.13 = (f32[256,256]{1,0:T(8,128)S(1)}, f32[256,256]{1,0:T(8,128)S(1)}, u32[]{:S(2)}, u32[]{:S(2)}) collective-permute-start(f32[256,256]{1,0:T(8,128)S(1)} %get-tuple-element.39), channel_id=1, source_target_pairs={{0,30},{1,29},{2,0},{3,31},{4,2},{5,1},{6,4},{7,3},{8,6},{9,5},{10... | collective-permute-start | bytes 786440 | tf_op jit(solution)/shard_map/ppermute | solution.py:30
  67.9 4.5 %copy-start.2 = (f32[2,6,128,128]{3,2,1,0:T(8,128)S(1)}, f32[2,6,128,128]{3,2,1,0:T(8,128)}, u32[]{:S(2)}) copy-start(f32[2,6,128,128]{3,2,1,0:T(8,128)} %z.9) | copy-start | bytes 2359300

commit v5 on v4

--- a/solution.py
+++ b/solution.py
@@ -46,12 +46,12 @@
     return i + 2 if i % 2 == 0 else i - 2
 
 
-def far_up(i):
-    return i + 4 if i % 2 == 0 else i + 2
-
-
-def far_down(i):
-    return i - 2 if i % 2 == 0 else i - 4
+def far_first(i):
+    return i + (1, 1, -2, -4)[i % 4]
+
+
+def far_second(i):
+    return i + (4, 2, -1, -1)[i % 4]
 
 
 def split(value):
@@ -155,10 +155,13 @@
 
 
 def both(layouts, tile_of, rows, chip, link):
-    for j, (first, second) in enumerate(zip(*layouts)):
-        a, b = tile_of(*first), tile_of(*second)
-        chip[j] = jnp.where(rows.even_pair, a, b)
-        link[j] = jnp.where(rows.even_pair, b, a)
+    for even, outs in ((True, (chip, link)), (False, (link, chip))):
+
+        @pl.when(rows.even_pair == even)
+        def _():
+            for out, layout in zip(outs, layouts):
+                for j, place in enumerate(layout):
+                    out[j] = tile_of(*place)
 
 
 def pack_kernel(meta, z, z0, z1, chip, link):
@@ -166,6 +169,14 @@
         for slot in range(2 * REACH):
             out[0, slot] = z[r, slot]
     both((Z_UP, Z_DOWN), lambda i, slot: z[i, slot], Rows(meta), chip, link)
+
+
+def hold_kernel(meta, s, s0, s1, nearer):
+    for slot in range(2 * REACH):
+        a, b = s[0, slot], s[1, slot]
+        s0[0, slot] = a
+        s1[0, slot] = b
+        nearer[0, slot] = jnp.where(meta[WIDE] == 0, b, a)
 
 
 def far_tile(rows, refs, sign, r, c, tile):
@@ -186,21 +197,40 @@
     return jnp.where(present, value, 0.0)
 
 
-def far_kernel(meta, t_up, t_down, nearer, farther, up, down, high, low):
+def far_kernel(meta, t_up, t_down, t_far_up, t_far_down, pi, pc, nearer, farther, first, second, high, low):
     tile = nearer.shape[-1]
     rows = Rows(meta)
-    for turned, sign, out in ((t_up, 1, up), (t_down, -1, down)):
-        c0 = 0 if sign > 0 else 2
+
+    def block(turned, place, out, tile_of):
         for r in range(2):
             for c in range(2):
-                put(high, low, r, c0 + c, tile, far_tile(rows, (nearer, farther), sign, r, c, tile))
-        n = slice(c0 * tile, (c0 + 2) * tile)
-        out[...] = dot3(*halves(turned, 0, 1, tile), flat(high, slice(0, 2), n), flat(low, slice(0, 2), n))
-
-
-def product_kernel(meta, s, z, x0, x1, n0, n1, zi, zc, p0, p1, pf, chip, link, z_high, z_low, s_high, s_low, dense):
-    tile = s.shape[-1]
+                put(high, low, r, c, tile, tile_of(r, c))
+        out[...] = dot3(*halves(turned, place, place + 1, tile), flat(high, slice(None), slice(None)), flat(low, slice(None), slice(None)))
+
+    def swapped(sign):
+        return lambda r, c: far_tile(rows, (nearer, farther), sign, r, c, tile)
+
+    def from_down(r, c):
+        return rows.packed((pc, pi), UP, -4, r, c - 1) if c - 1 - (r - 4) <= REACH else zero(tile)
+
+    def from_up(r, c):
+        return rows.packed((pi, pc), DOWN, 4, r, c + 1) if r + 4 - (c + 1) <= REACH else zero(tile)
+
+    @pl.when(rows.even_pair)
+    def _():
+        block(t_up, 1, first, from_down)
+        block(t_far_up, 0, second, swapped(1))
+
+    @pl.when(jnp.logical_not(rows.even_pair))
+    def _():
+        block(t_far_down, 0, first, swapped(-1))
+        block(t_down, 0, second, from_up)
+
+
+def product_kernel(meta, s0, s1, z0, z1, x0, x1, n0, n1, zi, zc, p0, p1, pf, chip, link, z_high, z_low, s_high, s_low, dense):
+    tile = z0.shape[-1]
     rows = Rows(meta)
+    s, z = (s0, s1), (z0, z1)
     for c in range(COLS):
         col = c + COL0
         for i in range(OWN):
@@ -224,13 +254,13 @@
     both((UP, DOWN), lambda i, slot: dense[i, rows.dense_slot(i, slot)], rows, chip, link)
 
 
-def side_kernel(meta, s, z, x0, x1, n0, n1, zi, zc, out, z_high, z_low, s_high, s_low, dense):
+def side_kernel(meta, s, z0, z1, x0, x1, n0, n1, zi, zc, out, z_high, z_low, s_high, s_low, dense):
     tile = s.shape[-1]
     rows = Rows(meta)
     width = 2 * REACH + 1
 
     def own():
-        return lambda row, col: rows.own(z, row, col)
+        return lambda row, col: rows.own((z0, z1), row, col)
 
     def swapped(r):
         return lambda row, col: rows.side((x0, x1)[r], 0, r, col)
@@ -280,9 +310,10 @@
         out[0, slot] = dense[REACH if slot == 0 else pos + jnp.where(pos >= REACH, 1, 0)]
 
 
-def turn_kernel(meta, z, x0, x1, n0, n1, zi, zc, t_own, t_up, t_down, t_swap, t_near, t_far_up, t_far_down, z_own):
-    tile = z.shape[-1]
+def turn_kernel(meta, z0, z1, x0, x1, n0, n1, zi, zc, t_own, t_up, t_down, t_swap, t_near, t_far_up, t_far_down, z_own):
+    tile = z0.shape[-1]
     rows = Rows(meta)
+    z = (z0, z1)
 
     def store(out, c, r, value):
         high, low = split(value.T)
@@ -365,10 +396,12 @@
 
 
 def refine_kernel(
-    meta, z, z_own, t_near, early, nearer, farther, far_up, far_down, refined, correction, high, low, late, d_high, d_low, dense, z_high, z_low,
+    meta, z0, z1, z_own, t_near, early, nearer, farther, first, second, refined, correction, high, low, late, d_high, d_low, dense, z_high, z_low,
 ):
-    tile = z.shape[-1]
+    tile = z0.shape[-1]
     rows = Rows(meta)
+    z = (z0, z1)
+    ends = rows.parity != jnp.where(rows.even_pair, 0, 1)
 
     def add(a, b, value):
         late[SIDE * a + b] = value
@@ -387,7 +420,8 @@
             there = (ia >= 0) & (ia < SIDE) & (ib >= 0) & (ib < SIDE)
             gram = gram + jnp.where(there, late[jnp.clip(SIDE * ia + ib, 0, SIDE * SIDE - 1)], 0.0)
             if a == b and a in (0, PAIRS - 1):
-                gram = gram + (far_up if a == 0 else far_down)[...]
+                one, other = (first, second) if a == 0 else (second, first)
+                gram = gram + jnp.where(ends, one[...], other[...])
             for i in range(2):
                 for j in range(2):
                     k, c = 2 * a + i, 2 * b + j
@@ -410,7 +444,7 @@
     row_matmul(z_high, z_low, d_high, d_low, dense, tile)
     for i in range(OWN):
         for slot in range(2 * REACH):
-            refined[i, slot] = z[i, slot] + 0.5 * dense[i, rows.dense_slot(i, slot)]
+            refined[i, slot] = z[i][0, slot] + 0.5 * dense[i, rows.dense_slot(i, slot)]
 
 
 def body(correlation, factor, pattern):
@@ -449,17 +483,18 @@
     seven = shape(len(UP), tile, tile)
     nine = shape(len(Z_UP), tile, tile)
     block = shape(2 * tile, 2 * tile)
-    parity = device % 2
     dense = pltpu.VMEM((OWN, COLS, tile, tile), F32)
 
     z0, z1, zi, zc = call(pack_kernel, (place, factor), (row, row, nine, nine), [], 1000)
     x = [send(v, swap) for v in (z0, z1)]
     zi, zc = send(zi, inside), send(zc, across)
     n = [send(x[r], near) for r in range(OWN)]
-    sx = send(lax.dynamic_slice_in_dim(correlation, 1 - parity, 1, 0), swap)
+    s0, s1, near_row = call(hold_kernel, (place, correlation), (row, row, row), [], 1000)
+    sx = send(near_row, swap)
+    own = (z0, z1)
     p0, p1, pf, pi, pc = call(
         product_kernel,
-        (meta, correlation, factor, *x, *n, zi, zc),
+        (meta, s0, s1, *own, *x, *n, zi, zc),
         (row, row, row, seven, seven),
         halves_of(COLS, COLS) + halves_of(OWN, COLS) + [dense],
         int(2e9),
@@ -470,7 +505,7 @@
     width = 2 * REACH + 1
     ps = call(
         side_kernel,
-        (meta, sx, factor, *x, *n, zi, zc),
+        (meta, sx, *own, *x, *n, zi, zc),
         row,
         halves_of(width, width) + halves_of(1, width) + [pltpu.VMEM((width, tile, tile), F32)],
         int(2e9),
@@ -482,14 +517,20 @@
 
     t_own, t_up, t_down, t_swap, t_near, t_far_up, t_far_down, z_own = call(
         turn_kernel,
-        (meta, factor, *x, *n, zi, zc),
+        (meta, *own, *x, *n, zi, zc),
         (turned(COLS), turned(4), turned(4), turned(2 * SIDE), turned(2 * SIDE), turned(2), turned(2),
          shape(OWN, tile, 2 * COLS * tile, dtype=BF16)),
         [],
         int(2e9),
     )
-    gu, gd = call(far_kernel, (meta, t_far_up, t_far_down, ps, px), (block, block), halves_of(2, 4), int(1e8))
-    gu, gd = send(gu, far_up), send(gd, far_down)
+    far = call(
+        far_kernel,
+        (meta, t_up, t_down, t_far_up, t_far_down, pi, pc, ps, px),
+        (block, block),
+        halves_of(2, 2),
+        int(1e8),
+    )
+    far = (send(far[0], far_first), send(far[1], far_second))
     early = call(
         gram_kernel,
         (meta, t_own, t_up, t_down, t_swap, p0, p1, pi, pc, ps, px),
@@ -499,7 +540,7 @@
     )
     return call(
         refine_kernel,
-        (meta, factor, z_own, t_near, early, *pn, gu, gd),
+        (meta, *own, z_own, t_near, early, *pn, *far),
         (shape(*factor.shape), shape(*factor.shape)),
         halves_of(2, 2 * SIDE)
         + [pltpu.VMEM((SIDE * SIDE, 2 * tile, 2 * tile), F32)]

time: 79.1 us -> 78.4 us (level)
  waiting for transfers between devices: 23.4 us -> 19.6 us
  Pallas kernels: 21.5 us -> 22.9 us
  starting transfers between devices: 23.9 us -> 24.8 us
    ppermute x14, waiting for transfers between devices: 23.4 us -> 19.6 us  [send(): return lax.ppermute(value, AXES, [(i, to(i) % count) for i in range(count)])]
    unnamed x9 -> x13, local copies, waits for them, and re-layouts: 4.79 us -> 7.13 us
    dynamic_slice x1 -> x0, local copies, waits for them, and re-layouts: 1.77 us -> none  [body(): sx = send(lax.dynamic_slice_in_dim(correlation, 1 - parity, 1, 0), swap)]
    pallas_call x7 -> x8, Pallas kernels: 21.5 us -> 22.9 us  [call(): pl.pallas_call(kernel, in_specs=[smem] * scalars + [vmem] * (len(ins) - s...]
    ppermute x14, starting transfers between devices: 23.9 us -> 24.8 us  [send(): return lax.ppermute(value, AXES, [(i, to(i) % count) for i in range(count)])]
  transfers between devices with their start and end apart: 14 -> 14, of which waited for: 5 -> 6; matrix products, arithmetic and copies ran while one was open for 7% -> 5% of each run, Pallas kernels for 18% -> 21%
where the time goes in v5:
time: 78.4 us; the launch traced here: 77.5 us
  starting transfers between devices  24.8 us (32%)
  Pallas kernels  22.9 us (29%)
  waiting for transfers between devices  19.6 us (25%)
  local copies, waits for them, and re-layouts  8.54 us (11%)
  other arithmetic  0.96 us (1%)
  between operations  0.79 us (1%)
    ppermute x14, starting transfers between devices, send(): return lax.ppermute(value, AXES, [(i, to(i) % count) for i in range(count)])  24.8 us
    pallas_call x8, Pallas kernels, call(): pl.pallas_call(kernel, in_specs=[smem] * scalars + [vmem] * (len(ins) - s...  22.9 us
    ppermute x14, waiting for transfers between devices, send(): return lax.ppermute(value, AXES, [(i, to(i) % count) for i in range(count)])  19.6 us
    unnamed x13, local copies, waits for them, and re-layouts  7.13 us
  transfers between devices with their start and end apart: 14, of which 6 were waited for; matrix products, arithmetic and copies ran while one was open for 5% of the time, Pallas kernels for 21%

profile of v5, /device:TPU:1, one launch (start us, length us, event | category | flops | bytes accessed | tf_op | source)
XLA Modules:
  0.0 77.5 jit_solution(12054119448997311148)
XLA Ops:
  0.7 0.1 stack.2.meta
  0.8 0.0 copy-start
  0.8 1.1 %copy-done = f32[2,6,128,128]{3,2,1,0:T(8,128)S(1)} copy-done((f32[2,6,128,128]{3,2,1,0:T(8,128)S(1)}, f32[2,6,128,128]{3,2,1,0:T(8,128)}, u32[]{:S(2)}) %copy-start) | copy-done | bytes 786456
  1.9 0.7 shard_map.59
  2.6 2.1 %collective-permute-start = (f32[1,6,128,128]{3,2,1,0:T(8,128)S(1)}, f32[1,6,128,128]{3,2,1,0:T(8,128)S(1)}, u32[]{:S(2)}, u32[]{:S(2)}) collective-permute-start(f32[1,6,128,128]{3,2,1,0:T(8,128)S(1)} %get-tuple-element.24.z0), channel_id=1, source_target_pairs={{0,1},{1,0},{2,3},{3,2},{4,5},{5,4},{6,7},{7,6},{8,9},{9,8},{10,11... | collective-permute-start | bytes 1179656 | tf_op jit(solution)/shard_map/ppermute | solution.py:30
  4.7 0.1 collective-permute-start.1
  4.8 1.0 %collective-permute-start.4 = (f32[9,128,128]{2,1,0:T(8,128)S(1)}, f32[9,128,128]{2,1,0:T(8,128)S(1)}, u32[]{:S(2)}, u32[]{:S(2)}) collective-permute-start(f32[9,128,128]{2,1,0:T(8,128)S(1)} %get-tuple-element.26), channel_id=1, source_target_pairs={{0,2},{1,3},{2,0},{3,1},{4,6},{5,7},{6,4},{7,5},{8,10},{9,11},{10,... | collective-permute-start | bytes 1769480 | tf_op jit(solution)/shard_map/ppermute | solution.py:30
  5.7 1.6 %collective-permute-start.5 = (f32[9,128,128]{2,1,0:T(8,128)S(1)}, f32[9,128,128]{2,1,0:T(8,128)S(1)}, u32[]{:S(2)}, u32[]{:S(2)}) collective-permute-start(f32[9,128,128]{2,1,0:T(8,128)S(1)} %get-tuple-element.27), channel_id=1, source_target_pairs={{0,30},{1,31},{2,4},{3,5},{4,2},{5,3},{6,8},{7,9},{8,6},{9,7},{10,... | collective-permute-start | bytes 1769480 | tf_op jit(solution)/shard_map/ppermute | solution.py:30
  7.3 1.1 %copy-done.1 = f32[2,6,128,128]{3,2,1,0:T(8,128)S(1)} copy-done((f32[2,6,128,128]{3,2,1,0:T(8,128)S(1)}, f32[2,6,128,128]{3,2,1,0:T(8,128)}, u32[]{:S(2)}) %copy-start.1) | copy-done | bytes 786456
  8.4 1.4 %shard_map.61 = (f32[1,6,128,128]{3,2,1,0:T(8,128)S(1)}, f32[1,6,128,128]{3,2,1,0:T(8,128)S(1)}, f32[1,6,128,128]{3,2,1,0:T(8,128)}) custom-call(s32[16]{0:T(128)S(1)} %stack.2.meta, f32[2,6,128,128]{3,2,1,0:T(8,128)S(1)} %copy-done.1), custom_call_target="tpu_custom_call" | custom-call | flops 1000 | bytes 4194304 | tf_op jit(solution)/shard_map/pallas_call | solution.py:466
  9.8 0.7 copy-done.2
  10.6 0.7 copy-done.4
  11.3 1.2 %collective-permute-start.8 = (f32[1,6,128,128]{3,2,1,0:T(8,128)}, f32[1,6,128,128]{3,2,1,0:T(8,128)}, u32[]{:S(2)}, u32[]{:S(2)}) collective-permute-start(f32[1,6,128,128]{3,2,1,0:T(8,128)} %get-tuple-element.40), channel_id=1, source_target_pairs={{0,1},{1,0},{2,3},{3,2},{4,5},{5,4},{6,7},{7,6},{8,9},{9,8},{10,11... | collective-permute-start | bytes 1179656 | tf_op jit(solution)/shard_map/ppermute | solution.py:30
  12.5 1.0 %collective-permute-done.x0 = f32[1,6,128,128]{3,2,1,0:T(8,128)S(1)} collective-permute-done((f32[1,6,128,128]{3,2,1,0:T(8,128)S(1)}, f32[1,6,128,128]{3,2,1,0:T(8,128)S(1)}, u32[]{:S(2)}, u32[]{:S(2)}) %collective-permute-start) | collective-permute-done | bytes 393248 | tf_op jit(solution)/shard_map/ppermute | solution.py:30
  13.5 3.8 %collective-permute-start.2 = (f32[1,6,128,128]{3,2,1,0:T(8,128)S(1)}, f32[1,6,128,128]{3,2,1,0:T(8,128)}, u32[]{:S(2)}, u32[]{:S(2)}) collective-permute-start(f32[1,6,128,128]{3,2,1,0:T(8,128)S(1)} %collective-permute-done.x0), channel_id=1, source_target_pairs={{0,2},{1,31},{2,4},{3,1},{4,6},{5,3},{6,8},{7,5},{8,10},{9,7},{10,... | collective-permute-start | bytes 1179656 | tf_op jit(solution)/shard_map/ppermute | solution.py:30
  17.3 4.8 %collective-permute-done.1.x1 = f32[1,6,128,128]{3,2,1,0:T(8,128)} collective-permute-done((f32[1,6,128,128]{3,2,1,0:T(8,128)S(1)}, f32[1,6,128,128]{3,2,1,0:T(8,128)}, u32[]{:S(2)}, u32[]{:S(2)}) %collective-permute-start.1) | collective-permute-done | bytes 393248 | tf_op jit(solution)/shard_map/ppermute | solution.py:30
  22.0 3.8 %collective-permute-start.3 = (f32[1,6,128,128]{3,2,1,0:T(8,128)}, f32[1,6,128,128]{3,2,1,0:T(8,128)}, u32[]{:S(2)}, u32[]{:S(2)}) collective-permute-start(f32[1,6,128,128]{3,2,1,0:T(8,128)} %collective-permute-done.1.x1), channel_id=1, source_target_pairs={{0,2},{1,31},{2,4},{3,1},{4,6},{5,3},{6,8},{7,5},{8,10},{9,7},{10,... | collective-permute-start | bytes 1179656 | tf_op jit(solution)/shard_map/ppermute | solution.py:30
  25.8 1.4 %copy.6 = s32[64,6]{1,0:T(8,128)} copy(s32[64,6]{0,1:T(8,128)} %param.6) | data formatting | bytes 3072 | tf_op args[2]
  27.2 1.3 %gather_fusion = s32[14,6]{1,0:T(8,128)S(1)} fusion(s32[64,6]{1,0:T(8,128)} %copy.6, s32[1024]{0:T(1024)S(1)} %pad_clamp_fusion), kind=kCustom, calls=%fused_computation | custom fusion | bytes 728 | tf_op jit(solution)/shard_map/gather | solution.py:456
  28.5 0.8 %convert_reduce_fusion = s32[14]{0:T(128)S(1)} fusion(s32[14,6]{1,0:T(8,128)S(1)} %gather_fusion, s32[5]{0:T(128)} %constant.78.clone, s32[14]{0:T(128)S(1)} %and_select_fusion), kind=kLoop, calls=%fused_computation.9 | loop fusion | flops 1176 | bytes 412 | tf_op jit(solution)/shard_map/reduce_sum | solution.py:458
  29.4 0.1 pad_add_fusion.meta
  29.5 0.0 collective-permute-done.4.zi
  29.5 0.0 collective-permute-done.5.zc
  29.5 0.0 collective-permute-done.2.n0
  29.5 1.4 %collective-permute-done.3.n1 = f32[1,6,128,128]{3,2,1,0:T(8,128)} collective-permute-done((f32[1,6,128,128]{3,2,1,0:T(8,128)}, f32[1,6,128,128]{3,2,1,0:T(8,128)}, u32[]{:S(2)}, u32[]{:S(2)}) %collective-permute-start.3) | collective-permute-done | bytes 393248 | tf_op jit(solution)/shard_map/ppermute | solution.py:30
  30.8 1.0 %copy-done.3 = f32[1,6,128,128]{3,2,1,0:T(8,128)S(1)} copy-done((f32[1,6,128,128]{3,2,1,0:T(8,128)S(1)}, f32[1,6,128,128]{3,2,1,0:T(8,128)}, u32[]{:S(2)}) %copy-start.3) | copy-done | bytes 393240
  31.8 1.0 %copy-done.5 = f32[1,6,128,128]{3,2,1,0:T(8,128)S(1)} copy-done((f32[1,6,128,128]{3,2,1,0:T(8,128)S(1)}, f32[1,6,128,128]{3,2,1,0:T(8,128)}, u32[]{:S(2)}) %copy-start.5) | copy-done | bytes 393240
  32.8 4.2 %shard_map.62 = (f32[1,6,128,128]{3,2,1,0:T(8,128)S(1)}, f32[1,6,128,128]{3,2,1,0:T(8,128)S(1)}, f32[1,6,128,128]{3,2,1,0:T(8,128)S(1)}, f32[7,128,128]{2,1,0:T(8,128)S(1)}, f32[7,128,128]{2,1,0:T(8,128)S(1)}) custom-call(s32[16]{0:T(128)S(1)} %pad_add_fusion.meta, f32[1,6,128,128]{3,2,1,0:T(8,128)S(1)} %copy-done.3, f32[1,6,128,128]{3,2,1,0:T(8,128)S(1)} %copy-done.5, ...), custom_call_target="tpu_custom_call" | custom-call | flops 2000000000 | bytes 4194304 | tf_op jit(solution)/shard_map/pallas_call | solution.py:466
  37.0 2.0 %collective-permute-start.9 = (f32[1,6,128,128]{3,2,1,0:T(8,128)S(1)}, f32[1,6,128,128]{3,2,1,0:T(8,128)S(1)}, u32[]{:S(2)}, u32[]{:S(2)}) collective-permute-start(f32[1,6,128,128]{3,2,1,0:T(8,128)S(1)} %get-tuple-element.41), channel_id=1, source_target_pairs={{0,1},{1,0},{2,3},{3,2},{4,5},{5,4},{6,7},{7,6},{8,9},{9,8},{10,11... | collective-permute-start | bytes 1179656 | tf_op jit(solution)/shard_map/ppermute | solution.py:30
  39.0 1.7 %collective-permute-start.6 = (f32[7,128,128]{2,1,0:T(8,128)S(1)}, f32[7,128,128]{2,1,0:T(8,128)S(1)}, u32[]{:S(2)}, u32[]{:S(2)}) collective-permute-start(f32[7,128,128]{2,1,0:T(8,128)S(1)} %get-tuple-element.38), channel_id=1, source_target_pairs={{0,2},{1,3},{2,0},{3,1},{4,6},{5,7},{6,4},{7,5},{8,10},{9,11},{10,... | collective-permute-start | bytes 1376264 | tf_op jit(solution)/shard_map/ppermute | solution.py:30
  40.7 0.0 collective-permute-start.7
  40.7 0.0 collective-permute-done.8.s
  40.7 2.7 %shard_map.63.nearer = f32[1,6,128,128]{3,2,1,0:T(8,128)S(1)} custom-call(s32[16]{0:T(128)S(1)} %pad_add_fusion.meta, f32[1,6,128,128]{3,2,1,0:T(8,128)} %collective-permute-done.8.s, f32[1,6,128,128]{3,2,1,0:T(8,128)S(1)} %get-tuple-element.24.z0, f32[1,6,128,128]{3,2,1,0:T(8,128)S(1)} %get-tuple-element.25.z1, ...), custom_call_target="tpu_custom_call" | custom-call | flops 2000000000 | bytes 4194304 | tf_op jit(solution)/shard_map/pallas_call | solution.py:466
  43.3 1.8 %collective-permute-start.10 = (f32[1,6,128,128]{3,2,1,0:T(8,128)S(1)}, f32[1,6,128,128]{3,2,1,0:T(8,128)S(1)}, u32[]{:S(2)}, u32[]{:S(2)}) collective-permute-start(f32[1,6,128,128]{3,2,1,0:T(8,128)S(1)} %shard_map.63.nearer), channel_id=1, source_target_pairs={{0,2},{1,31},{2,4},{3,1},{4,6},{5,3},{6,8},{7,5},{8,10},{9,7},{10,... | collective-permute-start | bytes 1179656 | tf_op jit(solution)/shard_map/ppermute | solution.py:30
  45.2 1.0 %collective-permute-done.9.farther = f32[1,6,128,128]{3,2,1,0:T(8,128)S(1)} collective-permute-done((f32[1,6,128,128]{3,2,1,0:T(8,128)S(1)}, f32[1,6,128,128]{3,2,1,0:T(8,128)S(1)}, u32[]{:S(2)}, u32[]{:S(2)}) %collective-permute-start.9) | collective-permute-done | bytes 393248 | tf_op jit(solution)/shard_map/ppermute | solution.py:30
  46.2 4.0 %collective-permute-start.11 = (f32[1,6,128,128]{3,2,1,0:T(8,128)S(1)}, f32[1,6,128,128]{3,2,1,0:T(8,128)S(1)}, u32[]{:S(2)}, u32[]{:S(2)}) collective-permute-start(f32[1,6,128,128]{3,2,1,0:T(8,128)S(1)} %collective-permute-done.9.farther), channel_id=1, source_target_pairs={{0,2},{1,31},{2,4},{3,1},{4,6},{5,3},{6,8},{7,5},{8,10},{9,7},{10,... | collective-permute-start | bytes 1179656 | tf_op jit(solution)/shard_map/ppermute | solution.py:30
  50.2 2.4 %shard_map.60 = (bf16[1024,512]{1,0:T(8,128)(2,1)S(1)}, bf16[512,512]{1,0:T(8,128)(2,1)S(1)}, bf16[512,512]{1,0:T(8,128)(2,1)S(1)}, bf16[768,512]{1,0:T(8,128)(2...) custom-call(s32[16]{0:T(128)S(1)} %pad_add_fusion.meta, ...), custom_call_target="tpu_custom_call" | custom-call | flops 2000000000 | bytes 4194304 | tf_op jit(solution)/shard_map/pallas_call | solution.py:466
  52.6 0.0 collective-permute-done.6.pi
  52.6 9.3 %collective-permute-done.7.pc = f32[7,128,128]{2,1,0:T(8,128)S(1)} collective-permute-done((f32[7,128,128]{2,1,0:T(8,128)S(1)}, f32[7,128,128]{2,1,0:T(8,128)S(1)}, u32[]{:S(2)}, u32[]{:S(2)}) %collective-permute-start.7) | collective-permute-done | bytes 458784 | tf_op jit(solution)/shard_map/ppermute | solution.py:30
  61.9 1.0 %shard_map.65 = (f32[256,256]{1,0:T(8,128)S(1)}, f32[256,256]{1,0:T(8,128)S(1)}) custom-call(s32[16]{0:T(128)S(1)} %pad_add_fusion.meta, bf16[512,512]{1,0:T(8,128)(2,1)S(1)} %get-tuple-element.31.t_up, bf16[512,512]{1,0:T(8,128)(2,1)S(1)} %get-tuple-element.32.t_down, bf16[256,512]{1,0:T(8,128)(2,1)S(1)} %get-tuple-element.42.t_far_up, ...), custom_call_target="tpu_custom_call" | custom-call | flops 100000000 | bytes 4194304 | tf_op jit(solution)/shard_map/pallas_call | solution.py:466
  62.9 0.1 collective-permute-start.12
  63.0 1.7 %collective-permute-start.13 = (f32[256,256]{1,0:T(8,128)S(1)}, f32[256,256]{1,0:T(8,128)S(1)}, u32[]{:S(2)}, u32[]{:S(2)}) collective-permute-start(f32[256,256]{1,0:T(8,128)S(1)} %get-tuple-element.45), channel_id=1, source_target_pairs={{0,4},{1,3},{2,1},{3,2},{4,8},{5,7},{6,5},{7,6},{8,12},{9,11},{10,... | collective-permute-start | bytes 786440 | tf_op jit(solution)/shard_map/ppermute | solution.py:30
  64.7 4.5 %shard_map.64.early = f32[16,256,256]{2,1,0:T(8,128)S(1)} custom-call(s32[16]{0:T(128)S(1)} %pad_add_fusion.meta, bf16[1024,512]{1,0:T(8,128)(2,1)S(1)} %get-tuple-element.30.t_own, bf16[512,512]{1,0:T(8,128)(2,1)S(1)} %get-tuple-element.31.t_up, bf16[512,512]{1,0:T(8,128)(2,1)S(1)} %get-tuple-element.32.t_down, ...), custom_call_target="tpu_custom_call" | custom-call | flops 4000000000 | bytes 4194304 | tf_op jit(solution)/shard_map/pallas_call | solution.py:466
  69.2 0.0 collective-permute-done.10.nearer
  69.2 2.1 %collective-permute-done.12.first = f32[256,256]{1,0:T(8,128)S(1)} collective-permute-done((f32[256,256]{1,0:T(8,128)S(1)}, f32[256,256]{1,0:T(8,128)S(1)}, u32[]{:S(2)}, u32[]{:S(2)}) %collective-permute-start.12) | collective-permute-done | bytes 262176 | tf_op jit(solution)/shard_map/ppermute | solution.py:30
  71.3 0.0 collective-permute-done.13.second
  71.4 0.0 collective-permute-done.11.farther
  71.4 6.2 %shard_map.66 = (f32[2,6,128,128]{3,2,1,0:T(8,128)}, f32[2,6,128,128]{3,2,1,0:T(8,128)}) custom-call(s32[16]{0:T(128)S(1)} %pad_add_fusion.meta, f32[1,6,128,128]{3,2,1,0:T(8,128)S(1)} %get-tuple-element.24.z0, f32[1,6,128,128]{3,2,1,0:T(8,128)S(1)} %get-tuple-element.25.z1, bf16[2,128,2048]{2,1,0:T(8,128)(2,1)S(1)} %get-tuple-element.28.z_own, ...), custom_call_target="tpu_custom_call" | custom-call | flops 4000000000 | bytes 4194304 | tf_op jit(solution)/shard_map/pallas_call | solution.py:466
  (11 shorter events, 0.0 us)
Async XLA Ops:
  0.8 1.1 %copy-start = (f32[2,6,128,128]{3,2,1,0:T(8,128)S(1)}, f32[2,6,128,128]{3,2,1,0:T(8,128)}, u32[]{:S(2)}) copy-start(f32[2,6,128,128]{3,2,1,0:T(8,128)} %z.1) | copy-start | bytes 2359300
  2.6 10.9 %collective-permute-start = (f32[1,6,128,128]{3,2,1,0:T(8,128)S(1)}, f32[1,6,128,128]{3,2,1,0:T(8,128)S(1)}, u32[]{:S(2)}, u32[]{:S(2)}) collective-permute-start(f32[1,6,128,128]{3,2,1,0:T(8,128)S(1)} %get-tuple-element.24.z0), channel_id=1, source_target_pairs={{0,1},{1,0},{2,3},{3,2},{4,5},{5,4},{6,7},{7,6},{8,9},{9,8},{10,11... | collective-permute-start | bytes 1179656 | tf_op jit(solution)/shard_map/ppermute | solution.py:30
  4.7 17.3 %collective-permute-start.1 = (f32[1,6,128,128]{3,2,1,0:T(8,128)S(1)}, f32[1,6,128,128]{3,2,1,0:T(8,128)}, u32[]{:S(2)}, u32[]{:S(2)}) collective-permute-start(f32[1,6,128,128]{3,2,1,0:T(8,128)S(1)} %get-tuple-element.25.z1), channel_id=1, source_target_pairs={{0,1},{1,0},{2,3},{3,2},{4,5},{5,4},{6,7},{7,6},{8,9},{9,8},{10,11... | collective-permute-start | bytes 1179656 | tf_op jit(solution)/shard_map/ppermute | solution.py:30
  4.8 24.7 %collective-permute-start.4 = (f32[9,128,128]{2,1,0:T(8,128)S(1)}, f32[9,128,128]{2,1,0:T(8,128)S(1)}, u32[]{:S(2)}, u32[]{:S(2)}) collective-permute-start(f32[9,128,128]{2,1,0:T(8,128)S(1)} %get-tuple-element.26), channel_id=1, source_target_pairs={{0,2},{1,3},{2,0},{3,1},{4,6},{5,7},{6,4},{7,5},{8,10},{9,11},{10,... | collective-permute-start | bytes 1769480 | tf_op jit(solution)/shard_map/ppermute | solution.py:30
  5.7 23.7 %collective-permute-start.5 = (f32[9,128,128]{2,1,0:T(8,128)S(1)}, f32[9,128,128]{2,1,0:T(8,128)S(1)}, u32[]{:S(2)}, u32[]{:S(2)}) collective-permute-start(f32[9,128,128]{2,1,0:T(8,128)S(1)} %get-tuple-element.27), channel_id=1, source_target_pairs={{0,30},{1,31},{2,4},{3,5},{4,2},{5,3},{6,8},{7,9},{8,6},{9,7},{10,... | collective-permute-start | bytes 1769480 | tf_op jit(solution)/shard_map/ppermute | solution.py:30
  7.3 1.1 %copy-start.1 = (f32[2,6,128,128]{3,2,1,0:T(8,128)S(1)}, f32[2,6,128,128]{3,2,1,0:T(8,128)}, u32[]{:S(2)}) copy-start(f32[2,6,128,128]{3,2,1,0:T(8,128)} %s.1) | copy-start | bytes 2359300
  9.8 0.7 copy-start.2
  10.6 0.7 copy-start.4
  11.3 29.4 %collective-permute-start.8 = (f32[1,6,128,128]{3,2,1,0:T(8,128)}, f32[1,6,128,128]{3,2,1,0:T(8,128)}, u32[]{:S(2)}, u32[]{:S(2)}) collective-permute-start(f32[1,6,128,128]{3,2,1,0:T(8,128)} %get-tuple-element.40), channel_id=1, source_target_pairs={{0,1},{1,0},{2,3},{3,2},{4,5},{5,4},{6,7},{7,6},{8,9},{9,8},{10,11... | collective-permute-start | bytes 1179656 | tf_op jit(solution)/shard_map/ppermute | solution.py:30
  13.5 16.0 %collective-permute-start.2 = (f32[1,6,128,128]{3,2,1,0:T(8,128)S(1)}, f32[1,6,128,128]{3,2,1,0:T(8,128)}, u32[]{:S(2)}, u32[]{:S(2)}) collective-permute-start(f32[1,6,128,128]{3,2,1,0:T(8,128)S(1)} %collective-permute-done.x0), channel_id=1, source_target_pairs={{0,2},{1,31},{2,4},{3,1},{4,6},{5,3},{6,8},{7,5},{8,10},{9,7},{10,... | collective-permute-start | bytes 1179656 | tf_op jit(solution)/shard_map/ppermute | solution.py:30
  22.0 8.8 %collective-permute-start.3 = (f32[1,6,128,128]{3,2,1,0:T(8,128)}, f32[1,6,128,128]{3,2,1,0:T(8,128)}, u32[]{:S(2)}, u32[]{:S(2)}) collective-permute-start(f32[1,6,128,128]{3,2,1,0:T(8,128)} %collective-permute-done.1.x1), channel_id=1, source_target_pairs={{0,2},{1,31},{2,4},{3,1},{4,6},{5,3},{6,8},{7,5},{8,10},{9,7},{10,... | collective-permute-start | bytes 1179656 | tf_op jit(solution)/shard_map/ppermute | solution.py:30
  30.8 1.0 %copy-start.3 = (f32[1,6,128,128]{3,2,1,0:T(8,128)S(1)}, f32[1,6,128,128]{3,2,1,0:T(8,128)}, u32[]{:S(2)}) copy-start(f32[1,6,128,128]{3,2,1,0:T(8,128)} %copy-done.2) | copy-start | bytes 1179652
  31.8 1.0 %copy-start.5 = (f32[1,6,128,128]{3,2,1,0:T(8,128)S(1)}, f32[1,6,128,128]{3,2,1,0:T(8,128)}, u32[]{:S(2)}) copy-start(f32[1,6,128,128]{3,2,1,0:T(8,128)} %copy-done.4) | copy-start | bytes 1179652
  37.0 9.2 %collective-permute-start.9 = (f32[1,6,128,128]{3,2,1,0:T(8,128)S(1)}, f32[1,6,128,128]{3,2,1,0:T(8,128)S(1)}, u32[]{:S(2)}, u32[]{:S(2)}) collective-permute-start(f32[1,6,128,128]{3,2,1,0:T(8,128)S(1)} %get-tuple-element.41), channel_id=1, source_target_pairs={{0,1},{1,0},{2,3},{3,2},{4,5},{5,4},{6,7},{7,6},{8,9},{9,8},{10,11... | collective-permute-start | bytes 1179656 | tf_op jit(solution)/shard_map/ppermute | solution.py:30
  39.0 13.6 %collective-permute-start.6 = (f32[7,128,128]{2,1,0:T(8,128)S(1)}, f32[7,128,128]{2,1,0:T(8,128)S(1)}, u32[]{:S(2)}, u32[]{:S(2)}) collective-permute-start(f32[7,128,128]{2,1,0:T(8,128)S(1)} %get-tuple-element.38), channel_id=1, source_target_pairs={{0,2},{1,3},{2,0},{3,1},{4,6},{5,7},{6,4},{7,5},{8,10},{9,11},{10,... | collective-permute-start | bytes 1376264 | tf_op jit(solution)/shard_map/ppermute | solution.py:30
  40.7 21.2 %collective-permute-start.7 = (f32[7,128,128]{2,1,0:T(8,128)S(1)}, f32[7,128,128]{2,1,0:T(8,128)S(1)}, u32[]{:S(2)}, u32[]{:S(2)}) collective-permute-start(f32[7,128,128]{2,1,0:T(8,128)S(1)} %get-tuple-element.39), channel_id=1, source_target_pairs={{0,30},{1,31},{2,4},{3,5},{4,2},{5,3},{6,8},{7,9},{8,6},{9,7},{10,... | collective-permute-start | bytes 1376264 | tf_op jit(solution)/shard_map/ppermute | solution.py:30
  43.3 25.9 %collective-permute-start.10 = (f32[1,6,128,128]{3,2,1,0:T(8,128)S(1)}, f32[1,6,128,128]{3,2,1,0:T(8,128)S(1)}, u32[]{:S(2)}, u32[]{:S(2)}) collective-permute-start(f32[1,6,128,128]{3,2,1,0:T(8,128)S(1)} %shard_map.63.nearer), channel_id=1, source_target_pairs={{0,2},{1,31},{2,4},{3,1},{4,6},{5,3},{6,8},{7,5},{8,10},{9,7},{10,... | collective-permute-start | bytes 1179656 | tf_op jit(solution)/shard_map/ppermute | solution.py:30
  46.2 25.2 %collective-permute-start.11 = (f32[1,6,128,128]{3,2,1,0:T(8,128)S(1)}, f32[1,6,128,128]{3,2,1,0:T(8,128)S(1)}, u32[]{:S(2)}, u32[]{:S(2)}) collective-permute-start(f32[1,6,128,128]{3,2,1,0:T(8,128)S(1)} %collective-permute-done.9.farther), channel_id=1, source_target_pairs={{0,2},{1,31},{2,4},{3,1},{4,6},{5,3},{6,8},{7,5},{8,10},{9,7},{10,... | collective-permute-start | bytes 1179656 | tf_op jit(solution)/shard_map/ppermute | solution.py:30
  62.9 8.4 %collective-permute-start.12 = (f32[256,256]{1,0:T(8,128)S(1)}, f32[256,256]{1,0:T(8,128)S(1)}, u32[]{:S(2)}, u32[]{:S(2)}) collective-permute-start(f32[256,256]{1,0:T(8,128)S(1)} %get-tuple-element.44), channel_id=1, source_target_pairs={{0,1},{1,2},{2,0},{3,31},{4,5},{5,6},{6,4},{7,3},{8,9},{9,10},{10,... | collective-permute-start | bytes 786440 | tf_op jit(solution)/shard_map/ppermute | solution.py:30
  63.0 8.3 %collective-permute-start.13 = (f32[256,256]{1,0:T(8,128)S(1)}, f32[256,256]{1,0:T(8,128)S(1)}, u32[]{:S(2)}, u32[]{:S(2)}) collective-permute-start(f32[256,256]{1,0:T(8,128)S(1)} %get-tuple-element.45), channel_id=1, source_target_pairs={{0,4},{1,3},{2,1},{3,2},{4,8},{5,7},{6,5},{7,6},{8,12},{9,11},{10,... | collective-permute-start | bytes 786440 | tf_op jit(solution)/shard_map/ppermute | solution.py:30

commit v6 on v4

--- a/solution.py
+++ b/solution.py
@@ -46,12 +46,12 @@
     return i + 2 if i % 2 == 0 else i - 2
 
 
-def far_up(i):
-    return i + 4 if i % 2 == 0 else i + 2
-
-
-def far_down(i):
-    return i - 2 if i % 2 == 0 else i - 4
+def far_first(i):
+    return i + (1, 1, -2, -4)[i % 4]
+
+
+def far_second(i):
+    return i + (4, 2, -1, -1)[i % 4]
 
 
 def split(value):
@@ -155,10 +155,13 @@
 
 
 def both(layouts, tile_of, rows, chip, link):
-    for j, (first, second) in enumerate(zip(*layouts)):
-        a, b = tile_of(*first), tile_of(*second)
-        chip[j] = jnp.where(rows.even_pair, a, b)
-        link[j] = jnp.where(rows.even_pair, b, a)
+    for even, outs in ((True, (chip, link)), (False, (link, chip))):
+
+        @pl.when(rows.even_pair == even)
+        def _():
+            for out, layout in zip(outs, layouts):
+                for j, place in enumerate(layout):
+                    out[j] = tile_of(*place)
 
 
 def pack_kernel(meta, z, z0, z1, chip, link):
@@ -186,20 +189,48 @@
     return jnp.where(present, value, 0.0)
 
 
-def far_kernel(meta, t_up, t_down, nearer, farther, up, down, high, low):
+def edge_kernel(
+    meta, t_up, t_down, t_far_up, t_far_down, pi, pc, nearer, farther, early, edge, first, second,
+    high, low, far_high, far_low,
+):
     tile = nearer.shape[-1]
     rows = Rows(meta)
-    for turned, sign, out in ((t_up, 1, up), (t_down, -1, down)):
-        c0 = 0 if sign > 0 else 2
+    for r in range(2):
+        for c in range(4):
+            col = c + COL0
+            value = rows.packed((pc, pi), UP, -4, r, col) if abs(col - (r - 4)) <= REACH else zero(tile)
+            put(high, low, r, c, tile, value)
+            col = c + COL0 + 4
+            value = rows.packed((pi, pc), DOWN, 4, r, col) if abs(col - (r + 4)) <= REACH else zero(tile)
+            put(high, low, r, 4 + c, tile, value)
+    for b in range(PAIRS):
+        n = slice(2 * b * tile, (2 * b + 2) * tile)
+        block = dot3(
+            *halves(t_up if b < 2 else t_down, 0, 2, tile), flat(high, slice(None), n), flat(low, slice(None), n)
+        )
+        for e in range(2):
+            edge[2 * b + e] = block[2 * e * tile : (2 * e + 2) * tile]
+
+    def far_block(turned, sign, out):
         for r in range(2):
             for c in range(2):
-                put(high, low, r, c0 + c, tile, far_tile(rows, (nearer, farther), sign, r, c, tile))
-        n = slice(c0 * tile, (c0 + 2) * tile)
-        out[...] = dot3(*halves(turned, 0, 1, tile), flat(high, slice(0, 2), n), flat(low, slice(0, 2), n))
+                put(far_high, far_low, r, c, tile, far_tile(rows, (nearer, farther), sign, r, c, tile))
+        whole = slice(None), slice(None)
+        out[...] = dot3(*halves(turned, 0, 1, tile), flat(far_high, *whole), flat(far_low, *whole))
+
+    @pl.when(rows.even_pair)
+    def _():
+        first[...] = edge[3]
+        far_block(t_far_up, 1, second)
+
+    @pl.when(jnp.logical_not(rows.even_pair))
+    def _():
+        far_block(t_far_down, -1, first)
+        second[...] = edge[4]
 
 
 def product_kernel(meta, s, z, x0, x1, n0, n1, zi, zc, p0, p1, pf, chip, link, z_high, z_low, s_high, s_low, dense):
-    tile = s.shape[-1]
+    tile = z.shape[-1]
     rows = Rows(meta)
     for c in range(COLS):
         col = c + COL0
@@ -280,9 +311,11 @@
         out[0, slot] = dense[REACH if slot == 0 else pos + jnp.where(pos >= REACH, 1, 0)]
 
 
-def turn_kernel(meta, z, x0, x1, n0, n1, zi, zc, t_own, t_up, t_down, t_swap, t_near, t_far_up, t_far_down, z_own):
+def turn_kernel(meta, z, x0, x1, n0, n1, zi, zc, after, z_kept, t_own, t_up, t_down, t_swap, t_near, t_far_up, t_far_down, z_own):
     tile = z.shape[-1]
     rows = Rows(meta)
+
+    z_kept[...] = z[...]
 
     def store(out, c, r, value):
         high, low = split(value.T)
@@ -329,33 +362,19 @@
             add(a, b, block[2 * a * tile : (2 * a + 2) * tile])
 
 
-def gram_kernel(meta, t_own, t_up, t_down, t_swap, p0, p1, pi, pc, nearer, farther, gram, high, low, side_high, side_low):
+def gram_kernel(meta, t_own, t_swap, p0, p1, nearer, farther, gram, high, low, side_high, side_low):
     tile = p0.shape[-1]
     rows = Rows(meta)
     for r in range(2):
         for c in range(COLS):
             col = c + COL0
             put(high, low, r, c, tile, rows.own((p0, p1), r, col) if abs(col - r) <= REACH else zero(tile))
-        for c in range(4):
-            col = c + COL0
-            value = rows.packed((pc, pi), UP, -4, r, col) if abs(col - (r - 4)) <= REACH else zero(tile)
-            put(high, low, 2 + r, c, tile, value)
-            col = c + COL0 + 4
-            value = rows.packed((pi, pc), DOWN, 4, r, col) if abs(col - (r + 4)) <= REACH else zero(tile)
-            put(high, low, 2 + r, 4 + c, tile, value)
     for b in range(PAIRS):
         n = slice(2 * b * tile, (2 * b + 2) * tile)
         first, last = max(0, b - 2), min(PAIRS, b + 3)
         block = dot3(*halves(t_own, first, last, tile), flat(high, slice(0, 2), n), flat(low, slice(0, 2), n))
-        edge = dot3(
-            *halves(t_up if b < 2 else t_down, 0, 2, tile), flat(high, slice(2, 4), n), flat(low, slice(2, 4), n)
-        )
         for a in range(first, last):
-            value = block[2 * (a - first) * tile : 2 * (a - first + 1) * tile]
-            e = a if b < 2 else a - 2
-            if 0 <= e < 2:
-                value = value + edge[2 * e * tile : (2 * e + 2) * tile]
-            gram[PAIRS * a + b] = value
+            gram[PAIRS * a + b] = block[2 * (a - first) * tile : 2 * (a - first + 1) * tile]
 
     def add(a, b, value):
         index = PAIRS * a + b + (PAIRS + 1) * rows.side_pair(0)
@@ -365,10 +384,11 @@
 
 
 def refine_kernel(
-    meta, z, z_own, t_near, early, nearer, farther, far_up, far_down, refined, correction, high, low, late, d_high, d_low, dense, z_high, z_low,
+    meta, z, z_own, t_near, early, edge, nearer, farther, first, second, refined, correction, high, low, late, d_high, d_low, dense, z_high, z_low,
 ):
     tile = z.shape[-1]
     rows = Rows(meta)
+    ends = rows.parity != jnp.where(rows.even_pair, 0, 1)
 
     def add(a, b, value):
         late[SIDE * a + b] = value
@@ -386,8 +406,12 @@
             ia, ib = a - shift, b - shift
             there = (ia >= 0) & (ia < SIDE) & (ib >= 0) & (ib < SIDE)
             gram = gram + jnp.where(there, late[jnp.clip(SIDE * ia + ib, 0, SIDE * SIDE - 1)], 0.0)
+            e = a if b < 2 else a - 2
+            if 0 <= e < 2:
+                gram = gram + edge[2 * b + e]
             if a == b and a in (0, PAIRS - 1):
-                gram = gram + (far_up if a == 0 else far_down)[...]
+                one, other = (first, second) if a == 0 else (second, first)
+                gram = gram + jnp.where(ends, one[...], other[...])
             for i in range(2):
                 for j in range(2):
                     k, c = 2 * a + i, 2 * b + j
@@ -428,6 +452,11 @@
     vmem = pl.BlockSpec(memory_space=pltpu.VMEM)
     smem = pl.BlockSpec(memory_space=pltpu.SMEM)
 
+    def resident(value):
+        if value is factor or value is correlation:
+            return pltpu.with_memory_space_constraint(value, pltpu.HBM)
+        return pltpu.with_memory_space_constraint(value, pltpu.VMEM)
+
     def call(kernel, ins, outs, scratch, flops, scalars=1):
         return pl.pallas_call(
             kernel,
@@ -437,7 +466,7 @@
             scratch_shapes=scratch,
             compiler_params=pltpu.CompilerParams(vmem_limit_bytes=VMEM_LIMIT),
             cost_estimate=pl.CostEstimate(flops=flops, bytes_accessed=4 << 20, transcendentals=0),
-        )(*ins[:scalars], *(pltpu.with_memory_space_constraint(v, pltpu.VMEM) for v in ins[scalars:]))
+        )(*ins[:scalars], *map(resident, ins[scalars:]))
 
     def shape(*dims, dtype=F32):
         return jax.ShapeDtypeStruct(dims, dtype)
@@ -449,14 +478,13 @@
     seven = shape(len(UP), tile, tile)
     nine = shape(len(Z_UP), tile, tile)
     block = shape(2 * tile, 2 * tile)
-    parity = device % 2
     dense = pltpu.VMEM((OWN, COLS, tile, tile), F32)
 
     z0, z1, zi, zc = call(pack_kernel, (place, factor), (row, row, nine, nine), [], 1000)
     x = [send(v, swap) for v in (z0, z1)]
     zi, zc = send(zi, inside), send(zc, across)
     n = [send(x[r], near) for r in range(OWN)]
-    sx = send(lax.dynamic_slice_in_dim(correlation, 1 - parity, 1, 0), swap)
+    sx = send(lax.dynamic_slice_in_dim(correlation, 1 - device % 2, 1, 0), swap)
     p0, p1, pf, pi, pc = call(
         product_kernel,
         (meta, correlation, factor, *x, *n, zi, zc),
@@ -480,26 +508,32 @@
     def turned(columns):
         return shape(columns * tile, 4 * tile, dtype=BF16)
 
-    t_own, t_up, t_down, t_swap, t_near, t_far_up, t_far_down, z_own = call(
+    z_kept, t_own, t_up, t_down, t_swap, t_near, t_far_up, t_far_down, z_own = call(
         turn_kernel,
-        (meta, factor, *x, *n, zi, zc),
-        (turned(COLS), turned(4), turned(4), turned(2 * SIDE), turned(2 * SIDE), turned(2), turned(2),
+        (meta, factor, *x, *n, zi, zc, ps),
+        (shape(*factor.shape), turned(COLS), turned(4), turned(4), turned(2 * SIDE), turned(2 * SIDE), turned(2), turned(2),
          shape(OWN, tile, 2 * COLS * tile, dtype=BF16)),
         [],
         int(2e9),
     )
-    gu, gd = call(far_kernel, (meta, t_far_up, t_far_down, ps, px), (block, block), halves_of(2, 4), int(1e8))
-    gu, gd = send(gu, far_up), send(gd, far_down)
     early = call(
         gram_kernel,
-        (meta, t_own, t_up, t_down, t_swap, p0, p1, pi, pc, ps, px),
+        (meta, t_own, t_swap, p0, p1, ps, px),
         shape(PAIRS * PAIRS, 2 * tile, 2 * tile),
-        halves_of(4, COLS) + halves_of(2, 2 * SIDE),
+        halves_of(2, COLS) + halves_of(2, 2 * SIDE),
         int(4e9),
     )
+    edge, *far = call(
+        edge_kernel,
+        (meta, t_up, t_down, t_far_up, t_far_down, pi, pc, ps, px, early),
+        (shape(2 * PAIRS, 2 * tile, 2 * tile), block, block),
+        halves_of(2, COLS) + halves_of(2, 2),
+        int(1e9),
+    )
+    far = (send(far[0], far_first), send(far[1], far_second))
     return call(
         refine_kernel,
-        (meta, factor, z_own, t_near, early, *pn, gu, gd),
+        (meta, z_kept, z_own, t_near, early, edge, *pn, *far),
         (shape(*factor.shape), shape(*factor.shape)),
         halves_of(2, 2 * SIDE)
         + [pltpu.VMEM((SIDE * SIDE, 2 * tile, 2 * tile), F32)]

time: 79.1 us -> 77.4 us (0.979)
  local copies, waits for them, and re-layouts: 7.97 us -> 4.56 us
  Pallas kernels: 21.5 us -> 23.1 us
    unnamed x9 -> x1, local copies, waits for them, and re-layouts: 4.79 us -> 1.39 us
    pallas_call x7, Pallas kernels: 21.5 us -> 23.1 us  [call(): pl.pallas_call(kernel, in_specs=[smem] * scalars + [vmem] * (len(ins) - s...]
  transfers between devices with their start and end apart: 14 -> 14, of which waited for: 5 -> 5; matrix products, arithmetic and copies ran while one was open for 7% -> 7% of each run, Pallas kernels for 18% -> 19%
where the time goes in v6:
time: 77.4 us; the launch traced here: 76.6 us
  waiting for transfers between devices  23.8 us (31%)
  starting transfers between devices  23.4 us (30%)
  Pallas kernels  23.1 us (30%)
  local copies, waits for them, and re-layouts  4.56 us (6%)
  other arithmetic  0.96 us (1%)
  between operations  0.78 us (1%)
    ppermute x14, waiting for transfers between devices, send(): return lax.ppermute(value, AXES, [(i, to(i) % count) for i in range(count)])  23.8 us
    ppermute x14, starting transfers between devices, send(): return lax.ppermute(value, AXES, [(i, to(i) % count) for i in range(count)])  23.4 us
    pallas_call x7, Pallas kernels, call(): pl.pallas_call(kernel, in_specs=[smem] * scalars + [vmem] * (len(ins) - s...  23.1 us
    dynamic_slice x1, local copies, waits for them, and re-layouts, body(): sx = send(lax.dynamic_slice_in_dim(correlation, 1 - device % 2, 1, 0), swap)  1.77 us
  transfers between devices with their start and end apart: 14, of which 5 were waited for; matrix products, arithmetic and copies ran while one was open for 7% of the time, Pallas kernels for 19%

profile of v6, /device:TPU:1, one launch (start us, length us, event | category | flops | bytes accessed | tf_op | source)
XLA Modules:
  0.0 76.6 jit_solution(16327972067001043075)
XLA Ops:
  0.7 0.1 stack.2.meta
  0.8 2.0 %shard_map.59 = (f32[1,6,128,128]{3,2,1,0:T(8,128)S(1)}, f32[1,6,128,128]{3,2,1,0:T(8,128)}, f32[9,128,128]{2,1,0:T(8,128)S(1)}, f32[9,128,128]{2,1,0:T(8,128)S(1)}) custom-call(s32[16]{0:T(128)S(1)} %stack.2.meta, f32[2,6,128,128]{3,2,1,0:T(8,128)} %z.7), custom_call_target="tpu_custom_call" | custom-call | flops 1000 | bytes 4194304 | tf_op jit(solution)/shard_map/pallas_call | solution.py:461
  2.8 2.0 %collective-permute-start = (f32[1,6,128,128]{3,2,1,0:T(8,128)S(1)}, f32[1,6,128,128]{3,2,1,0:T(8,128)S(1)}, u32[]{:S(2)}, u32[]{:S(2)}) collective-permute-start(f32[1,6,128,128]{3,2,1,0:T(8,128)S(1)} %get-tuple-element.23), channel_id=1, source_target_pairs={{0,1},{1,0},{2,3},{3,2},{4,5},{5,4},{6,7},{7,6},{8,9},{9,8},{10,11... | collective-permute-start | bytes 1179656 | tf_op jit(solution)/shard_map/ppermute | solution.py:30
  4.8 0.0 collective-permute-start.1
  4.9 1.0 %collective-permute-start.4 = (f32[9,128,128]{2,1,0:T(8,128)S(1)}, f32[9,128,128]{2,1,0:T(8,128)S(1)}, u32[]{:S(2)}, u32[]{:S(2)}) collective-permute-start(f32[9,128,128]{2,1,0:T(8,128)S(1)} %get-tuple-element.25), channel_id=1, source_target_pairs={{0,2},{1,3},{2,0},{3,1},{4,6},{5,7},{6,4},{7,5},{8,10},{9,11},{10,... | collective-permute-start | bytes 1769480 | tf_op jit(solution)/shard_map/ppermute | solution.py:30
  5.8 1.6 %collective-permute-start.5 = (f32[9,128,128]{2,1,0:T(8,128)S(1)}, f32[9,128,128]{2,1,0:T(8,128)S(1)}, u32[]{:S(2)}, u32[]{:S(2)}) collective-permute-start(f32[9,128,128]{2,1,0:T(8,128)S(1)} %get-tuple-element.26), channel_id=1, source_target_pairs={{0,30},{1,31},{2,4},{3,5},{4,2},{5,3},{6,8},{7,9},{8,6},{9,7},{10,... | collective-permute-start | bytes 1769480 | tf_op jit(solution)/shard_map/ppermute | solution.py:30
  7.5 1.8 %constant_dynamic-slice_fusion = f32[1,6,128,128]{3,2,1,0:T(8,128)} fusion(f32[2,6,128,128]{3,2,1,0:T(8,128)} %s.1, s32[]{:T(128)S(6)} %select_n.66), kind=kLoop, calls=%fused_computation.22 | loop fusion | bytes 786436 | tf_op jit(solution)/shard_map/dynamic_slice | solution.py:487
  9.2 1.2 %collective-permute-start.6 = (f32[1,6,128,128]{3,2,1,0:T(8,128)}, f32[1,6,128,128]{3,2,1,0:T(8,128)}, u32[]{:S(2)}, u32[]{:S(2)}) collective-permute-start(f32[1,6,128,128]{3,2,1,0:T(8,128)} %constant_dynamic-slice_fusion), channel_id=1, source_target_pairs={{0,1},{1,0},{2,3},{3,2},{4,5},{5,4},{6,7},{7,6},{8,9},{9,8},{10,11... | collective-permute-start | bytes 1179656 | tf_op jit(solution)/shard_map/ppermute | solution.py:30
  10.4 3.2 %collective-permute-done.x0 = f32[1,6,128,128]{3,2,1,0:T(8,128)S(1)} collective-permute-done((f32[1,6,128,128]{3,2,1,0:T(8,128)S(1)}, f32[1,6,128,128]{3,2,1,0:T(8,128)S(1)}, u32[]{:S(2)}, u32[]{:S(2)}) %collective-permute-start) | collective-permute-done | bytes 393248 | tf_op jit(solution)/shard_map/ppermute | solution.py:30
  13.6 3.8 %collective-permute-start.2 = (f32[1,6,128,128]{3,2,1,0:T(8,128)S(1)}, f32[1,6,128,128]{3,2,1,0:T(8,128)S(1)}, u32[]{:S(2)}, u32[]{:S(2)}) collective-permute-start(f32[1,6,128,128]{3,2,1,0:T(8,128)S(1)} %collective-permute-done.x0), channel_id=1, source_target_pairs={{0,2},{1,31},{2,4},{3,1},{4,6},{5,3},{6,8},{7,5},{8,10},{9,7},{10,... | collective-permute-start | bytes 1179656 | tf_op jit(solution)/shard_map/ppermute | solution.py:30
  17.4 4.7 %collective-permute-done.1.x1 = f32[1,6,128,128]{3,2,1,0:T(8,128)S(1)} collective-permute-done((f32[1,6,128,128]{3,2,1,0:T(8,128)}, f32[1,6,128,128]{3,2,1,0:T(8,128)S(1)}, u32[]{:S(2)}, u32[]{:S(2)}) %collective-permute-start.1) | collective-permute-done | bytes 393248 | tf_op jit(solution)/shard_map/ppermute | solution.py:30
  22.1 3.8 %collective-permute-start.3 = (f32[1,6,128,128]{3,2,1,0:T(8,128)S(1)}, f32[1,6,128,128]{3,2,1,0:T(8,128)}, u32[]{:S(2)}, u32[]{:S(2)}) collective-permute-start(f32[1,6,128,128]{3,2,1,0:T(8,128)S(1)} %collective-permute-done.1.x1), channel_id=1, source_target_pairs={{0,2},{1,31},{2,4},{3,1},{4,6},{5,3},{6,8},{7,5},{8,10},{9,7},{10,... | collective-permute-start | bytes 1179656 | tf_op jit(solution)/shard_map/ppermute | solution.py:30
  25.8 1.4 %copy.6 = s32[64,6]{1,0:T(8,128)} copy(s32[64,6]{0,1:T(8,128)} %param.6) | data formatting | bytes 3072 | tf_op args[2]
  27.2 1.3 %gather_fusion = s32[14,6]{1,0:T(8,128)S(1)} fusion(s32[64,6]{1,0:T(8,128)} %copy.6, s32[1024]{0:T(1024)S(1)} %pad_clamp_fusion), kind=kCustom, calls=%fused_computation | custom fusion | bytes 728 | tf_op jit(solution)/shard_map/gather | solution.py:446
  28.6 0.8 %convert_reduce_fusion = s32[14]{0:T(128)S(1)} fusion(s32[14,6]{1,0:T(8,128)S(1)} %gather_fusion, s32[5]{0:T(128)} %constant.83.clone, s32[14]{0:T(128)S(1)} %and_select_fusion), kind=kLoop, calls=%fused_computation.9 | loop fusion | flops 1176 | bytes 412 | tf_op jit(solution)/shard_map/reduce_sum | solution.py:448
  29.4 0.1 pad_add_fusion.meta
  29.5 0.0 collective-permute-done.4.zi
  29.5 0.0 collective-permute-done.5.zc
  29.5 0.0 collective-permute-done.2.n0
  29.5 1.0 %collective-permute-done.3.n1 = f32[1,6,128,128]{3,2,1,0:T(8,128)} collective-permute-done((f32[1,6,128,128]{3,2,1,0:T(8,128)S(1)}, f32[1,6,128,128]{3,2,1,0:T(8,128)}, u32[]{:S(2)}, u32[]{:S(2)}) %collective-permute-start.3) | collective-permute-done | bytes 393248 | tf_op jit(solution)/shard_map/ppermute | solution.py:30
  30.6 4.4 %shard_map.62 = (f32[1,6,128,128]{3,2,1,0:T(8,128)S(1)}, f32[1,6,128,128]{3,2,1,0:T(8,128)S(1)}, f32[1,6,128,128]{3,2,1,0:T(8,128)S(1)}, f32[7,128,128]{2,1,0:T(8,128)S(1)}, f32[7,128,128]{2,1,0:T(8,128)S(1)}) custom-call(s32[16]{0:T(128)S(1)} %pad_add_fusion.meta, f32[2,6,128,128]{3,2,1,0:T(8,128)} %s.1, f32[2,6,128,128]{3,2,1,0:T(8,128)} %z.7, ...), custom_call_target="tpu_custom_call" | custom-call | flops 2000000000 | bytes 4194304 | tf_op jit(solution)/shard_map/pallas_call | solution.py:461
  34.9 2.4 %collective-permute-start.7 = (f32[1,6,128,128]{3,2,1,0:T(8,128)S(1)}, f32[1,6,128,128]{3,2,1,0:T(8,128)S(1)}, u32[]{:S(2)}, u32[]{:S(2)}) collective-permute-start(f32[1,6,128,128]{3,2,1,0:T(8,128)S(1)} %get-tuple-element.34), channel_id=1, source_target_pairs={{0,1},{1,0},{2,3},{3,2},{4,5},{5,4},{6,7},{7,6},{8,9},{9,8},{10,11... | collective-permute-start | bytes 1179656 | tf_op jit(solution)/shard_map/ppermute | solution.py:30
  37.3 1.4 %collective-permute-start.8 = (f32[7,128,128]{2,1,0:T(8,128)S(1)}, f32[7,128,128]{2,1,0:T(8,128)S(1)}, u32[]{:S(2)}, u32[]{:S(2)}) collective-permute-start(f32[7,128,128]{2,1,0:T(8,128)S(1)} %get-tuple-element.39), channel_id=1, source_target_pairs={{0,2},{1,3},{2,0},{3,1},{4,6},{5,7},{6,4},{7,5},{8,10},{9,11},{10,... | collective-permute-start | bytes 1376264 | tf_op jit(solution)/shard_map/ppermute | solution.py:30
  38.7 0.0 collective-permute-start.9
  38.7 0.0 collective-permute-done.6.s
  38.7 2.7 %shard_map.60.after.nearer = f32[1,6,128,128]{3,2,1,0:T(8,128)S(1)} custom-call(s32[16]{0:T(128)S(1)} %pad_add_fusion.meta, f32[1,6,128,128]{3,2,1,0:T(8,128)} %collective-permute-done.6.s, f32[2,6,128,128]{3,2,1,0:T(8,128)} %z.7, f32[1,6,128,128]{3,2,1,0:T(8,128)S(1)} %collective-permute-done.x0, f32[1,6,128,128]{3,2,1,0:T(8,128)S(1)} %collective-permute-done.1.x1, ...), custom_call_target="tpu_custom_call" | custom-call | flops 2000000000 | bytes 4194304 | tf_op jit(solution)/shard_map/pallas_call | solution.py:461
  41.4 1.8 %collective-permute-start.10 = (f32[1,6,128,128]{3,2,1,0:T(8,128)S(1)}, f32[1,6,128,128]{3,2,1,0:T(8,128)S(1)}, u32[]{:S(2)}, u32[]{:S(2)}) collective-permute-start(f32[1,6,128,128]{3,2,1,0:T(8,128)S(1)} %shard_map.60.after.nearer), channel_id=1, source_target_pairs={{0,2},{1,31},{2,4},{3,1},{4,6},{5,3},{6,8},{7,5},{8,10},{9,7},{10,... | collective-permute-start | bytes 1179656 | tf_op jit(solution)/shard_map/ppermute | solution.py:30
  43.2 2.5 %shard_map.61 = (f32[2,6,128,128]{3,2,1,0:T(8,128)S(1)}, bf16[1024,512]{1,0:T(8,128)(2,1)S(1)}, bf16[512,512]{1,0:T(8,128)(2,1)S(1)}, bf16[512,512]{1,0:T(8,128)...) custom-call(s32[16]{0:T(128)S(1)} %pad_add_fusion.meta, ...), custom_call_target="tpu_custom_call" | custom-call | flops 2000000000 | bytes 4194304 | tf_op jit(solution)/shard_map/pallas_call | solution.py:461
  45.7 0.0 collective-permute-done.7.farther
  45.7 2.6 %collective-permute-start.11 = (f32[1,6,128,128]{3,2,1,0:T(8,128)S(1)}, f32[1,6,128,128]{3,2,1,0:T(8,128)S(1)}, u32[]{:S(2)}, u32[]{:S(2)}) collective-permute-start(f32[1,6,128,128]{3,2,1,0:T(8,128)S(1)} %collective-permute-done.7.farther), channel_id=1, source_target_pairs={{0,2},{1,31},{2,4},{3,1},{4,6},{5,3},{6,8},{7,5},{8,10},{9,7},{10,... | collective-permute-start | bytes 1179656 | tf_op jit(solution)/shard_map/ppermute | solution.py:30
  48.3 3.4 %shard_map.63.early = f32[16,256,256]{2,1,0:T(8,128)S(1)} custom-call(s32[16]{0:T(128)S(1)} %pad_add_fusion.meta, bf16[1024,512]{1,0:T(8,128)(2,1)S(1)} %get-tuple-element.30.t_own, bf16[768,512]{1,0:T(8,128)(2,1)S(1)} %get-tuple-element.31.t_swap, f32[1,6,128,128]{3,2,1,0:T(8,128)S(1)} %get-tuple-element.32.p0, ...), custom_call_target="tpu_custom_call" | custom-call | flops 4000000000 | bytes 4194304 | tf_op jit(solution)/shard_map/pallas_call | solution.py:461
  51.6 0.0 collective-permute-done.8.pi
  51.6 8.3 %collective-permute-done.9.pc = f32[7,128,128]{2,1,0:T(8,128)S(1)} collective-permute-done((f32[7,128,128]{2,1,0:T(8,128)S(1)}, f32[7,128,128]{2,1,0:T(8,128)S(1)}, u32[]{:S(2)}, u32[]{:S(2)}) %collective-permute-start.9) | collective-permute-done | bytes 458784 | tf_op jit(solution)/shard_map/ppermute | solution.py:30
  60.0 2.0 %shard_map.64 = (f32[8,256,256]{2,1,0:T(8,128)S(1)}, f32[256,256]{1,0:T(8,128)S(1)}, f32[256,256]{1,0:T(8,128)S(1)}) custom-call(s32[16]{0:T(128)S(1)} %pad_add_fusion.meta, bf16[512,512]{1,0:T(8,128)(2,1)S(1)} %get-tuple-element.35.t_up, bf16[512,512]{1,0:T(8,128)(2,1)S(1)} %get-tuple-element.36.t_down, bf16[256,512]{1,0:T(8,128)(2,1)S(1)} %get-tuple-element.37.t_far_up, ...), custom_call_target="tpu_custom_call" | custom-call | flops 1000000000 | bytes 4194304 | tf_op jit(solution)/shard_map/pallas_call | solution.py:461
  62.0 0.1 collective-permute-start.12
  62.1 1.7 %collective-permute-start.13 = (f32[256,256]{1,0:T(8,128)S(1)}, f32[256,256]{1,0:T(8,128)S(1)}, u32[]{:S(2)}, u32[]{:S(2)}) collective-permute-start(f32[256,256]{1,0:T(8,128)S(1)} %get-tuple-element.43), channel_id=1, source_target_pairs={{0,4},{1,3},{2,1},{3,2},{4,8},{5,7},{6,5},{7,6},{8,12},{9,11},{10,... | collective-permute-start | bytes 786440 | tf_op jit(solution)/shard_map/ppermute | solution.py:30
  63.8 0.0 collective-permute-done.10.nearer
  63.8 6.6 %collective-permute-done.12.first = f32[256,256]{1,0:T(8,128)S(1)} collective-permute-done((f32[256,256]{1,0:T(8,128)S(1)}, f32[256,256]{1,0:T(8,128)S(1)}, u32[]{:S(2)}, u32[]{:S(2)}) %collective-permute-start.12) | collective-permute-done | bytes 262176 | tf_op jit(solution)/shard_map/ppermute | solution.py:30
  70.4 0.0 collective-permute-done.13.second
  70.4 0.0 collective-permute-done.11.farther
  70.4 6.2 %shard_map.65 = (f32[2,6,128,128]{3,2,1,0:T(8,128)}, f32[2,6,128,128]{3,2,1,0:T(8,128)}) custom-call(s32[16]{0:T(128)S(1)} %pad_add_fusion.meta, f32[2,6,128,128]{3,2,1,0:T(8,128)S(1)} %get-tuple-element.27.z, bf16[2,128,2048]{2,1,0:T(8,128)(2,1)S(1)} %get-tuple-element.28.z_own, bf16[768,512]{1,0:T(8,128)(2,1)S(1)} %get-tuple-element.29.t_near, ...), custom_call_target="tpu_custom_call" | custom-call | flops 4000000000 | bytes 4194304 | tf_op jit(solution)/shard_map/pallas_call | solution.py:461
  (6 shorter events, 0.0 us)
Async XLA Ops:
  2.8 10.8 %collective-permute-start = (f32[1,6,128,128]{3,2,1,0:T(8,128)S(1)}, f32[1,6,128,128]{3,2,1,0:T(8,128)S(1)}, u32[]{:S(2)}, u32[]{:S(2)}) collective-permute-start(f32[1,6,128,128]{3,2,1,0:T(8,128)S(1)} %get-tuple-element.23), channel_id=1, source_target_pairs={{0,1},{1,0},{2,3},{3,2},{4,5},{5,4},{6,7},{7,6},{8,9},{9,8},{10,11... | collective-permute-start | bytes 1179656 | tf_op jit(solution)/shard_map/ppermute | solution.py:30
  4.8 17.2 %collective-permute-start.1 = (f32[1,6,128,128]{3,2,1,0:T(8,128)}, f32[1,6,128,128]{3,2,1,0:T(8,128)S(1)}, u32[]{:S(2)}, u32[]{:S(2)}) collective-permute-start(f32[1,6,128,128]{3,2,1,0:T(8,128)} %get-tuple-element.24), channel_id=1, source_target_pairs={{0,1},{1,0},{2,3},{3,2},{4,5},{5,4},{6,7},{7,6},{8,9},{9,8},{10,11... | collective-permute-start | bytes 1179656 | tf_op jit(solution)/shard_map/ppermute | solution.py:30
  4.9 24.6 %collective-permute-start.4 = (f32[9,128,128]{2,1,0:T(8,128)S(1)}, f32[9,128,128]{2,1,0:T(8,128)S(1)}, u32[]{:S(2)}, u32[]{:S(2)}) collective-permute-start(f32[9,128,128]{2,1,0:T(8,128)S(1)} %get-tuple-element.25), channel_id=1, source_target_pairs={{0,2},{1,3},{2,0},{3,1},{4,6},{5,7},{6,4},{7,5},{8,10},{9,11},{10,... | collective-permute-start | bytes 1769480 | tf_op jit(solution)/shard_map/ppermute | solution.py:30
  5.8 23.7 %collective-permute-start.5 = (f32[9,128,128]{2,1,0:T(8,128)S(1)}, f32[9,128,128]{2,1,0:T(8,128)S(1)}, u32[]{:S(2)}, u32[]{:S(2)}) collective-permute-start(f32[9,128,128]{2,1,0:T(8,128)S(1)} %get-tuple-element.26), channel_id=1, source_target_pairs={{0,30},{1,31},{2,4},{3,5},{4,2},{5,3},{6,8},{7,9},{8,6},{9,7},{10,... | collective-permute-start | bytes 1769480 | tf_op jit(solution)/shard_map/ppermute | solution.py:30
  9.2 29.5 %collective-permute-start.6 = (f32[1,6,128,128]{3,2,1,0:T(8,128)}, f32[1,6,128,128]{3,2,1,0:T(8,128)}, u32[]{:S(2)}, u32[]{:S(2)}) collective-permute-start(f32[1,6,128,128]{3,2,1,0:T(8,128)} %constant_dynamic-slice_fusion), channel_id=1, source_target_pairs={{0,1},{1,0},{2,3},{3,2},{4,5},{5,4},{6,7},{7,6},{8,9},{9,8},{10,11... | collective-permute-start | bytes 1179656 | tf_op jit(solution)/shard_map/ppermute | solution.py:30
  13.6 15.9 %collective-permute-start.2 = (f32[1,6,128,128]{3,2,1,0:T(8,128)S(1)}, f32[1,6,128,128]{3,2,1,0:T(8,128)S(1)}, u32[]{:S(2)}, u32[]{:S(2)}) collective-permute-start(f32[1,6,128,128]{3,2,1,0:T(8,128)S(1)} %collective-permute-done.x0), channel_id=1, source_target_pairs={{0,2},{1,31},{2,4},{3,1},{4,6},{5,3},{6,8},{7,5},{8,10},{9,7},{10,... | collective-permute-start | bytes 1179656 | tf_op jit(solution)/shard_map/ppermute | solution.py:30
  22.1 8.5 %collective-permute-start.3 = (f32[1,6,128,128]{3,2,1,0:T(8,128)S(1)}, f32[1,6,128,128]{3,2,1,0:T(8,128)}, u32[]{:S(2)}, u32[]{:S(2)}) collective-permute-start(f32[1,6,128,128]{3,2,1,0:T(8,128)S(1)} %collective-permute-done.1.x1), channel_id=1, source_target_pairs={{0,2},{1,31},{2,4},{3,1},{4,6},{5,3},{6,8},{7,5},{8,10},{9,7},{10,... | collective-permute-start | bytes 1179656 | tf_op jit(solution)/shard_map/ppermute | solution.py:30
  34.9 10.7 %collective-permute-start.7 = (f32[1,6,128,128]{3,2,1,0:T(8,128)S(1)}, f32[1,6,128,128]{3,2,1,0:T(8,128)S(1)}, u32[]{:S(2)}, u32[]{:S(2)}) collective-permute-start(f32[1,6,128,128]{3,2,1,0:T(8,128)S(1)} %get-tuple-element.34), channel_id=1, source_target_pairs={{0,1},{1,0},{2,3},{3,2},{4,5},{5,4},{6,7},{7,6},{8,9},{9,8},{10,11... | collective-permute-start | bytes 1179656 | tf_op jit(solution)/shard_map/ppermute | solution.py:30
  37.3 14.3 %collective-permute-start.8 = (f32[7,128,128]{2,1,0:T(8,128)S(1)}, f32[7,128,128]{2,1,0:T(8,128)S(1)}, u32[]{:S(2)}, u32[]{:S(2)}) collective-permute-start(f32[7,128,128]{2,1,0:T(8,128)S(1)} %get-tuple-element.39), channel_id=1, source_target_pairs={{0,2},{1,3},{2,0},{3,1},{4,6},{5,7},{6,4},{7,5},{8,10},{9,11},{10,... | collective-permute-start | bytes 1376264 | tf_op jit(solution)/shard_map/ppermute | solution.py:30
  38.7 21.2 %collective-permute-start.9 = (f32[7,128,128]{2,1,0:T(8,128)S(1)}, f32[7,128,128]{2,1,0:T(8,128)S(1)}, u32[]{:S(2)}, u32[]{:S(2)}) collective-permute-start(f32[7,128,128]{2,1,0:T(8,128)S(1)} %get-tuple-element.40), channel_id=1, source_target_pairs={{0,30},{1,31},{2,4},{3,5},{4,2},{5,3},{6,8},{7,9},{8,6},{9,7},{10,... | collective-permute-start | bytes 1376264 | tf_op jit(solution)/shard_map/ppermute | solution.py:30
  41.4 22.4 %collective-permute-start.10 = (f32[1,6,128,128]{3,2,1,0:T(8,128)S(1)}, f32[1,6,128,128]{3,2,1,0:T(8,128)S(1)}, u32[]{:S(2)}, u32[]{:S(2)}) collective-permute-start(f32[1,6,128,128]{3,2,1,0:T(8,128)S(1)} %shard_map.60.after.nearer), channel_id=1, source_target_pairs={{0,2},{1,31},{2,4},{3,1},{4,6},{5,3},{6,8},{7,5},{8,10},{9,7},{10,... | collective-permute-start | bytes 1179656 | tf_op jit(solution)/shard_map/ppermute | solution.py:30
  45.7 24.7 %collective-permute-start.11 = (f32[1,6,128,128]{3,2,1,0:T(8,128)S(1)}, f32[1,6,128,128]{3,2,1,0:T(8,128)S(1)}, u32[]{:S(2)}, u32[]{:S(2)}) collective-permute-start(f32[1,6,128,128]{3,2,1,0:T(8,128)S(1)} %collective-permute-done.7.farther), channel_id=1, source_target_pairs={{0,2},{1,31},{2,4},{3,1},{4,6},{5,3},{6,8},{7,5},{8,10},{9,7},{10,... | collective-permute-start | bytes 1179656 | tf_op jit(solution)/shard_map/ppermute | solution.py:30
  62.0 8.4 %collective-permute-start.12 = (f32[256,256]{1,0:T(8,128)S(1)}, f32[256,256]{1,0:T(8,128)S(1)}, u32[]{:S(2)}, u32[]{:S(2)}) collective-permute-start(f32[256,256]{1,0:T(8,128)S(1)} %get-tuple-element.42), channel_id=1, source_target_pairs={{0,1},{1,2},{2,0},{3,31},{4,5},{5,6},{6,4},{7,3},{8,9},{9,10},{10,... | collective-permute-start | bytes 786440 | tf_op jit(solution)/shard_map/ppermute | solution.py:30
  62.1 8.4 %collective-permute-start.13 = (f32[256,256]{1,0:T(8,128)S(1)}, f32[256,256]{1,0:T(8,128)S(1)}, u32[]{:S(2)}, u32[]{:S(2)}) collective-permute-start(f32[256,256]{1,0:T(8,128)S(1)} %get-tuple-element.43), channel_id=1, source_target_pairs={{0,4},{1,3},{2,1},{3,2},{4,8},{5,7},{6,5},{7,6},{8,12},{9,11},{10,... | collective-permute-start | bytes 786440 | tf_op jit(solution)/shard_map/ppermute | solution.py:30

commit v7 on v6

--- a/solution.py
+++ b/solution.py
@@ -138,8 +138,8 @@
     return value.reshape(value.shape[0] * value.shape[1], value.shape[2])
 
 
-def row_matmul(left_high, left_low, right_high, right_low, out, tile):
-    for c in range(0, COLS, 2):
+def row_matmul(left_high, left_low, right_high, right_low, out, tile, columns=range(0, COLS, 2)):
+    for c in columns:
         lo, hi = max(c - REACH, 0), min(c + 1 + REACH, COLS - 1) + 1
         k = slice(lo * tile, hi * tile)
         n = slice(c * tile, (c + 2) * tile)
@@ -229,7 +229,7 @@
         second[...] = edge[4]
 
 
-def product_kernel(meta, s, z, x0, x1, n0, n1, zi, zc, p0, p1, pf, chip, link, z_high, z_low, s_high, s_low, dense):
+def prepare_kernel(meta, s, z, x0, x1, z_high, z_low, s_high, s_low):
     tile = z.shape[-1]
     rows = Rows(meta)
     for c in range(COLS):
@@ -238,14 +238,22 @@
             near_by = abs(col - i) <= REACH
             put(s_high, s_low, i, c, tile, rows.own(s, i, col) if near_by else zero(tile))
             put(z_high, z_low, i - COL0, c, tile, rows.own(z, i, col) if near_by else zero(tile))
-        for side, refs in enumerate(((x0, x1), (n0, n1))):
-            for r in range(2):
-                where = rows.side_row(side) + r - COL0
-                put(z_high, z_low, where, c, tile, rows.side(refs[r], side, r, col))
-        row = -REACH
-        put(z_high, z_low, 0, c, tile, rows.packed((zc, zi), Z_UP, -4, 1, col) if abs(col - row) <= REACH else zero(tile))
-        row = OWN - 1 + REACH
-        put(z_high, z_low, COLS - 1, c, tile, rows.packed((zi, zc), Z_DOWN, 4, 0, col) if abs(col - row) <= REACH else zero(tile))
+            put(z_high, z_low, rows.side_row(0) + i - COL0, c, tile, rows.side((x0, x1)[i], 0, i, col))
+
+
+def product_kernel(
+    meta, z_high_in, z_low_in, s_high, s_low, n0, n1, zi, zc, p0, p1, pf, chip, link, z_high, z_low, dense
+):
+    tile = n0.shape[-1]
+    rows = Rows(meta)
+    for c in range(COLS):
+        col = c + COL0
+        for r, ref in enumerate((n0, n1)):
+            put(z_high, z_low, rows.side_row(1) + r - COL0, c, tile, rows.side(ref, 1, r, col))
+        value = rows.packed((zc, zi), Z_UP, -4, 1, col) if col <= 0 else zero(tile)
+        put(z_high, z_low, 0, c, tile, value)
+        value = rows.packed((zi, zc), Z_DOWN, 4, 0, col) if col >= 1 else zero(tile)
+        put(z_high, z_low, COLS - 1, c, tile, value)
     row_matmul(s_high, s_low, z_high, z_low, dense, tile)
     for i, ref in enumerate((p0, p1)):
         for slot in range(2 * REACH):
@@ -311,7 +319,7 @@
         out[0, slot] = dense[REACH if slot == 0 else pos + jnp.where(pos >= REACH, 1, 0)]
 
 
-def turn_kernel(meta, z, x0, x1, n0, n1, zi, zc, after, z_kept, t_own, t_up, t_down, t_swap, t_near, t_far_up, t_far_down, z_own):
+def turn_kernel(meta, z, x0, x1, n0, n1, zi, zc, after, z_kept, t_own, t_up, t_down, t_swap, t_near, t_far_up, t_far_down, z_high, z_low):
     tile = z.shape[-1]
     rows = Rows(meta)
 
@@ -327,9 +335,7 @@
             col = c + COL0
             value = rows.own(z, r, col) if abs(col - r) <= REACH else zero(tile)
             store(t_own, c, r, value)
-            high, low = split(value)
-            z_own[r, :, c * tile : (c + 1) * tile] = high
-            z_own[r, :, (COLS + c) * tile : (COLS + c + 1) * tile] = low
+            put(z_high, z_low, r, c, tile, value)
         for c in range(4):
             col = c + COL0
             store(t_up, c, r, rows.packed((zc, zi), Z_UP, -4, r, col) if abs(col - (r - 4)) <= REACH else zero(tile))
@@ -384,7 +390,8 @@
 
 
 def refine_kernel(
-    meta, z, z_own, t_near, early, edge, nearer, farther, first, second, refined, correction, high, low, late, d_high, d_low, dense, z_high, z_low,
+    meta, z, z_high, z_low, t_near, early, edge, nearer, farther, first, second, refined, correction,
+    high, low, late, d_high, d_low, d_own, update,
 ):
     tile = z.shape[-1]
     rows = Rows(meta)
@@ -398,14 +405,14 @@
         lax.broadcasted_iota(jnp.int32, (tile, tile), 0) == lax.broadcasted_iota(jnp.int32, (tile, tile), 1)
     ).astype(F32)
     shift = rows.side_pair(1)
-    for a in range(PAIRS):
-        for b in range(PAIRS):
-            if abs(a - b) > 2:
-                continue
+    for b in range(PAIRS):
+        for a in range(max(0, b - 2), min(PAIRS, b + 3)):
             gram = early[PAIRS * a + b]
             ia, ib = a - shift, b - shift
             there = (ia >= 0) & (ia < SIDE) & (ib >= 0) & (ib < SIDE)
-            gram = gram + jnp.where(there, late[jnp.clip(SIDE * ia + ib, 0, SIDE * SIDE - 1)], 0.0)
+            part = late[jnp.clip(SIDE * ia + ib, 0, SIDE * SIDE - 1)]
+            always = 0 < a < SIDE and 0 < b < SIDE
+            gram = gram + (part if always else jnp.where(there, part, 0.0))
             e = a if b < 2 else a - 2
             if 0 <= e < 2:
                 gram = gram + edge[2 * b + e]
@@ -424,17 +431,12 @@
                         value = zero(tile)
                     put(d_high, d_low, k, c, tile, value)
                     if k + COL0 in (0, 1):
-                        dense[k + COL0, c] = value
+                        d_own[k + COL0, c] = value
+        row_matmul(z_high, z_low, d_high, d_low, update, tile, (2 * b,))
     for i in range(OWN):
         for slot in range(2 * REACH):
-            correction[i, slot] = dense[i, rows.dense_slot(i, slot)]
-    half = COLS * tile
-    z_high[...] = z_own[:, :, :half]
-    z_low[...] = z_own[:, :, half:]
-    row_matmul(z_high, z_low, d_high, d_low, dense, tile)
-    for i in range(OWN):
-        for slot in range(2 * REACH):
-            refined[i, slot] = z[i, slot] + 0.5 * dense[i, rows.dense_slot(i, slot)]
+            correction[i, slot] = d_own[i, rows.dense_slot(i, slot)]
+            refined[i, slot] = z[i, slot] + 0.5 * update[i, rows.dense_slot(i, slot)]
 
 
 def body(correlation, factor, pattern):
@@ -457,13 +459,15 @@
             return pltpu.with_memory_space_constraint(value, pltpu.HBM)
         return pltpu.with_memory_space_constraint(value, pltpu.VMEM)
 
-    def call(kernel, ins, outs, scratch, flops, scalars=1):
+    def call(kernel, ins, outs, scratch, flops, aliases={}):
+        scalars = 1
         return pl.pallas_call(
             kernel,
             in_specs=[smem] * scalars + [vmem] * (len(ins) - scalars),
             out_specs=jax.tree.map(lambda _: vmem, outs),
             out_shape=outs,
             scratch_shapes=scratch,
+            input_output_aliases=aliases,
             compiler_params=pltpu.CompilerParams(vmem_limit_bytes=VMEM_LIMIT),
             cost_estimate=pl.CostEstimate(flops=flops, bytes_accessed=4 << 20, transcendentals=0),
         )(*ins[:scalars], *map(resident, ins[scalars:]))
@@ -485,12 +489,16 @@
     zi, zc = send(zi, inside), send(zc, across)
     n = [send(x[r], near) for r in range(OWN)]
     sx = send(lax.dynamic_slice_in_dim(correlation, 1 - device % 2, 1, 0), swap)
-    p0, p1, pf, pi, pc = call(
+    square = shape(COLS, tile, COLS * tile, dtype=BF16)
+    pair = shape(OWN, tile, COLS * tile, dtype=BF16)
+    ready = call(prepare_kernel, (meta, correlation, factor, *x), (square, square, pair, pair), [], int(1e9))
+    p0, p1, pf, pi, pc, *_ = call(
         product_kernel,
-        (meta, correlation, factor, *x, *n, zi, zc),
-        (row, row, row, seven, seven),
-        halves_of(COLS, COLS) + halves_of(OWN, COLS) + [dense],
+        (meta, *ready, *n, zi, zc),
+        (row, row, row, seven, seven, square, square),
+        [dense],
         int(2e9),
+        aliases={1: 5, 2: 6},
     )
     pc = send(pc, across)
     px = send(pf, swap)
@@ -508,11 +516,11 @@
     def turned(columns):
         return shape(columns * tile, 4 * tile, dtype=BF16)
 
-    z_kept, t_own, t_up, t_down, t_swap, t_near, t_far_up, t_far_down, z_own = call(
+    z_kept, t_own, t_up, t_down, t_swap, t_near, t_far_up, t_far_down, *z_own = call(
         turn_kernel,
         (meta, factor, *x, *n, zi, zc, ps),
         (shape(*factor.shape), turned(COLS), turned(4), turned(4), turned(2 * SIDE), turned(2 * SIDE), turned(2), turned(2),
-         shape(OWN, tile, 2 * COLS * tile, dtype=BF16)),
+         *[shape(OWN, tile, COLS * tile, dtype=BF16)] * 2),
         [],
         int(2e9),
     )
@@ -533,13 +541,12 @@
     far = (send(far[0], far_first), send(far[1], far_second))
     return call(
         refine_kernel,
-        (meta, z_kept, z_own, t_near, early, edge, *pn, *far),
+        (meta, z_kept, *z_own, t_near, early, edge, *pn, *far),
         (shape(*factor.shape), shape(*factor.shape)),
         halves_of(2, 2 * SIDE)
         + [pltpu.VMEM((SIDE * SIDE, 2 * tile, 2 * tile), F32)]
         + halves_of(COLS, COLS)
-        + [dense]
-        + halves_of(OWN, COLS),
+        + [dense, dense],
         int(4e9),
     )
 

time: 77.4 us -> 76.1 us (0.983)
  waiting for transfers between devices: 23.8 us -> 21.7 us
    ppermute x14, waiting for transfers between devices: 23.8 us -> 21.7 us  [send(): return lax.ppermute(value, AXES, [(i, to(i) % count) for i in range(count)])]
    pallas_call x7 -> x8, Pallas kernels: 23.1 us -> 23.7 us  [call(): pl.pallas_call(kernel, in_specs=[smem] * scalars + [vmem] * (len(ins) - s...]
  transfers between devices with their start and end apart: 14 -> 14, of which waited for: 5 -> 5; matrix products, arithmetic and copies ran while one was open for 7% -> 7% of each run, Pallas kernels for 19% -> 20%
where the time goes in v7:
time: 76.1 us; the launch traced here: 75.3 us
  Pallas kernels  23.7 us (31%)
  starting transfers between devices  23.6 us (31%)
  waiting for transfers between devices  21.7 us (29%)
  local copies, waits for them, and re-layouts  4.56 us (6%)
  other arithmetic  0.95 us (1%)
  between operations  0.8 us (1%)
    pallas_call x8, Pallas kernels, call(): pl.pallas_call(kernel, in_specs=[smem] * scalars + [vmem] * (len(ins) - s...  23.7 us
    ppermute x14, starting transfers between devices, send(): return lax.ppermute(value, AXES, [(i, to(i) % count) for i in range(count)])  23.6 us
    ppermute x14, waiting for transfers between devices, send(): return lax.ppermute(value, AXES, [(i, to(i) % count) for i in range(count)])  21.7 us
    dynamic_slice x1, local copies, waits for them, and re-layouts, body(): sx = send(lax.dynamic_slice_in_dim(correlation, 1 - device % 2, 1, 0), swap)  1.78 us
  transfers between devices with their start and end apart: 14, of which 5 were waited for; matrix products, arithmetic and copies ran while one was open for 7% of the time, Pallas kernels for 20%

profile of v7, /device:TPU:1, one launch (start us, length us, event | category | flops | bytes accessed | tf_op | source)
XLA Modules:
  0.0 75.3 jit_solution(1502753722059814321)
XLA Ops:
  0.7 0.1 stack.2.meta
  0.8 2.1 %shard_map.59 = (f32[1,6,128,128]{3,2,1,0:T(8,128)}, f32[1,6,128,128]{3,2,1,0:T(8,128)}, f32[9,128,128]{2,1,0:T(8,128)S(1)}, f32[9,128,128]{2,1,0:T(8,128)S(1)}) custom-call(s32[16]{0:T(128)S(1)} %stack.2.meta, f32[2,6,128,128]{3,2,1,0:T(8,128)} %z.7), custom_call_target="tpu_custom_call" | custom-call | flops 1000 | bytes 4194304 | tf_op jit(solution)/shard_map/pallas_call | solution.py:464
  2.9 2.0 %collective-permute-start = (f32[1,6,128,128]{3,2,1,0:T(8,128)}, f32[1,6,128,128]{3,2,1,0:T(8,128)S(1)}, u32[]{:S(2)}, u32[]{:S(2)}) collective-permute-start(f32[1,6,128,128]{3,2,1,0:T(8,128)} %get-tuple-element.28), channel_id=1, source_target_pairs={{0,1},{1,0},{2,3},{3,2},{4,5},{5,4},{6,7},{7,6},{8,9},{9,8},{10,11... | collective-permute-start | bytes 1179656 | tf_op jit(solution)/shard_map/ppermute | solution.py:30
  5.0 0.0 collective-permute-start.1
  5.0 1.0 %collective-permute-start.4 = (f32[9,128,128]{2,1,0:T(8,128)S(1)}, f32[9,128,128]{2,1,0:T(8,128)S(1)}, u32[]{:S(2)}, u32[]{:S(2)}) collective-permute-start(f32[9,128,128]{2,1,0:T(8,128)S(1)} %get-tuple-element.30), channel_id=1, source_target_pairs={{0,2},{1,3},{2,0},{3,1},{4,6},{5,7},{6,4},{7,5},{8,10},{9,11},{10,... | collective-permute-start | bytes 1769480 | tf_op jit(solution)/shard_map/ppermute | solution.py:30
  5.9 1.6 %collective-permute-start.5 = (f32[9,128,128]{2,1,0:T(8,128)S(1)}, f32[9,128,128]{2,1,0:T(8,128)S(1)}, u32[]{:S(2)}, u32[]{:S(2)}) collective-permute-start(f32[9,128,128]{2,1,0:T(8,128)S(1)} %get-tuple-element.31), channel_id=1, source_target_pairs={{0,30},{1,31},{2,4},{3,5},{4,2},{5,3},{6,8},{7,9},{8,6},{9,7},{10,... | collective-permute-start | bytes 1769480 | tf_op jit(solution)/shard_map/ppermute | solution.py:30
  7.6 1.8 %constant_dynamic-slice_fusion = f32[1,6,128,128]{3,2,1,0:T(8,128)} fusion(f32[2,6,128,128]{3,2,1,0:T(8,128)} %s.1, s32[]{:T(128)S(6)} %select_n.66), kind=kLoop, calls=%fused_computation.22 | loop fusion | bytes 786436 | tf_op jit(solution)/shard_map/dynamic_slice | solution.py:491
  9.4 1.2 %collective-permute-start.6 = (f32[1,6,128,128]{3,2,1,0:T(8,128)}, f32[1,6,128,128]{3,2,1,0:T(8,128)S(1)}, u32[]{:S(2)}, u32[]{:S(2)}) collective-permute-start(f32[1,6,128,128]{3,2,1,0:T(8,128)} %constant_dynamic-slice_fusion), channel_id=1, source_target_pairs={{0,1},{1,0},{2,3},{3,2},{4,5},{5,4},{6,7},{7,6},{8,9},{9,8},{10,11... | collective-permute-start | bytes 1179656 | tf_op jit(solution)/shard_map/ppermute | solution.py:30
  10.6 1.4 %copy.8 = s32[64,6]{1,0:T(8,128)} copy(s32[64,6]{0,1:T(8,128)} %param.6) | data formatting | bytes 3072 | tf_op args[2]
  12.0 1.3 %gather_fusion = s32[14,6]{1,0:T(8,128)S(1)} fusion(s32[64,6]{1,0:T(8,128)} %copy.8, s32[1024]{0:T(1024)S(1)} %pad_clamp_fusion), kind=kCustom, calls=%fused_computation | custom fusion | bytes 728 | tf_op jit(solution)/shard_map/gather | solution.py:448
  13.3 0.7 collective-permute-done.x0
  14.0 3.8 %collective-permute-start.2 = (f32[1,6,128,128]{3,2,1,0:T(8,128)S(1)}, f32[1,6,128,128]{3,2,1,0:T(8,128)S(1)}, u32[]{:S(2)}, u32[]{:S(2)}) collective-permute-start(f32[1,6,128,128]{3,2,1,0:T(8,128)S(1)} %collective-permute-done.x0), channel_id=1, source_target_pairs={{0,2},{1,31},{2,4},{3,1},{4,6},{5,3},{6,8},{7,5},{8,10},{9,7},{10,... | collective-permute-start | bytes 1179656 | tf_op jit(solution)/shard_map/ppermute | solution.py:30
  17.8 4.7 %collective-permute-done.1.x1 = f32[1,6,128,128]{3,2,1,0:T(8,128)S(1)} collective-permute-done((f32[1,6,128,128]{3,2,1,0:T(8,128)}, f32[1,6,128,128]{3,2,1,0:T(8,128)S(1)}, u32[]{:S(2)}, u32[]{:S(2)}) %collective-permute-start.1) | collective-permute-done | bytes 393248 | tf_op jit(solution)/shard_map/ppermute | solution.py:30
  22.4 3.8 %collective-permute-start.3 = (f32[1,6,128,128]{3,2,1,0:T(8,128)S(1)}, f32[1,6,128,128]{3,2,1,0:T(8,128)S(1)}, u32[]{:S(2)}, u32[]{:S(2)}) collective-permute-start(f32[1,6,128,128]{3,2,1,0:T(8,128)S(1)} %collective-permute-done.1.x1), channel_id=1, source_target_pairs={{0,2},{1,31},{2,4},{3,1},{4,6},{5,3},{6,8},{7,5},{8,10},{9,7},{10,... | collective-permute-start | bytes 1179656 | tf_op jit(solution)/shard_map/ppermute | solution.py:30
  26.2 0.8 %convert_reduce_fusion = s32[14]{0:T(128)S(1)} fusion(s32[14,6]{1,0:T(8,128)S(1)} %gather_fusion, s32[5]{0:T(128)} %constant.83.clone, s32[14]{0:T(128)S(1)} %and_select_fusion), kind=kLoop, calls=%fused_computation.9 | loop fusion | flops 1176 | bytes 412 | tf_op jit(solution)/shard_map/reduce_sum | solution.py:450
  27.0 0.1 pad_add_fusion.meta
  27.1 2.3 %shard_map.62 = (bf16[8,128,1024]{2,1,0:T(8,128)(2,1)S(1)}, bf16[8,128,1024]{2,1,0:T(8,128)(2,1)S(1)}, bf16[2,128,1024]{2,1,0:T(8,128)(2,1)S(1)}, bf16[2,128,1024]{2,1,0:T(8,128)(2,1)S(1)}) custom-call(s32[16]{0:T(128)S(1)} %pad_add_fusion.meta, f32[2,6,128,128]{3,2,1,0:T(8,128)} %s.1, f32[2,6,128,128]{3,2,1,0:T(8,128)} %z.7, ...), custom_call_target="tpu_custom_call" | custom-call | flops 1000000000 | bytes 4194304 | tf_op jit(solution)/shard_map/pallas_call | solution.py:464
  29.5 0.0 collective-permute-done.4.zi
  29.5 0.0 collective-permute-done.5.zc
  29.5 0.0 collective-permute-done.2.n0
  29.5 1.4 %collective-permute-done.3.n1 = f32[1,6,128,128]{3,2,1,0:T(8,128)S(1)} collective-permute-done((f32[1,6,128,128]{3,2,1,0:T(8,128)S(1)}, f32[1,6,128,128]{3,2,1,0:T(8,128)S(1)}, u32[]{:S(2)}, u32[]{:S(2)}) %collective-permute-start.3) | collective-permute-done | bytes 393248 | tf_op jit(solution)/shard_map/ppermute | solution.py:30
  30.9 2.9 %shard_map.63 = (f32[1,6,128,128]{3,2,1,0:T(8,128)S(1)}, f32[1,6,128,128]{3,2,1,0:T(8,128)S(1)}, f32[1,6,128,128]{3,2,1,0:T(8,128)S(1)}, f32[7,128,128]{2,1,0:T(...) custom-call(s32[16]{0:T(128)S(1)} %pad_add_fusion.meta, ...), custom_call_target="tpu_custom_call", output_to_operand_aliasing={{5}: (1, {}), {6}: (2, {})} | custom-call | flops 2000000000 | bytes 4194304 | tf_op jit(solution)/shard_map/pallas_call | solution.py:464
  33.8 2.3 %collective-permute-start.7 = (f32[1,6,128,128]{3,2,1,0:T(8,128)S(1)}, f32[1,6,128,128]{3,2,1,0:T(8,128)S(1)}, u32[]{:S(2)}, u32[]{:S(2)}) collective-permute-start(f32[1,6,128,128]{3,2,1,0:T(8,128)S(1)} %get-tuple-element.44), channel_id=1, source_target_pairs={{0,1},{1,0},{2,3},{3,2},{4,5},{5,4},{6,7},{7,6},{8,9},{9,8},{10,11... | collective-permute-start | bytes 1179656 | tf_op jit(solution)/shard_map/ppermute | solution.py:30
  36.1 1.3 %collective-permute-start.8 = (f32[7,128,128]{2,1,0:T(8,128)S(1)}, f32[7,128,128]{2,1,0:T(8,128)S(1)}, u32[]{:S(2)}, u32[]{:S(2)}) collective-permute-start(f32[7,128,128]{2,1,0:T(8,128)S(1)} %get-tuple-element.49), channel_id=1, source_target_pairs={{0,2},{1,3},{2,0},{3,1},{4,6},{5,7},{6,4},{7,5},{8,10},{9,11},{10,... | collective-permute-start | bytes 1376264 | tf_op jit(solution)/shard_map/ppermute | solution.py:30
  37.4 0.0 collective-permute-start.9
  37.4 0.0 collective-permute-done.6.s
  37.5 2.5 %shard_map.60.after.nearer = f32[1,6,128,128]{3,2,1,0:T(8,128)S(1)} custom-call(s32[16]{0:T(128)S(1)} %pad_add_fusion.meta, f32[1,6,128,128]{3,2,1,0:T(8,128)S(1)} %collective-permute-done.6.s, f32[2,6,128,128]{3,2,1,0:T(8,128)} %z.7, f32[1,6,128,128]{3,2,1,0:T(8,128)S(1)} %collective-permute-done.x0, f32[1,6,128,128]{3,2,1,0:T(8,128)S(1)} %collective-permute-done.1.x1, ...), custom_call_target="tpu_custom_call" | custom-call | flops 2000000000 | bytes 4194304 | tf_op jit(solution)/shard_map/pallas_call | solution.py:464
  39.9 1.8 %collective-permute-start.10 = (f32[1,6,128,128]{3,2,1,0:T(8,128)S(1)}, f32[1,6,128,128]{3,2,1,0:T(8,128)S(1)}, u32[]{:S(2)}, u32[]{:S(2)}) collective-permute-start(f32[1,6,128,128]{3,2,1,0:T(8,128)S(1)} %shard_map.60.after.nearer), channel_id=1, source_target_pairs={{0,2},{1,31},{2,4},{3,1},{4,6},{5,3},{6,8},{7,5},{8,10},{9,7},{10,... | collective-permute-start | bytes 1179656 | tf_op jit(solution)/shard_map/ppermute | solution.py:30
  41.7 2.3 %shard_map.61 = (f32[2,6,128,128]{3,2,1,0:T(8,128)S(1)}, bf16[1024,512]{1,0:T(8,128)(2,1)S(1)}, bf16[512,512]{1,0:T(8,128)(2,1)S(1)}, bf16[512,512]{1,0:T(8,128)...) custom-call(s32[16]{0:T(128)S(1)} %pad_add_fusion.meta, ...), custom_call_target="tpu_custom_call" | custom-call | flops 2000000000 | bytes 4194304 | tf_op jit(solution)/shard_map/pallas_call | solution.py:464
  44.0 0.0 collective-permute-done.7.farther
  44.1 2.9 %collective-permute-start.11 = (f32[1,6,128,128]{3,2,1,0:T(8,128)S(1)}, f32[1,6,128,128]{3,2,1,0:T(8,128)S(1)}, u32[]{:S(2)}, u32[]{:S(2)}) collective-permute-start(f32[1,6,128,128]{3,2,1,0:T(8,128)S(1)} %collective-permute-done.7.farther), channel_id=1, source_target_pairs={{0,2},{1,31},{2,4},{3,1},{4,6},{5,3},{6,8},{7,5},{8,10},{9,7},{10,... | collective-permute-start | bytes 1179656 | tf_op jit(solution)/shard_map/ppermute | solution.py:30
  47.0 3.4 %shard_map.64.early = f32[16,256,256]{2,1,0:T(8,128)S(1)} custom-call(s32[16]{0:T(128)S(1)} %pad_add_fusion.meta, bf16[1024,512]{1,0:T(8,128)(2,1)S(1)} %get-tuple-element.36.t_own, bf16[768,512]{1,0:T(8,128)(2,1)S(1)} %get-tuple-element.37.t_swap, f32[1,6,128,128]{3,2,1,0:T(8,128)S(1)} %get-tuple-element.42.p0, ...), custom_call_target="tpu_custom_call" | custom-call | flops 4000000000 | bytes 4194304 | tf_op jit(solution)/shard_map/pallas_call | solution.py:464
  50.4 0.0 collective-permute-done.8.pi
  50.4 8.3 %collective-permute-done.9.pc = f32[7,128,128]{2,1,0:T(8,128)S(1)} collective-permute-done((f32[7,128,128]{2,1,0:T(8,128)S(1)}, f32[7,128,128]{2,1,0:T(8,128)S(1)}, u32[]{:S(2)}, u32[]{:S(2)}) %collective-permute-start.9) | collective-permute-done | bytes 458784 | tf_op jit(solution)/shard_map/ppermute | solution.py:30
  58.7 2.0 %shard_map.65 = (f32[8,256,256]{2,1,0:T(8,128)S(1)}, f32[256,256]{1,0:T(8,128)S(1)}, f32[256,256]{1,0:T(8,128)S(1)}) custom-call(s32[16]{0:T(128)S(1)} %pad_add_fusion.meta, bf16[512,512]{1,0:T(8,128)(2,1)S(1)} %get-tuple-element.45.t_up, bf16[512,512]{1,0:T(8,128)(2,1)S(1)} %get-tuple-element.46.t_down, bf16[256,512]{1,0:T(8,128)(2,1)S(1)} %get-tuple-element.47.t_far_up, ...), custom_call_target="tpu_custom_call" | custom-call | flops 1000000000 | bytes 4194304 | tf_op jit(solution)/shard_map/pallas_call | solution.py:464
  60.7 0.1 collective-permute-start.12
  60.8 1.7 %collective-permute-start.13 = (f32[256,256]{1,0:T(8,128)S(1)}, f32[256,256]{1,0:T(8,128)S(1)}, u32[]{:S(2)}, u32[]{:S(2)}) collective-permute-start(f32[256,256]{1,0:T(8,128)S(1)} %get-tuple-element.53), channel_id=1, source_target_pairs={{0,4},{1,3},{2,1},{3,2},{4,8},{5,7},{6,5},{7,6},{8,12},{9,11},{10,... | collective-permute-start | bytes 786440 | tf_op jit(solution)/shard_map/ppermute | solution.py:30
  62.5 0.0 collective-permute-done.10.nearer
  62.5 6.6 %collective-permute-done.12.first = f32[256,256]{1,0:T(8,128)S(1)} collective-permute-done((f32[256,256]{1,0:T(8,128)S(1)}, f32[256,256]{1,0:T(8,128)S(1)}, u32[]{:S(2)}, u32[]{:S(2)}) %collective-permute-start.12) | collective-permute-done | bytes 262176 | tf_op jit(solution)/shard_map/ppermute | solution.py:30
  69.1 0.0 collective-permute-done.13.second
  69.1 0.0 collective-permute-done.11.farther
  69.1 6.2 %shard_map.66 = (f32[2,6,128,128]{3,2,1,0:T(8,128)}, f32[2,6,128,128]{3,2,1,0:T(8,128)}) custom-call(s32[16]{0:T(128)S(1)} %pad_add_fusion.meta, f32[2,6,128,128]{3,2,1,0:T(8,128)S(1)} %get-tuple-element.32.z, bf16[2,128,1024]{2,1,0:T(8,128)(2,1)S(1)} %get-tuple-element.33.z_high, bf16[2,128,1024]{2,1,0:T(8,128)(2,1)S(1)} %get-tuple-element.34.z_low, ...), custom_call_target="tpu_custom_call" | custom-call | flops 4000000000 | bytes 4194304 | tf_op jit(solution)/shard_map/pallas_call | solution.py:464
  (6 shorter events, 0.0 us)
Async XLA Ops:
  2.9 11.1 %collective-permute-start = (f32[1,6,128,128]{3,2,1,0:T(8,128)}, f32[1,6,128,128]{3,2,1,0:T(8,128)S(1)}, u32[]{:S(2)}, u32[]{:S(2)}) collective-permute-start(f32[1,6,128,128]{3,2,1,0:T(8,128)} %get-tuple-element.28), channel_id=1, source_target_pairs={{0,1},{1,0},{2,3},{3,2},{4,5},{5,4},{6,7},{7,6},{8,9},{9,8},{10,11... | collective-permute-start | bytes 1179656 | tf_op jit(solution)/shard_map/ppermute | solution.py:30
  5.0 17.4 %collective-permute-start.1 = (f32[1,6,128,128]{3,2,1,0:T(8,128)}, f32[1,6,128,128]{3,2,1,0:T(8,128)S(1)}, u32[]{:S(2)}, u32[]{:S(2)}) collective-permute-start(f32[1,6,128,128]{3,2,1,0:T(8,128)} %get-tuple-element.29), channel_id=1, source_target_pairs={{0,1},{1,0},{2,3},{3,2},{4,5},{5,4},{6,7},{7,6},{8,9},{9,8},{10,11... | collective-permute-start | bytes 1179656 | tf_op jit(solution)/shard_map/ppermute | solution.py:30
  5.0 24.5 %collective-permute-start.4 = (f32[9,128,128]{2,1,0:T(8,128)S(1)}, f32[9,128,128]{2,1,0:T(8,128)S(1)}, u32[]{:S(2)}, u32[]{:S(2)}) collective-permute-start(f32[9,128,128]{2,1,0:T(8,128)S(1)} %get-tuple-element.30), channel_id=1, source_target_pairs={{0,2},{1,3},{2,0},{3,1},{4,6},{5,7},{6,4},{7,5},{8,10},{9,11},{10,... | collective-permute-start | bytes 1769480 | tf_op jit(solution)/shard_map/ppermute | solution.py:30
  5.9 23.5 %collective-permute-start.5 = (f32[9,128,128]{2,1,0:T(8,128)S(1)}, f32[9,128,128]{2,1,0:T(8,128)S(1)}, u32[]{:S(2)}, u32[]{:S(2)}) collective-permute-start(f32[9,128,128]{2,1,0:T(8,128)S(1)} %get-tuple-element.31), channel_id=1, source_target_pairs={{0,30},{1,31},{2,4},{3,5},{4,2},{5,3},{6,8},{7,9},{8,6},{9,7},{10,... | collective-permute-start | bytes 1769480 | tf_op jit(solution)/shard_map/ppermute | solution.py:30
  9.4 28.1 %collective-permute-start.6 = (f32[1,6,128,128]{3,2,1,0:T(8,128)}, f32[1,6,128,128]{3,2,1,0:T(8,128)S(1)}, u32[]{:S(2)}, u32[]{:S(2)}) collective-permute-start(f32[1,6,128,128]{3,2,1,0:T(8,128)} %constant_dynamic-slice_fusion), channel_id=1, source_target_pairs={{0,1},{1,0},{2,3},{3,2},{4,5},{5,4},{6,7},{7,6},{8,9},{9,8},{10,11... | collective-permute-start | bytes 1179656 | tf_op jit(solution)/shard_map/ppermute | solution.py:30
  14.0 15.5 %collective-permute-start.2 = (f32[1,6,128,128]{3,2,1,0:T(8,128)S(1)}, f32[1,6,128,128]{3,2,1,0:T(8,128)S(1)}, u32[]{:S(2)}, u32[]{:S(2)}) collective-permute-start(f32[1,6,128,128]{3,2,1,0:T(8,128)S(1)} %collective-permute-done.x0), channel_id=1, source_target_pairs={{0,2},{1,31},{2,4},{3,1},{4,6},{5,3},{6,8},{7,5},{8,10},{9,7},{10,... | collective-permute-start | bytes 1179656 | tf_op jit(solution)/shard_map/ppermute | solution.py:30
  22.4 8.5 %collective-permute-start.3 = (f32[1,6,128,128]{3,2,1,0:T(8,128)S(1)}, f32[1,6,128,128]{3,2,1,0:T(8,128)S(1)}, u32[]{:S(2)}, u32[]{:S(2)}) collective-permute-start(f32[1,6,128,128]{3,2,1,0:T(8,128)S(1)} %collective-permute-done.1.x1), channel_id=1, source_target_pairs={{0,2},{1,31},{2,4},{3,1},{4,6},{5,3},{6,8},{7,5},{8,10},{9,7},{10,... | collective-permute-start | bytes 1179656 | tf_op jit(solution)/shard_map/ppermute | solution.py:30
  33.8 10.3 %collective-permute-start.7 = (f32[1,6,128,128]{3,2,1,0:T(8,128)S(1)}, f32[1,6,128,128]{3,2,1,0:T(8,128)S(1)}, u32[]{:S(2)}, u32[]{:S(2)}) collective-permute-start(f32[1,6,128,128]{3,2,1,0:T(8,128)S(1)} %get-tuple-element.44), channel_id=1, source_target_pairs={{0,1},{1,0},{2,3},{3,2},{4,5},{5,4},{6,7},{7,6},{8,9},{9,8},{10,11... | collective-permute-start | bytes 1179656 | tf_op jit(solution)/shard_map/ppermute | solution.py:30
  36.1 14.3 %collective-permute-start.8 = (f32[7,128,128]{2,1,0:T(8,128)S(1)}, f32[7,128,128]{2,1,0:T(8,128)S(1)}, u32[]{:S(2)}, u32[]{:S(2)}) collective-permute-start(f32[7,128,128]{2,1,0:T(8,128)S(1)} %get-tuple-element.49), channel_id=1, source_target_pairs={{0,2},{1,3},{2,0},{3,1},{4,6},{5,7},{6,4},{7,5},{8,10},{9,11},{10,... | collective-permute-start | bytes 1376264 | tf_op jit(solution)/shard_map/ppermute | solution.py:30
  37.4 21.2 %collective-permute-start.9 = (f32[7,128,128]{2,1,0:T(8,128)S(1)}, f32[7,128,128]{2,1,0:T(8,128)S(1)}, u32[]{:S(2)}, u32[]{:S(2)}) collective-permute-start(f32[7,128,128]{2,1,0:T(8,128)S(1)} %get-tuple-element.50), channel_id=1, source_target_pairs={{0,30},{1,31},{2,4},{3,5},{4,2},{5,3},{6,8},{7,9},{8,6},{9,7},{10,... | collective-permute-start | bytes 1376264 | tf_op jit(solution)/shard_map/ppermute | solution.py:30
  39.9 22.6 %collective-permute-start.10 = (f32[1,6,128,128]{3,2,1,0:T(8,128)S(1)}, f32[1,6,128,128]{3,2,1,0:T(8,128)S(1)}, u32[]{:S(2)}, u32[]{:S(2)}) collective-permute-start(f32[1,6,128,128]{3,2,1,0:T(8,128)S(1)} %shard_map.60.after.nearer), channel_id=1, source_target_pairs={{0,2},{1,31},{2,4},{3,1},{4,6},{5,3},{6,8},{7,5},{8,10},{9,7},{10,... | collective-permute-start | bytes 1179656 | tf_op jit(solution)/shard_map/ppermute | solution.py:30
  44.1 25.1 %collective-permute-start.11 = (f32[1,6,128,128]{3,2,1,0:T(8,128)S(1)}, f32[1,6,128,128]{3,2,1,0:T(8,128)S(1)}, u32[]{:S(2)}, u32[]{:S(2)}) collective-permute-start(f32[1,6,128,128]{3,2,1,0:T(8,128)S(1)} %collective-permute-done.7.farther), channel_id=1, source_target_pairs={{0,2},{1,31},{2,4},{3,1},{4,6},{5,3},{6,8},{7,5},{8,10},{9,7},{10,... | collective-permute-start | bytes 1179656 | tf_op jit(solution)/shard_map/ppermute | solution.py:30
  60.7 8.4 %collective-permute-start.12 = (f32[256,256]{1,0:T(8,128)S(1)}, f32[256,256]{1,0:T(8,128)S(1)}, u32[]{:S(2)}, u32[]{:S(2)}) collective-permute-start(f32[256,256]{1,0:T(8,128)S(1)} %get-tuple-element.52), channel_id=1, source_target_pairs={{0,1},{1,2},{2,0},{3,31},{4,5},{5,6},{6,4},{7,3},{8,9},{9,10},{10,... | collective-permute-start | bytes 786440 | tf_op jit(solution)/shard_map/ppermute | solution.py:30
  60.8 8.4 %collective-permute-start.13 = (f32[256,256]{1,0:T(8,128)S(1)}, f32[256,256]{1,0:T(8,128)S(1)}, u32[]{:S(2)}, u32[]{:S(2)}) collective-permute-start(f32[256,256]{1,0:T(8,128)S(1)} %get-tuple-element.53), channel_id=1, source_target_pairs={{0,4},{1,3},{2,1},{3,2},{4,8},{5,7},{6,5},{7,6},{8,12},{9,11},{10,... | collective-permute-start | bytes 786440 | tf_op jit(solution)/shard_map/ppermute | solution.py:30

commit v8 on v7

--- a/solution.py
+++ b/solution.py
@@ -189,9 +189,17 @@
     return jnp.where(present, value, 0.0)
 
 
+def tiles_of(tile, columns=range(PAIRS)):
+    for b in columns:
+        for a in range(max(0, b - 2), min(PAIRS, b + 3)):
+            for i in range(2):
+                for j in range(2):
+                    yield a, b, 2 * a + i, 2 * b + j, (pl.ds(i * tile, tile), pl.ds(j * tile, tile))
+
+
 def edge_kernel(
-    meta, t_up, t_down, t_far_up, t_far_down, pi, pc, nearer, farther, early, edge, first, second,
-    high, low, far_high, far_low,
+    meta, t_up, t_down, t_far_up, t_far_down, pi, pc, nearer, farther, early, base, first, second,
+    high, low, far_high, far_low, edge,
 ):
     tile = nearer.shape[-1]
     rows = Rows(meta)
@@ -227,6 +235,23 @@
     def _():
         far_block(t_far_down, -1, first)
         second[...] = edge[4]
+
+    eye = (
+        lax.broadcasted_iota(jnp.int32, (tile, tile), 0) == lax.broadcasted_iota(jnp.int32, (tile, tile), 1)
+    ).astype(F32)
+    for a, b, k, c, inner in tiles_of(tile):
+        gram = early[PAIRS * a + b, inner[0], inner[1]]
+        e = a if b < 2 else a - 2
+        if 0 <= e < 2:
+            gram = gram + edge[2 * b + e, inner[0], inner[1]]
+        value = -gram
+        if k == c:
+            value = value + eye
+        elif abs(k - c) <= REACH:
+            value = jnp.where(rows.present(k + COL0, c + COL0), value, 0.0)
+        else:
+            value = zero(tile)
+        base[PAIRS * a + b, inner[0], inner[1]] = value
 
 
 def prepare_kernel(meta, s, z, x0, x1, z_high, z_low, s_high, s_low):
@@ -366,6 +391,7 @@
         block = dot3(*left, flat(high, slice(0, 2), n), flat(low, slice(0, 2), n))
         for a in range(SIDE):
             add(a, b, block[2 * a * tile : (2 * a + 2) * tile])
+        yield
 
 
 def gram_kernel(meta, t_own, t_swap, p0, p1, nearer, farther, gram, high, low, side_high, side_low):
@@ -386,57 +412,67 @@
         index = PAIRS * a + b + (PAIRS + 1) * rows.side_pair(0)
         gram[index] = gram[index] + value
 
-    side_gram(rows, 0, (nearer, farther), t_swap, side_high, side_low, add, tile)
+    for _ in side_gram(rows, 0, (nearer, farther), t_swap, side_high, side_low, add, tile):
+        pass
 
 
 def refine_kernel(
-    meta, z, z_high, z_low, t_near, early, edge, nearer, farther, first, second, refined, correction,
-    high, low, late, d_high, d_low, d_own, update,
+    meta, z, z_high, z_low, t_near, base, nearer, farther, first, second, refined, correction,
+    high, low, late, d_high, d_low, d_own, update, d_out, z_out, sems,
 ):
     tile = z.shape[-1]
     rows = Rows(meta)
     ends = rows.parity != jnp.where(rows.even_pair, 0, 1)
+    shift = rows.side_pair(1)
 
     def add(a, b, value):
         late[SIDE * a + b] = value
 
-    side_gram(rows, 1, (nearer, farther), t_near, high, low, add, tile)
-    eye = (
-        lax.broadcasted_iota(jnp.int32, (tile, tile), 0) == lax.broadcasted_iota(jnp.int32, (tile, tile), 1)
-    ).astype(F32)
-    shift = rows.side_pair(1)
-    for b in range(PAIRS):
-        for a in range(max(0, b - 2), min(PAIRS, b + 3)):
-            gram = early[PAIRS * a + b]
-            ia, ib = a - shift, b - shift
-            there = (ia >= 0) & (ia < SIDE) & (ib >= 0) & (ib < SIDE)
-            part = late[jnp.clip(SIDE * ia + ib, 0, SIDE * SIDE - 1)]
-            always = 0 < a < SIDE and 0 < b < SIDE
-            gram = gram + (part if always else jnp.where(there, part, 0.0))
-            e = a if b < 2 else a - 2
-            if 0 <= e < 2:
-                gram = gram + edge[2 * b + e]
-            if a == b and a in (0, PAIRS - 1):
-                one, other = (first, second) if a == 0 else (second, first)
-                gram = gram + jnp.where(ends, one[...], other[...])
-            for i in range(2):
-                for j in range(2):
-                    k, c = 2 * a + i, 2 * b + j
-                    value = -gram[i * tile : (i + 1) * tile, j * tile : (j + 1) * tile]
-                    if k == c:
-                        value = value + eye
-                    elif abs(k - c) <= REACH:
-                        value = jnp.where(rows.present(k + COL0, c + COL0), value, 0.0)
-                    else:
-                        value = zero(tile)
-                    put(d_high, d_low, k, c, tile, value)
-                    if k + COL0 in (0, 1):
-                        d_own[k + COL0, c] = value
-        row_matmul(z_high, z_low, d_high, d_low, update, tile, (2 * b,))
+    def finish(column):
+        for a, b, k, c, inner in tiles_of(tile, (column,)):
+            value = base[PAIRS * a + b, inner[0], inner[1]]
+            if abs(k - c) <= REACH:
+                ia, ib = a - shift, b - shift
+                there = rows.present(k + COL0, c + COL0)
+                if not (0 < a < SIDE and 0 < b < SIDE):
+                    there = there & (ia >= 0) & (ia < SIDE) & (ib >= 0) & (ib < SIDE)
+                gram = late[jnp.clip(SIDE * ia + ib, 0, SIDE * SIDE - 1), inner[0], inner[1]]
+                value = value - jnp.where(there, gram, 0.0)
+                if a == b and a in (0, PAIRS - 1):
+                    one, other = (first, second) if a == 0 else (second, first)
+                    far = jnp.where(ends, one[inner[0], inner[1]], other[inner[0], inner[1]])
+                    value = value - (far if k == c else jnp.where(rows.present(k + COL0, c + COL0), far, 0.0))
+            put(d_high, d_low, k, c, tile, value)
+            if k + COL0 in (0, 1):
+                d_own[k + COL0, c] = value
+
+    def multiply(column):
+        row_matmul(z_high, z_low, d_high, d_low, update, tile, (2 * column,))
+
+    steps = side_gram(rows, 1, (nearer, farther), t_near, high, low, add, tile)
+    next(steps)
+    next(steps)
+    finish(0)
+    next(steps)
+    finish(1)
+    multiply(0)
+    finish(2)
+    multiply(1)
+    finish(3)
+    multiply(2)
     for i in range(OWN):
         for slot in range(2 * REACH):
-            correction[i, slot] = d_own[i, rows.dense_slot(i, slot)]
-            refined[i, slot] = z[i, slot] + 0.5 * update[i, rows.dense_slot(i, slot)]
+            d_out[i, slot] = d_own[i, rows.dense_slot(i, slot)]
+    copies = [pltpu.make_async_copy(d_out, correction, sems.at[OWN])]
+    copies[0].start()
+    multiply(3)
+    for i in range(OWN):
+        for slot in range(2 * REACH):
+            z_out[i, slot] = z[i, slot] + 0.5 * update[i, rows.dense_slot(i, slot)]
+        copies.append(pltpu.make_async_copy(z_out.at[i], refined.at[i], sems.at[i]))
+        copies[-1].start()
+    for copy in copies:
+        copy.wait()
 
 
 def body(correlation, factor, pattern):
@@ -459,12 +495,12 @@
             return pltpu.with_memory_space_constraint(value, pltpu.HBM)
         return pltpu.with_memory_space_constraint(value, pltpu.VMEM)
 
-    def call(kernel, ins, outs, scratch, flops, aliases={}):
+    def call(kernel, ins, outs, scratch, flops, aliases={}, where=pltpu.VMEM):
         scalars = 1
         return pl.pallas_call(
             kernel,
             in_specs=[smem] * scalars + [vmem] * (len(ins) - scalars),
-            out_specs=jax.tree.map(lambda _: vmem, outs),
+            out_specs=jax.tree.map(lambda _: pl.BlockSpec(memory_space=where), outs),
             out_shape=outs,
             scratch_shapes=scratch,
             input_output_aliases=aliases,
@@ -531,23 +567,24 @@
         halves_of(2, COLS) + halves_of(2, 2 * SIDE),
         int(4e9),
     )
-    edge, *far = call(
+    base, *far = call(
         edge_kernel,
         (meta, t_up, t_down, t_far_up, t_far_down, pi, pc, ps, px, early),
-        (shape(2 * PAIRS, 2 * tile, 2 * tile), block, block),
-        halves_of(2, COLS) + halves_of(2, 2),
+        (shape(PAIRS * PAIRS, 2 * tile, 2 * tile), block, block),
+        halves_of(2, COLS) + halves_of(2, 2) + [pltpu.VMEM((2 * PAIRS, 2 * tile, 2 * tile), F32)],
         int(1e9),
     )
     far = (send(far[0], far_first), send(far[1], far_second))
     return call(
         refine_kernel,
-        (meta, z_kept, *z_own, t_near, early, edge, *pn, *far),
+        (meta, z_kept, *z_own, t_near, base, *pn, *far),
         (shape(*factor.shape), shape(*factor.shape)),
         halves_of(2, 2 * SIDE)
         + [pltpu.VMEM((SIDE * SIDE, 2 * tile, 2 * tile), F32)]
         + halves_of(COLS, COLS)
-        + [dense, dense],
+        + [dense, dense, pltpu.VMEM(factor.shape, F32), pltpu.VMEM(factor.shape, F32), pltpu.SemaphoreType.DMA((OWN + 1,))],
         int(4e9),
+        where=pl.ANY,
     )
 
 

time: 76.1 us -> 76.1 us (level)
  transfers between devices with their start and end apart: 14 -> 14, of which waited for: 5 -> 5; matrix products, arithmetic and copies ran while one was open for 7% -> 7% of each run, Pallas kernels for 20% -> 21%
where the time goes in v8:
time: 76.1 us; the launch traced here: 75.3 us
  starting transfers between devices  23.6 us (31%)
  Pallas kernels  23.5 us (31%)
  waiting for transfers between devices  21.7 us (29%)
  local copies, waits for them, and re-layouts  4.56 us (6%)
  between operations  0.96 us (1%)
  other arithmetic  0.95 us (1%)
    ppermute x14, starting transfers between devices, send(): return lax.ppermute(value, AXES, [(i, to(i) % count) for i in range(count)])  23.6 us
    pallas_call x8, Pallas kernels, call(): pl.pallas_call(kernel, in_specs=[smem] * scalars + [vmem] * (len(ins) - s...  23.5 us
    ppermute x14, waiting for transfers between devices, send(): return lax.ppermute(value, AXES, [(i, to(i) % count) for i in range(count)])  21.7 us
    dynamic_slice x1, local copies, waits for them, and re-layouts, body(): sx = send(lax.dynamic_slice_in_dim(correlation, 1 - device % 2, 1, 0), swap)  1.78 us
  transfers between devices with their start and end apart: 14, of which 5 were waited for; matrix products, arithmetic and copies ran while one was open for 7% of the time, Pallas kernels for 21%

profile of v8, /device:TPU:1, one launch (start us, length us, event | category | flops | bytes accessed | tf_op | source)
XLA Modules:
  0.0 75.3 jit_solution(16146686624202535435)
XLA Ops:
  0.7 0.1 stack.2.meta
  0.8 2.1 %shard_map.59 = (f32[1,6,128,128]{3,2,1,0:T(8,128)}, f32[1,6,128,128]{3,2,1,0:T(8,128)}, f32[9,128,128]{2,1,0:T(8,128)S(1)}, f32[9,128,128]{2,1,0:T(8,128)S(1)}) custom-call(s32[16]{0:T(128)S(1)} %stack.2.meta, f32[2,6,128,128]{3,2,1,0:T(8,128)} %z.7), custom_call_target="tpu_custom_call" | custom-call | flops 1000 | bytes 4194304 | tf_op jit(solution)/shard_map/pallas_call | solution.py:500
  2.9 2.0 %collective-permute-start = (f32[1,6,128,128]{3,2,1,0:T(8,128)}, f32[1,6,128,128]{3,2,1,0:T(8,128)S(1)}, u32[]{:S(2)}, u32[]{:S(2)}) collective-permute-start(f32[1,6,128,128]{3,2,1,0:T(8,128)} %get-tuple-element.28), channel_id=1, source_target_pairs={{0,1},{1,0},{2,3},{3,2},{4,5},{5,4},{6,7},{7,6},{8,9},{9,8},{10,11... | collective-permute-start | bytes 1179656 | tf_op jit(solution)/shard_map/ppermute | solution.py:30
  5.0 0.0 collective-permute-start.1
  5.0 1.0 %collective-permute-start.4 = (f32[9,128,128]{2,1,0:T(8,128)S(1)}, f32[9,128,128]{2,1,0:T(8,128)S(1)}, u32[]{:S(2)}, u32[]{:S(2)}) collective-permute-start(f32[9,128,128]{2,1,0:T(8,128)S(1)} %get-tuple-element.30), channel_id=1, source_target_pairs={{0,2},{1,3},{2,0},{3,1},{4,6},{5,7},{6,4},{7,5},{8,10},{9,11},{10,... | collective-permute-start | bytes 1769480 | tf_op jit(solution)/shard_map/ppermute | solution.py:30
  5.9 1.6 %collective-permute-start.5 = (f32[9,128,128]{2,1,0:T(8,128)S(1)}, f32[9,128,128]{2,1,0:T(8,128)S(1)}, u32[]{:S(2)}, u32[]{:S(2)}) collective-permute-start(f32[9,128,128]{2,1,0:T(8,128)S(1)} %get-tuple-element.31), channel_id=1, source_target_pairs={{0,30},{1,31},{2,4},{3,5},{4,2},{5,3},{6,8},{7,9},{8,6},{9,7},{10,... | collective-permute-start | bytes 1769480 | tf_op jit(solution)/shard_map/ppermute | solution.py:30
  7.6 1.8 %constant_dynamic-slice_fusion = f32[1,6,128,128]{3,2,1,0:T(8,128)} fusion(f32[2,6,128,128]{3,2,1,0:T(8,128)} %s.1, s32[]{:T(128)S(6)} %select_n.66), kind=kLoop, calls=%fused_computation.22 | loop fusion | bytes 786436 | tf_op jit(solution)/shard_map/dynamic_slice | solution.py:527
  9.4 1.2 %collective-permute-start.6 = (f32[1,6,128,128]{3,2,1,0:T(8,128)}, f32[1,6,128,128]{3,2,1,0:T(8,128)S(1)}, u32[]{:S(2)}, u32[]{:S(2)}) collective-permute-start(f32[1,6,128,128]{3,2,1,0:T(8,128)} %constant_dynamic-slice_fusion), channel_id=1, source_target_pairs={{0,1},{1,0},{2,3},{3,2},{4,5},{5,4},{6,7},{7,6},{8,9},{9,8},{10,11... | collective-permute-start | bytes 1179656 | tf_op jit(solution)/shard_map/ppermute | solution.py:30
  10.6 1.4 %copy.8 = s32[64,6]{1,0:T(8,128)} copy(s32[64,6]{0,1:T(8,128)} %param.6) | data formatting | bytes 3072 | tf_op args[2]
  12.0 1.3 %gather_fusion = s32[14,6]{1,0:T(8,128)S(1)} fusion(s32[64,6]{1,0:T(8,128)} %copy.8, s32[1024]{0:T(1024)S(1)} %pad_clamp_fusion), kind=kCustom, calls=%fused_computation | custom fusion | bytes 728 | tf_op jit(solution)/shard_map/gather | solution.py:484
  13.3 0.7 collective-permute-done.x0
  14.0 3.8 %collective-permute-start.2 = (f32[1,6,128,128]{3,2,1,0:T(8,128)S(1)}, f32[1,6,128,128]{3,2,1,0:T(8,128)S(1)}, u32[]{:S(2)}, u32[]{:S(2)}) collective-permute-start(f32[1,6,128,128]{3,2,1,0:T(8,128)S(1)} %collective-permute-done.x0), channel_id=1, source_target_pairs={{0,2},{1,31},{2,4},{3,1},{4,6},{5,3},{6,8},{7,5},{8,10},{9,7},{10,... | collective-permute-start | bytes 1179656 | tf_op jit(solution)/shard_map/ppermute | solution.py:30
  17.8 4.7 %collective-permute-done.1.x1 = f32[1,6,128,128]{3,2,1,0:T(8,128)S(1)} collective-permute-done((f32[1,6,128,128]{3,2,1,0:T(8,128)}, f32[1,6,128,128]{3,2,1,0:T(8,128)S(1)}, u32[]{:S(2)}, u32[]{:S(2)}) %collective-permute-start.1) | collective-permute-done | bytes 393248 | tf_op jit(solution)/shard_map/ppermute | solution.py:30
  22.4 3.8 %collective-permute-start.3 = (f32[1,6,128,128]{3,2,1,0:T(8,128)S(1)}, f32[1,6,128,128]{3,2,1,0:T(8,128)S(1)}, u32[]{:S(2)}, u32[]{:S(2)}) collective-permute-start(f32[1,6,128,128]{3,2,1,0:T(8,128)S(1)} %collective-permute-done.1.x1), channel_id=1, source_target_pairs={{0,2},{1,31},{2,4},{3,1},{4,6},{5,3},{6,8},{7,5},{8,10},{9,7},{10,... | collective-permute-start | bytes 1179656 | tf_op jit(solution)/shard_map/ppermute | solution.py:30
  26.2 0.8 %convert_reduce_fusion = s32[14]{0:T(128)S(1)} fusion(s32[14,6]{1,0:T(8,128)S(1)} %gather_fusion, s32[5]{0:T(128)} %constant.83.clone, s32[14]{0:T(128)S(1)} %and_select_fusion), kind=kLoop, calls=%fused_computation.9 | loop fusion | flops 1176 | bytes 412 | tf_op jit(solution)/shard_map/reduce_sum | solution.py:486
  27.0 0.1 pad_add_fusion.meta
  27.1 2.3 %shard_map.62 = (bf16[8,128,1024]{2,1,0:T(8,128)(2,1)S(1)}, bf16[8,128,1024]{2,1,0:T(8,128)(2,1)S(1)}, bf16[2,128,1024]{2,1,0:T(8,128)(2,1)S(1)}, bf16[2,128,1024]{2,1,0:T(8,128)(2,1)S(1)}) custom-call(s32[16]{0:T(128)S(1)} %pad_add_fusion.meta, f32[2,6,128,128]{3,2,1,0:T(8,128)} %s.1, f32[2,6,128,128]{3,2,1,0:T(8,128)} %z.7, ...), custom_call_target="tpu_custom_call" | custom-call | flops 1000000000 | bytes 4194304 | tf_op jit(solution)/shard_map/pallas_call | solution.py:500
  29.5 0.0 collective-permute-done.4.zi
  29.5 0.0 collective-permute-done.5.zc
  29.5 0.0 collective-permute-done.2.n0
  29.5 1.4 %collective-permute-done.3.n1 = f32[1,6,128,128]{3,2,1,0:T(8,128)S(1)} collective-permute-done((f32[1,6,128,128]{3,2,1,0:T(8,128)S(1)}, f32[1,6,128,128]{3,2,1,0:T(8,128)S(1)}, u32[]{:S(2)}, u32[]{:S(2)}) %collective-permute-start.3) | collective-permute-done | bytes 393248 | tf_op jit(solution)/shard_map/ppermute | solution.py:30
  30.9 2.9 %shard_map.63 = (f32[1,6,128,128]{3,2,1,0:T(8,128)S(1)}, f32[1,6,128,128]{3,2,1,0:T(8,128)S(1)}, f32[1,6,128,128]{3,2,1,0:T(8,128)S(1)}, f32[7,128,128]{2,1,0:T(...) custom-call(s32[16]{0:T(128)S(1)} %pad_add_fusion.meta, ...), custom_call_target="tpu_custom_call", output_to_operand_aliasing={{5}: (1, {}), {6}: (2, {})} | custom-call | flops 2000000000 | bytes 4194304 | tf_op jit(solution)/shard_map/pallas_call | solution.py:500
  33.8 2.3 %collective-permute-start.9 = (f32[1,6,128,128]{3,2,1,0:T(8,128)S(1)}, f32[1,6,128,128]{3,2,1,0:T(8,128)S(1)}, u32[]{:S(2)}, u32[]{:S(2)}) collective-permute-start(f32[1,6,128,128]{3,2,1,0:T(8,128)S(1)} %get-tuple-element.46), channel_id=1, source_target_pairs={{0,1},{1,0},{2,3},{3,2},{4,5},{5,4},{6,7},{7,6},{8,9},{9,8},{10,11... | collective-permute-start | bytes 1179656 | tf_op jit(solution)/shard_map/ppermute | solution.py:30
  36.1 1.3 %collective-permute-start.7 = (f32[7,128,128]{2,1,0:T(8,128)S(1)}, f32[7,128,128]{2,1,0:T(8,128)S(1)}, u32[]{:S(2)}, u32[]{:S(2)}) collective-permute-start(f32[7,128,128]{2,1,0:T(8,128)S(1)} %get-tuple-element.44), channel_id=1, source_target_pairs={{0,2},{1,3},{2,0},{3,1},{4,6},{5,7},{6,4},{7,5},{8,10},{9,11},{10,... | collective-permute-start | bytes 1376264 | tf_op jit(solution)/shard_map/ppermute | solution.py:30
  37.4 0.0 collective-permute-start.8
  37.4 0.0 collective-permute-done.6.s
  37.5 2.5 %shard_map.60.after.nearer = f32[1,6,128,128]{3,2,1,0:T(8,128)S(1)} custom-call(s32[16]{0:T(128)S(1)} %pad_add_fusion.meta, f32[1,6,128,128]{3,2,1,0:T(8,128)S(1)} %collective-permute-done.6.s, f32[2,6,128,128]{3,2,1,0:T(8,128)} %z.7, f32[1,6,128,128]{3,2,1,0:T(8,128)S(1)} %collective-permute-done.x0, f32[1,6,128,128]{3,2,1,0:T(8,128)S(1)} %collective-permute-done.1.x1, ...), custom_call_target="tpu_custom_call" | custom-call | flops 2000000000 | bytes 4194304 | tf_op jit(solution)/shard_map/pallas_call | solution.py:500
  39.9 1.8 %collective-permute-start.10 = (f32[1,6,128,128]{3,2,1,0:T(8,128)S(1)}, f32[1,6,128,128]{3,2,1,0:T(8,128)S(1)}, u32[]{:S(2)}, u32[]{:S(2)}) collective-permute-start(f32[1,6,128,128]{3,2,1,0:T(8,128)S(1)} %shard_map.60.after.nearer), channel_id=1, source_target_pairs={{0,2},{1,31},{2,4},{3,1},{4,6},{5,3},{6,8},{7,5},{8,10},{9,7},{10,... | collective-permute-start | bytes 1179656 | tf_op jit(solution)/shard_map/ppermute | solution.py:30
  41.7 2.3 %shard_map.61 = (f32[2,6,128,128]{3,2,1,0:T(8,128)S(1)}, bf16[1024,512]{1,0:T(8,128)(2,1)S(1)}, bf16[512,512]{1,0:T(8,128)(2,1)S(1)}, bf16[512,512]{1,0:T(8,128)...) custom-call(s32[16]{0:T(128)S(1)} %pad_add_fusion.meta, ...), custom_call_target="tpu_custom_call" | custom-call | flops 2000000000 | bytes 4194304 | tf_op jit(solution)/shard_map/pallas_call | solution.py:500
  44.0 0.0 collective-permute-done.9.farther
  44.1 2.9 %collective-permute-start.11 = (f32[1,6,128,128]{3,2,1,0:T(8,128)S(1)}, f32[1,6,128,128]{3,2,1,0:T(8,128)S(1)}, u32[]{:S(2)}, u32[]{:S(2)}) collective-permute-start(f32[1,6,128,128]{3,2,1,0:T(8,128)S(1)} %collective-permute-done.9.farther), channel_id=1, source_target_pairs={{0,2},{1,31},{2,4},{3,1},{4,6},{5,3},{6,8},{7,5},{8,10},{9,7},{10,... | collective-permute-start | bytes 1179656 | tf_op jit(solution)/shard_map/ppermute | solution.py:30
  47.0 3.4 %shard_map.64.early = f32[16,256,256]{2,1,0:T(8,128)S(1)} custom-call(s32[16]{0:T(128)S(1)} %pad_add_fusion.meta, bf16[1024,512]{1,0:T(8,128)(2,1)S(1)} %get-tuple-element.47.t_own, bf16[768,512]{1,0:T(8,128)(2,1)S(1)} %get-tuple-element.48.t_swap, f32[1,6,128,128]{3,2,1,0:T(8,128)S(1)} %get-tuple-element.49.p0, ...), custom_call_target="tpu_custom_call" | custom-call | flops 4000000000 | bytes 4194304 | tf_op jit(solution)/shard_map/pallas_call | solution.py:500
  50.4 0.0 collective-permute-done.7.pi
  50.4 8.3 %collective-permute-done.8.pc = f32[7,128,128]{2,1,0:T(8,128)S(1)} collective-permute-done((f32[7,128,128]{2,1,0:T(8,128)S(1)}, f32[7,128,128]{2,1,0:T(8,128)S(1)}, u32[]{:S(2)}, u32[]{:S(2)}) %collective-permute-start.8) | collective-permute-done | bytes 458784 | tf_op jit(solution)/shard_map/ppermute | solution.py:30
  58.7 2.4 %shard_map.65 = (f32[16,256,256]{2,1,0:T(8,128)S(1)}, f32[256,256]{1,0:T(8,128)S(1)}, f32[256,256]{1,0:T(8,128)S(1)}) custom-call(s32[16]{0:T(128)S(1)} %pad_add_fusion.meta, bf16[512,512]{1,0:T(8,128)(2,1)S(1)} %get-tuple-element.36.t_up, bf16[512,512]{1,0:T(8,128)(2,1)S(1)} %get-tuple-element.37.t_down, bf16[256,512]{1,0:T(8,128)(2,1)S(1)} %get-tuple-element.38.t_far_up, ...), custom_call_target="tpu_custom_call" | custom-call | flops 1000000000 | bytes 4194304 | tf_op jit(solution)/shard_map/pallas_call | solution.py:500
  61.1 0.1 collective-permute-start.12
  61.2 1.7 %collective-permute-start.13 = (f32[256,256]{1,0:T(8,128)S(1)}, f32[256,256]{1,0:T(8,128)S(1)}, u32[]{:S(2)}, u32[]{:S(2)}) collective-permute-start(f32[256,256]{1,0:T(8,128)S(1)} %get-tuple-element.53), channel_id=1, source_target_pairs={{0,4},{1,3},{2,1},{3,2},{4,8},{5,7},{6,5},{7,6},{8,12},{9,11},{10,... | collective-permute-start | bytes 786440 | tf_op jit(solution)/shard_map/ppermute | solution.py:30
  62.9 0.0 collective-permute-done.10.nearer
  62.9 6.6 %collective-permute-done.12.first = f32[256,256]{1,0:T(8,128)S(1)} collective-permute-done((f32[256,256]{1,0:T(8,128)S(1)}, f32[256,256]{1,0:T(8,128)S(1)}, u32[]{:S(2)}, u32[]{:S(2)}) %collective-permute-start.12) | collective-permute-done | bytes 262176 | tf_op jit(solution)/shard_map/ppermute | solution.py:30
  69.5 0.0 collective-permute-done.13.second
  69.5 0.0 collective-permute-done.11.farther
  69.5 5.7 %shard_map.66 = (f32[2,6,128,128]{3,2,1,0:T(8,128)}, f32[2,6,128,128]{3,2,1,0:T(8,128)}) custom-call(s32[16]{0:T(128)S(1)} %pad_add_fusion.meta, f32[2,6,128,128]{3,2,1,0:T(8,128)S(1)} %get-tuple-element.32.z, bf16[2,128,1024]{2,1,0:T(8,128)(2,1)S(1)} %get-tuple-element.33.z_high, bf16[2,128,1024]{2,1,0:T(8,128)(2,1)S(1)} %get-tuple-element.34.z_low, ...), custom_call_target="tpu_custom_call" | custom-call | flops 4000000000 | bytes 4194304 | tf_op jit(solution)/shard_map/pallas_call | solution.py:500
  (6 shorter events, 0.0 us)
Async XLA Ops:
  2.9 11.1 %collective-permute-start = (f32[1,6,128,128]{3,2,1,0:T(8,128)}, f32[1,6,128,128]{3,2,1,0:T(8,128)S(1)}, u32[]{:S(2)}, u32[]{:S(2)}) collective-permute-start(f32[1,6,128,128]{3,2,1,0:T(8,128)} %get-tuple-element.28), channel_id=1, source_target_pairs={{0,1},{1,0},{2,3},{3,2},{4,5},{5,4},{6,7},{7,6},{8,9},{9,8},{10,11... | collective-permute-start | bytes 1179656 | tf_op jit(solution)/shard_map/ppermute | solution.py:30
  5.0 17.4 %collective-permute-start.1 = (f32[1,6,128,128]{3,2,1,0:T(8,128)}, f32[1,6,128,128]{3,2,1,0:T(8,128)S(1)}, u32[]{:S(2)}, u32[]{:S(2)}) collective-permute-start(f32[1,6,128,128]{3,2,1,0:T(8,128)} %get-tuple-element.29), channel_id=1, source_target_pairs={{0,1},{1,0},{2,3},{3,2},{4,5},{5,4},{6,7},{7,6},{8,9},{9,8},{10,11... | collective-permute-start | bytes 1179656 | tf_op jit(solution)/shard_map/ppermute | solution.py:30
  5.0 24.5 %collective-permute-start.4 = (f32[9,128,128]{2,1,0:T(8,128)S(1)}, f32[9,128,128]{2,1,0:T(8,128)S(1)}, u32[]{:S(2)}, u32[]{:S(2)}) collective-permute-start(f32[9,128,128]{2,1,0:T(8,128)S(1)} %get-tuple-element.30), channel_id=1, source_target_pairs={{0,2},{1,3},{2,0},{3,1},{4,6},{5,7},{6,4},{7,5},{8,10},{9,11},{10,... | collective-permute-start | bytes 1769480 | tf_op jit(solution)/shard_map/ppermute | solution.py:30
  5.9 23.5 %collective-permute-start.5 = (f32[9,128,128]{2,1,0:T(8,128)S(1)}, f32[9,128,128]{2,1,0:T(8,128)S(1)}, u32[]{:S(2)}, u32[]{:S(2)}) collective-permute-start(f32[9,128,128]{2,1,0:T(8,128)S(1)} %get-tuple-element.31), channel_id=1, source_target_pairs={{0,30},{1,31},{2,4},{3,5},{4,2},{5,3},{6,8},{7,9},{8,6},{9,7},{10,... | collective-permute-start | bytes 1769480 | tf_op jit(solution)/shard_map/ppermute | solution.py:30
  9.4 28.1 %collective-permute-start.6 = (f32[1,6,128,128]{3,2,1,0:T(8,128)}, f32[1,6,128,128]{3,2,1,0:T(8,128)S(1)}, u32[]{:S(2)}, u32[]{:S(2)}) collective-permute-start(f32[1,6,128,128]{3,2,1,0:T(8,128)} %constant_dynamic-slice_fusion), channel_id=1, source_target_pairs={{0,1},{1,0},{2,3},{3,2},{4,5},{5,4},{6,7},{7,6},{8,9},{9,8},{10,11... | collective-permute-start | bytes 1179656 | tf_op jit(solution)/shard_map/ppermute | solution.py:30
  14.0 15.5 %collective-permute-start.2 = (f32[1,6,128,128]{3,2,1,0:T(8,128)S(1)}, f32[1,6,128,128]{3,2,1,0:T(8,128)S(1)}, u32[]{:S(2)}, u32[]{:S(2)}) collective-permute-start(f32[1,6,128,128]{3,2,1,0:T(8,128)S(1)} %collective-permute-done.x0), channel_id=1, source_target_pairs={{0,2},{1,31},{2,4},{3,1},{4,6},{5,3},{6,8},{7,5},{8,10},{9,7},{10,... | collective-permute-start | bytes 1179656 | tf_op jit(solution)/shard_map/ppermute | solution.py:30
  22.4 8.5 %collective-permute-start.3 = (f32[1,6,128,128]{3,2,1,0:T(8,128)S(1)}, f32[1,6,128,128]{3,2,1,0:T(8,128)S(1)}, u32[]{:S(2)}, u32[]{:S(2)}) collective-permute-start(f32[1,6,128,128]{3,2,1,0:T(8,128)S(1)} %collective-permute-done.1.x1), channel_id=1, source_target_pairs={{0,2},{1,31},{2,4},{3,1},{4,6},{5,3},{6,8},{7,5},{8,10},{9,7},{10,... | collective-permute-start | bytes 1179656 | tf_op jit(solution)/shard_map/ppermute | solution.py:30
  33.8 10.3 %collective-permute-start.9 = (f32[1,6,128,128]{3,2,1,0:T(8,128)S(1)}, f32[1,6,128,128]{3,2,1,0:T(8,128)S(1)}, u32[]{:S(2)}, u32[]{:S(2)}) collective-permute-start(f32[1,6,128,128]{3,2,1,0:T(8,128)S(1)} %get-tuple-element.46), channel_id=1, source_target_pairs={{0,1},{1,0},{2,3},{3,2},{4,5},{5,4},{6,7},{7,6},{8,9},{9,8},{10,11... | collective-permute-start | bytes 1179656 | tf_op jit(solution)/shard_map/ppermute | solution.py:30
  36.1 14.3 %collective-permute-start.7 = (f32[7,128,128]{2,1,0:T(8,128)S(1)}, f32[7,128,128]{2,1,0:T(8,128)S(1)}, u32[]{:S(2)}, u32[]{:S(2)}) collective-permute-start(f32[7,128,128]{2,1,0:T(8,128)S(1)} %get-tuple-element.44), channel_id=1, source_target_pairs={{0,2},{1,3},{2,0},{3,1},{4,6},{5,7},{6,4},{7,5},{8,10},{9,11},{10,... | collective-permute-start | bytes 1376264 | tf_op jit(solution)/shard_map/ppermute | solution.py:30
  37.4 21.2 %collective-permute-start.8 = (f32[7,128,128]{2,1,0:T(8,128)S(1)}, f32[7,128,128]{2,1,0:T(8,128)S(1)}, u32[]{:S(2)}, u32[]{:S(2)}) collective-permute-start(f32[7,128,128]{2,1,0:T(8,128)S(1)} %get-tuple-element.45), channel_id=1, source_target_pairs={{0,30},{1,31},{2,4},{3,5},{4,2},{5,3},{6,8},{7,9},{8,6},{9,7},{10,... | collective-permute-start | bytes 1376264 | tf_op jit(solution)/shard_map/ppermute | solution.py:30
  39.9 23.0 %collective-permute-start.10 = (f32[1,6,128,128]{3,2,1,0:T(8,128)S(1)}, f32[1,6,128,128]{3,2,1,0:T(8,128)S(1)}, u32[]{:S(2)}, u32[]{:S(2)}) collective-permute-start(f32[1,6,128,128]{3,2,1,0:T(8,128)S(1)} %shard_map.60.after.nearer), channel_id=1, source_target_pairs={{0,2},{1,31},{2,4},{3,1},{4,6},{5,3},{6,8},{7,5},{8,10},{9,7},{10,... | collective-permute-start | bytes 1179656 | tf_op jit(solution)/shard_map/ppermute | solution.py:30
  44.1 25.5 %collective-permute-start.11 = (f32[1,6,128,128]{3,2,1,0:T(8,128)S(1)}, f32[1,6,128,128]{3,2,1,0:T(8,128)S(1)}, u32[]{:S(2)}, u32[]{:S(2)}) collective-permute-start(f32[1,6,128,128]{3,2,1,0:T(8,128)S(1)} %collective-permute-done.9.farther), channel_id=1, source_target_pairs={{0,2},{1,31},{2,4},{3,1},{4,6},{5,3},{6,8},{7,5},{8,10},{9,7},{10,... | collective-permute-start | bytes 1179656 | tf_op jit(solution)/shard_map/ppermute | solution.py:30
  61.1 8.4 %collective-permute-start.12 = (f32[256,256]{1,0:T(8,128)S(1)}, f32[256,256]{1,0:T(8,128)S(1)}, u32[]{:S(2)}, u32[]{:S(2)}) collective-permute-start(f32[256,256]{1,0:T(8,128)S(1)} %get-tuple-element.52), channel_id=1, source_target_pairs={{0,1},{1,2},{2,0},{3,31},{4,5},{5,6},{6,4},{7,3},{8,9},{9,10},{10,... | collective-permute-start | bytes 786440 | tf_op jit(solution)/shard_map/ppermute | solution.py:30
  61.2 8.4 %collective-permute-start.13 = (f32[256,256]{1,0:T(8,128)S(1)}, f32[256,256]{1,0:T(8,128)S(1)}, u32[]{:S(2)}, u32[]{:S(2)}) collective-permute-start(f32[256,256]{1,0:T(8,128)S(1)} %get-tuple-element.53), channel_id=1, source_target_pairs={{0,4},{1,3},{2,1},{3,2},{4,8},{5,7},{6,5},{7,6},{8,12},{9,11},{10,... | collective-permute-start | bytes 786440 | tf_op jit(solution)/shard_map/ppermute | solution.py:30

commit v9 on v8

--- a/solution.py
+++ b/solution.py
@@ -189,6 +189,36 @@
     return jnp.where(present, value, 0.0)
 
 
+def far_kernel(meta, t_up, t_down, t_far_up, t_far_down, pi, pc, nearer, farther, after, first, second, high, low):
+    tile = nearer.shape[-1]
+    rows = Rows(meta)
+
+    def block(turned, place, out, tile_of):
+        for r in range(2):
+            for c in range(2):
+                put(high, low, r, c, tile, tile_of(r, c))
+        out[...] = dot3(*halves(turned, place, place + 1, tile), flat(high, slice(None), slice(None)), flat(low, slice(None), slice(None)))
+
+    def swapped(sign):
+        return lambda r, c: far_tile(rows, (nearer, farther), sign, r, c, tile)
+
+    def from_down(r, c):
+        return rows.packed((pc, pi), UP, -4, r, c - 1) if c - 1 - (r - 4) <= REACH else zero(tile)
+
+    def from_up(r, c):
+        return rows.packed((pi, pc), DOWN, 4, r, c + 1) if r + 4 - (c + 1) <= REACH else zero(tile)
+
+    @pl.when(rows.even_pair)
+    def _():
+        block(t_up, 1, first, from_down)
+        block(t_far_up, 0, second, swapped(1))
+
+    @pl.when(jnp.logical_not(rows.even_pair))
+    def _():
+        block(t_far_down, 0, first, swapped(-1))
+        block(t_down, 0, second, from_up)
+
+
 def tiles_of(tile, columns=range(PAIRS)):
     for b in columns:
         for a in range(max(0, b - 2), min(PAIRS, b + 3)):
@@ -198,10 +228,9 @@
 
 
 def edge_kernel(
-    meta, t_up, t_down, t_far_up, t_far_down, pi, pc, nearer, farther, early, base, first, second,
-    high, low, far_high, far_low, edge,
+    meta, t_up, t_down, pi, pc, early, base, high, low, edge,
 ):
-    tile = nearer.shape[-1]
+    tile = pi.shape[-1]
     rows = Rows(meta)
     for r in range(2):
         for c in range(4):
@@ -218,23 +247,6 @@
         )
         for e in range(2):
             edge[2 * b + e] = block[2 * e * tile : (2 * e + 2) * tile]
-
-    def far_block(turned, sign, out):
-        for r in range(2):
-            for c in range(2):
-                put(far_high, far_low, r, c, tile, far_tile(rows, (nearer, farther), sign, r, c, tile))
-        whole = slice(None), slice(None)
-        out[...] = dot3(*halves(turned, 0, 1, tile), flat(far_high, *whole), flat(far_low, *whole))
-
-    @pl.when(rows.even_pair)
-    def _():
-        first[...] = edge[3]
-        far_block(t_far_up, 1, second)
-
-    @pl.when(jnp.logical_not(rows.even_pair))
-    def _():
-        far_block(t_far_down, -1, first)
-        second[...] = edge[4]
 
     eye = (
         lax.broadcasted_iota(jnp.int32, (tile, tile), 0) == lax.broadcasted_iota(jnp.int32, (tile, tile), 1)
@@ -567,14 +579,21 @@
         halves_of(2, COLS) + halves_of(2, 2 * SIDE),
         int(4e9),
     )
-    base, *far = call(
+    far = call(
+        far_kernel,
+        (meta, t_up, t_down, t_far_up, t_far_down, pi, pc, ps, px, early),
+        (block, block),
+        halves_of(2, 2),
+        int(1e8),
+    )
+    far = (send(far[0], far_first), send(far[1], far_second))
+    base = call(
         edge_kernel,
-        (meta, t_up, t_down, t_far_up, t_far_down, pi, pc, ps, px, early),
-        (shape(PAIRS * PAIRS, 2 * tile, 2 * tile), block, block),
-        halves_of(2, COLS) + halves_of(2, 2) + [pltpu.VMEM((2 * PAIRS, 2 * tile, 2 * tile), F32)],
+        (meta, t_up, t_down, pi, pc, early),
+        shape(PAIRS * PAIRS, 2 * tile, 2 * tile),
+        halves_of(2, COLS) + [pltpu.VMEM((2 * PAIRS, 2 * tile, 2 * tile), F32)],
         int(1e9),
     )
-    far = (send(far[0], far_first), send(far[1], far_second))
     return call(
         refine_kernel,
         (meta, z_kept, *z_own, t_near, base, *pn, *far),

time: 76.1 us -> 74.7 us (0.982)
  waiting for transfers between devices: 21.7 us -> 19.9 us
    ppermute x14, waiting for transfers between devices: 21.7 us -> 19.9 us  [send(): return lax.ppermute(value, AXES, [(i, to(i) % count) for i in range(count)])]
    pallas_call x8 -> x9, Pallas kernels: 23.5 us -> 24 us  [call(): pl.pallas_call(kernel, in_specs=[smem] * scalars + [vmem] * (len(ins) - s...]
  transfers between devices with their start and end apart: 14 -> 14, of which waited for: 5 -> 5; matrix products, arithmetic and copies ran while one was open for 7% -> 7% of each run, Pallas kernels for 21% -> 22%
where the time goes in v9:
time: 74.7 us; the launch traced here: 74 us
  Pallas kernels  24 us (32%)
  starting transfers between devices  23.6 us (32%)
  waiting for transfers between devices  19.9 us (27%)
  local copies, waits for them, and re-layouts  4.56 us (6%)
  between operations  0.98 us (1%)
  other arithmetic  0.95 us (1%)
    pallas_call x9, Pallas kernels, call(): pl.pallas_call(kernel, in_specs=[smem] * scalars + [vmem] * (len(ins) - s...  24 us
    ppermute x14, starting transfers between devices, send(): return lax.ppermute(value, AXES, [(i, to(i) % count) for i in range(count)])  23.6 us
    ppermute x14, waiting for transfers between devices, send(): return lax.ppermute(value, AXES, [(i, to(i) % count) for i in range(count)])  19.9 us
    dynamic_slice x1, local copies, waits for them, and re-layouts, body(): sx = send(lax.dynamic_slice_in_dim(correlation, 1 - device % 2, 1, 0), swap)  1.78 us
  transfers between devices with their start and end apart: 14, of which 5 were waited for; matrix products, arithmetic and copies ran while one was open for 7% of the time, Pallas kernels for 22%

profile of v9, /device:TPU:1, one launch (start us, length us, event | category | flops | bytes accessed | tf_op | source)
XLA Modules:
  0.0 74.0 jit_solution(17915636535188496441)
XLA Ops:
  0.7 0.1 stack.2.meta
  0.8 2.1 %shard_map.59 = (f32[1,6,128,128]{3,2,1,0:T(8,128)}, f32[1,6,128,128]{3,2,1,0:T(8,128)}, f32[9,128,128]{2,1,0:T(8,128)S(1)}, f32[9,128,128]{2,1,0:T(8,128)S(1)}) custom-call(s32[16]{0:T(128)S(1)} %stack.2.meta, f32[2,6,128,128]{3,2,1,0:T(8,128)} %z.7), custom_call_target="tpu_custom_call" | custom-call | flops 1000 | bytes 4194304 | tf_op jit(solution)/shard_map/pallas_call | solution.py:512
  2.9 2.0 %collective-permute-start = (f32[1,6,128,128]{3,2,1,0:T(8,128)}, f32[1,6,128,128]{3,2,1,0:T(8,128)S(1)}, u32[]{:S(2)}, u32[]{:S(2)}) collective-permute-start(f32[1,6,128,128]{3,2,1,0:T(8,128)} %get-tuple-element.27), channel_id=1, source_target_pairs={{0,1},{1,0},{2,3},{3,2},{4,5},{5,4},{6,7},{7,6},{8,9},{9,8},{10,11... | collective-permute-start | bytes 1179656 | tf_op jit(solution)/shard_map/ppermute | solution.py:30
  5.0 0.0 collective-permute-start.1
  5.0 1.0 %collective-permute-start.4 = (f32[9,128,128]{2,1,0:T(8,128)S(1)}, f32[9,128,128]{2,1,0:T(8,128)S(1)}, u32[]{:S(2)}, u32[]{:S(2)}) collective-permute-start(f32[9,128,128]{2,1,0:T(8,128)S(1)} %get-tuple-element.29), channel_id=1, source_target_pairs={{0,2},{1,3},{2,0},{3,1},{4,6},{5,7},{6,4},{7,5},{8,10},{9,11},{10,... | collective-permute-start | bytes 1769480 | tf_op jit(solution)/shard_map/ppermute | solution.py:30
  5.9 1.6 %collective-permute-start.5 = (f32[9,128,128]{2,1,0:T(8,128)S(1)}, f32[9,128,128]{2,1,0:T(8,128)S(1)}, u32[]{:S(2)}, u32[]{:S(2)}) collective-permute-start(f32[9,128,128]{2,1,0:T(8,128)S(1)} %get-tuple-element.30), channel_id=1, source_target_pairs={{0,30},{1,31},{2,4},{3,5},{4,2},{5,3},{6,8},{7,9},{8,6},{9,7},{10,... | collective-permute-start | bytes 1769480 | tf_op jit(solution)/shard_map/ppermute | solution.py:30
  7.6 1.8 %constant_dynamic-slice_fusion = f32[1,6,128,128]{3,2,1,0:T(8,128)} fusion(f32[2,6,128,128]{3,2,1,0:T(8,128)} %s.1, s32[]{:T(128)S(6)} %select_n.66), kind=kLoop, calls=%fused_computation.22 | loop fusion | bytes 786436 | tf_op jit(solution)/shard_map/dynamic_slice | solution.py:539
  9.4 1.2 %collective-permute-start.6 = (f32[1,6,128,128]{3,2,1,0:T(8,128)}, f32[1,6,128,128]{3,2,1,0:T(8,128)S(1)}, u32[]{:S(2)}, u32[]{:S(2)}) collective-permute-start(f32[1,6,128,128]{3,2,1,0:T(8,128)} %constant_dynamic-slice_fusion), channel_id=1, source_target_pairs={{0,1},{1,0},{2,3},{3,2},{4,5},{5,4},{6,7},{7,6},{8,9},{9,8},{10,11... | collective-permute-start | bytes 1179656 | tf_op jit(solution)/shard_map/ppermute | solution.py:30
  10.6 1.4 %copy.8 = s32[64,6]{1,0:T(8,128)} copy(s32[64,6]{0,1:T(8,128)} %param.6) | data formatting | bytes 3072 | tf_op args[2]
  12.0 1.3 %gather_fusion = s32[14,6]{1,0:T(8,128)S(1)} fusion(s32[64,6]{1,0:T(8,128)} %copy.8, s32[1024]{0:T(1024)S(1)} %pad_clamp_fusion), kind=kCustom, calls=%fused_computation | custom fusion | bytes 728 | tf_op jit(solution)/shard_map/gather | solution.py:496
  13.3 0.7 collective-permute-done.x0
  14.0 3.8 %collective-permute-start.2 = (f32[1,6,128,128]{3,2,1,0:T(8,128)S(1)}, f32[1,6,128,128]{3,2,1,0:T(8,128)S(1)}, u32[]{:S(2)}, u32[]{:S(2)}) collective-permute-start(f32[1,6,128,128]{3,2,1,0:T(8,128)S(1)} %collective-permute-done.x0), channel_id=1, source_target_pairs={{0,2},{1,31},{2,4},{3,1},{4,6},{5,3},{6,8},{7,5},{8,10},{9,7},{10,... | collective-permute-start | bytes 1179656 | tf_op jit(solution)/shard_map/ppermute | solution.py:30
  17.8 4.7 %collective-permute-done.1.x1 = f32[1,6,128,128]{3,2,1,0:T(8,128)S(1)} collective-permute-done((f32[1,6,128,128]{3,2,1,0:T(8,128)}, f32[1,6,128,128]{3,2,1,0:T(8,128)S(1)}, u32[]{:S(2)}, u32[]{:S(2)}) %collective-permute-start.1) | collective-permute-done | bytes 393248 | tf_op jit(solution)/shard_map/ppermute | solution.py:30
  22.4 3.8 %collective-permute-start.3 = (f32[1,6,128,128]{3,2,1,0:T(8,128)S(1)}, f32[1,6,128,128]{3,2,1,0:T(8,128)S(1)}, u32[]{:S(2)}, u32[]{:S(2)}) collective-permute-start(f32[1,6,128,128]{3,2,1,0:T(8,128)S(1)} %collective-permute-done.1.x1), channel_id=1, source_target_pairs={{0,2},{1,31},{2,4},{3,1},{4,6},{5,3},{6,8},{7,5},{8,10},{9,7},{10,... | collective-permute-start | bytes 1179656 | tf_op jit(solution)/shard_map/ppermute | solution.py:30
  26.2 0.8 %convert_reduce_fusion = s32[14]{0:T(128)S(1)} fusion(s32[14,6]{1,0:T(8,128)S(1)} %gather_fusion, s32[5]{0:T(128)} %constant.83.clone, s32[14]{0:T(128)S(1)} %and_select_fusion), kind=kLoop, calls=%fused_computation.9 | loop fusion | flops 1176 | bytes 412 | tf_op jit(solution)/shard_map/reduce_sum | solution.py:498
  27.0 0.1 pad_add_fusion.meta
  27.1 2.3 %shard_map.62 = (bf16[8,128,1024]{2,1,0:T(8,128)(2,1)S(1)}, bf16[8,128,1024]{2,1,0:T(8,128)(2,1)S(1)}, bf16[2,128,1024]{2,1,0:T(8,128)(2,1)S(1)}, bf16[2,128,1024]{2,1,0:T(8,128)(2,1)S(1)}) custom-call(s32[16]{0:T(128)S(1)} %pad_add_fusion.meta, f32[2,6,128,128]{3,2,1,0:T(8,128)} %s.1, f32[2,6,128,128]{3,2,1,0:T(8,128)} %z.7, ...), custom_call_target="tpu_custom_call" | custom-call | flops 1000000000 | bytes 4194304 | tf_op jit(solution)/shard_map/pallas_call | solution.py:512
  29.5 0.0 collective-permute-done.4.zi
  29.5 0.0 collective-permute-done.5.zc
  29.5 0.0 collective-permute-done.2.n0
  29.5 1.4 %collective-permute-done.3.n1 = f32[1,6,128,128]{3,2,1,0:T(8,128)S(1)} collective-permute-done((f32[1,6,128,128]{3,2,1,0:T(8,128)S(1)}, f32[1,6,128,128]{3,2,1,0:T(8,128)S(1)}, u32[]{:S(2)}, u32[]{:S(2)}) %collective-permute-start.3) | collective-permute-done | bytes 393248 | tf_op jit(solution)/shard_map/ppermute | solution.py:30
  30.9 2.9 %shard_map.63 = (f32[1,6,128,128]{3,2,1,0:T(8,128)S(1)}, f32[1,6,128,128]{3,2,1,0:T(8,128)S(1)}, f32[1,6,128,128]{3,2,1,0:T(8,128)S(1)}, f32[7,128,128]{2,1,0:T(...) custom-call(s32[16]{0:T(128)S(1)} %pad_add_fusion.meta, ...), custom_call_target="tpu_custom_call", output_to_operand_aliasing={{5}: (1, {}), {6}: (2, {})} | custom-call | flops 2000000000 | bytes 4194304 | tf_op jit(solution)/shard_map/pallas_call | solution.py:512
  33.8 2.3 %collective-permute-start.9 = (f32[1,6,128,128]{3,2,1,0:T(8,128)S(1)}, f32[1,6,128,128]{3,2,1,0:T(8,128)S(1)}, u32[]{:S(2)}, u32[]{:S(2)}) collective-permute-start(f32[1,6,128,128]{3,2,1,0:T(8,128)S(1)} %get-tuple-element.47), channel_id=1, source_target_pairs={{0,1},{1,0},{2,3},{3,2},{4,5},{5,4},{6,7},{7,6},{8,9},{9,8},{10,11... | collective-permute-start | bytes 1179656 | tf_op jit(solution)/shard_map/ppermute | solution.py:30
  36.1 1.3 %collective-permute-start.7 = (f32[7,128,128]{2,1,0:T(8,128)S(1)}, f32[7,128,128]{2,1,0:T(8,128)S(1)}, u32[]{:S(2)}, u32[]{:S(2)}) collective-permute-start(f32[7,128,128]{2,1,0:T(8,128)S(1)} %get-tuple-element.41), channel_id=1, source_target_pairs={{0,2},{1,3},{2,0},{3,1},{4,6},{5,7},{6,4},{7,5},{8,10},{9,11},{10,... | collective-permute-start | bytes 1376264 | tf_op jit(solution)/shard_map/ppermute | solution.py:30
  37.4 0.0 collective-permute-start.8
  37.4 0.0 collective-permute-done.6.s
  37.5 2.5 %shard_map.60.after.nearer = f32[1,6,128,128]{3,2,1,0:T(8,128)S(1)} custom-call(s32[16]{0:T(128)S(1)} %pad_add_fusion.meta, f32[1,6,128,128]{3,2,1,0:T(8,128)S(1)} %collective-permute-done.6.s, f32[2,6,128,128]{3,2,1,0:T(8,128)} %z.7, f32[1,6,128,128]{3,2,1,0:T(8,128)S(1)} %collective-permute-done.x0, f32[1,6,128,128]{3,2,1,0:T(8,128)S(1)} %collective-permute-done.1.x1, ...), custom_call_target="tpu_custom_call" | custom-call | flops 2000000000 | bytes 4194304 | tf_op jit(solution)/shard_map/pallas_call | solution.py:512
  39.9 1.8 %collective-permute-start.10 = (f32[1,6,128,128]{3,2,1,0:T(8,128)S(1)}, f32[1,6,128,128]{3,2,1,0:T(8,128)S(1)}, u32[]{:S(2)}, u32[]{:S(2)}) collective-permute-start(f32[1,6,128,128]{3,2,1,0:T(8,128)S(1)} %shard_map.60.after.nearer), channel_id=1, source_target_pairs={{0,2},{1,31},{2,4},{3,1},{4,6},{5,3},{6,8},{7,5},{8,10},{9,7},{10,... | collective-permute-start | bytes 1179656 | tf_op jit(solution)/shard_map/ppermute | solution.py:30
  41.7 2.3 %shard_map.61 = (f32[2,6,128,128]{3,2,1,0:T(8,128)S(1)}, bf16[1024,512]{1,0:T(8,128)(2,1)S(1)}, bf16[512,512]{1,0:T(8,128)(2,1)S(1)}, bf16[512,512]{1,0:T(8,128)...) custom-call(s32[16]{0:T(128)S(1)} %pad_add_fusion.meta, ...), custom_call_target="tpu_custom_call" | custom-call | flops 2000000000 | bytes 4194304 | tf_op jit(solution)/shard_map/pallas_call | solution.py:512
  44.0 0.0 collective-permute-done.9.farther
  44.1 2.9 %collective-permute-start.11 = (f32[1,6,128,128]{3,2,1,0:T(8,128)S(1)}, f32[1,6,128,128]{3,2,1,0:T(8,128)S(1)}, u32[]{:S(2)}, u32[]{:S(2)}) collective-permute-start(f32[1,6,128,128]{3,2,1,0:T(8,128)S(1)} %collective-permute-done.9.farther), channel_id=1, source_target_pairs={{0,2},{1,31},{2,4},{3,1},{4,6},{5,3},{6,8},{7,5},{8,10},{9,7},{10,... | collective-permute-start | bytes 1179656 | tf_op jit(solution)/shard_map/ppermute | solution.py:30
  47.0 3.4 %shard_map.64.early.after = f32[16,256,256]{2,1,0:T(8,128)S(1)} custom-call(s32[16]{0:T(128)S(1)} %pad_add_fusion.meta, bf16[1024,512]{1,0:T(8,128)(2,1)S(1)} %get-tuple-element.43.t_own, bf16[768,512]{1,0:T(8,128)(2,1)S(1)} %get-tuple-element.44.t_swap, f32[1,6,128,128]{3,2,1,0:T(8,128)S(1)} %get-tuple-element.45.p0, ...), custom_call_target="tpu_custom_call" | custom-call | flops 4000000000 | bytes 4194304 | tf_op jit(solution)/shard_map/pallas_call | solution.py:512
  50.4 0.0 collective-permute-done.7.pi
  50.4 8.3 %collective-permute-done.8.pc = f32[7,128,128]{2,1,0:T(8,128)S(1)} collective-permute-done((f32[7,128,128]{2,1,0:T(8,128)S(1)}, f32[7,128,128]{2,1,0:T(8,128)S(1)}, u32[]{:S(2)}, u32[]{:S(2)}) %collective-permute-start.8) | collective-permute-done | bytes 458784 | tf_op jit(solution)/shard_map/ppermute | solution.py:30
  58.7 1.0 %shard_map.66 = (f32[256,256]{1,0:T(8,128)S(1)}, f32[256,256]{1,0:T(8,128)S(1)}) custom-call(s32[16]{0:T(128)S(1)} %pad_add_fusion.meta, bf16[512,512]{1,0:T(8,128)(2,1)S(1)} %get-tuple-element.35.t_up, bf16[512,512]{1,0:T(8,128)(2,1)S(1)} %get-tuple-element.36.t_down, bf16[256,512]{1,0:T(8,128)(2,1)S(1)} %get-tuple-element.48.t_far_up, ...), custom_call_target="tpu_custom_call" | custom-call | flops 100000000 | bytes 4194304 | tf_op jit(solution)/shard_map/pallas_call | solution.py:512
  59.7 0.1 collective-permute-start.12
  59.8 1.7 %collective-permute-start.13 = (f32[256,256]{1,0:T(8,128)S(1)}, f32[256,256]{1,0:T(8,128)S(1)}, u32[]{:S(2)}, u32[]{:S(2)}) collective-permute-start(f32[256,256]{1,0:T(8,128)S(1)} %get-tuple-element.51), channel_id=1, source_target_pairs={{0,4},{1,3},{2,1},{3,2},{4,8},{5,7},{6,5},{7,6},{8,12},{9,11},{10,... | collective-permute-start | bytes 786440 | tf_op jit(solution)/shard_map/ppermute | solution.py:30
  61.5 1.8 %shard_map.65.base = f32[16,256,256]{2,1,0:T(8,128)S(1)} custom-call(s32[16]{0:T(128)S(1)} %pad_add_fusion.meta, bf16[512,512]{1,0:T(8,128)(2,1)S(1)} %get-tuple-element.35.t_up, bf16[512,512]{1,0:T(8,128)(2,1)S(1)} %get-tuple-element.36.t_down, f32[7,128,128]{2,1,0:T(8,128)S(1)} %collective-permute-done.7.pi, f32[7,128,128]{2,1,0:T(8,128)S(1)} %collective-permute-done.8.pc, ...), custom_call_target="tpu_custom_call" | custom-call | flops 1000000000 | bytes 4194304 | tf_op jit(solution)/shard_map/pallas_call | solution.py:512
  63.3 0.0 collective-permute-done.10.nearer
  63.3 4.8 %collective-permute-done.12.first = f32[256,256]{1,0:T(8,128)S(1)} collective-permute-done((f32[256,256]{1,0:T(8,128)S(1)}, f32[256,256]{1,0:T(8,128)S(1)}, u32[]{:S(2)}, u32[]{:S(2)}) %collective-permute-start.12) | collective-permute-done | bytes 262176 | tf_op jit(solution)/shard_map/ppermute | solution.py:30
  68.1 0.0 collective-permute-done.13.second
  68.1 0.0 collective-permute-done.11.farther
  68.1 5.7 %shard_map.67 = (f32[2,6,128,128]{3,2,1,0:T(8,128)}, f32[2,6,128,128]{3,2,1,0:T(8,128)}) custom-call(s32[16]{0:T(128)S(1)} %pad_add_fusion.meta, f32[2,6,128,128]{3,2,1,0:T(8,128)S(1)} %get-tuple-element.31.z, bf16[2,128,1024]{2,1,0:T(8,128)(2,1)S(1)} %get-tuple-element.32.z_high, bf16[2,128,1024]{2,1,0:T(8,128)(2,1)S(1)} %get-tuple-element.33.z_low, ...), custom_call_target="tpu_custom_call" | custom-call | flops 4000000000 | bytes 4194304 | tf_op jit(solution)/shard_map/pallas_call | solution.py:512
  (6 shorter events, 0.0 us)
Async XLA Ops:
  2.9 11.1 %collective-permute-start = (f32[1,6,128,128]{3,2,1,0:T(8,128)}, f32[1,6,128,128]{3,2,1,0:T(8,128)S(1)}, u32[]{:S(2)}, u32[]{:S(2)}) collective-permute-start(f32[1,6,128,128]{3,2,1,0:T(8,128)} %get-tuple-element.27), channel_id=1, source_target_pairs={{0,1},{1,0},{2,3},{3,2},{4,5},{5,4},{6,7},{7,6},{8,9},{9,8},{10,11... | collective-permute-start | bytes 1179656 | tf_op jit(solution)/shard_map/ppermute | solution.py:30
  5.0 17.4 %collective-permute-start.1 = (f32[1,6,128,128]{3,2,1,0:T(8,128)}, f32[1,6,128,128]{3,2,1,0:T(8,128)S(1)}, u32[]{:S(2)}, u32[]{:S(2)}) collective-permute-start(f32[1,6,128,128]{3,2,1,0:T(8,128)} %get-tuple-element.28), channel_id=1, source_target_pairs={{0,1},{1,0},{2,3},{3,2},{4,5},{5,4},{6,7},{7,6},{8,9},{9,8},{10,11... | collective-permute-start | bytes 1179656 | tf_op jit(solution)/shard_map/ppermute | solution.py:30
  5.0 24.5 %collective-permute-start.4 = (f32[9,128,128]{2,1,0:T(8,128)S(1)}, f32[9,128,128]{2,1,0:T(8,128)S(1)}, u32[]{:S(2)}, u32[]{:S(2)}) collective-permute-start(f32[9,128,128]{2,1,0:T(8,128)S(1)} %get-tuple-element.29), channel_id=1, source_target_pairs={{0,2},{1,3},{2,0},{3,1},{4,6},{5,7},{6,4},{7,5},{8,10},{9,11},{10,... | collective-permute-start | bytes 1769480 | tf_op jit(solution)/shard_map/ppermute | solution.py:30
  5.9 23.5 %collective-permute-start.5 = (f32[9,128,128]{2,1,0:T(8,128)S(1)}, f32[9,128,128]{2,1,0:T(8,128)S(1)}, u32[]{:S(2)}, u32[]{:S(2)}) collective-permute-start(f32[9,128,128]{2,1,0:T(8,128)S(1)} %get-tuple-element.30), channel_id=1, source_target_pairs={{0,30},{1,31},{2,4},{3,5},{4,2},{5,3},{6,8},{7,9},{8,6},{9,7},{10,... | collective-permute-start | bytes 1769480 | tf_op jit(solution)/shard_map/ppermute | solution.py:30
  9.4 28.1 %collective-permute-start.6 = (f32[1,6,128,128]{3,2,1,0:T(8,128)}, f32[1,6,128,128]{3,2,1,0:T(8,128)S(1)}, u32[]{:S(2)}, u32[]{:S(2)}) collective-permute-start(f32[1,6,128,128]{3,2,1,0:T(8,128)} %constant_dynamic-slice_fusion), channel_id=1, source_target_pairs={{0,1},{1,0},{2,3},{3,2},{4,5},{5,4},{6,7},{7,6},{8,9},{9,8},{10,11... | collective-permute-start | bytes 1179656 | tf_op jit(solution)/shard_map/ppermute | solution.py:30
  14.0 15.5 %collective-permute-start.2 = (f32[1,6,128,128]{3,2,1,0:T(8,128)S(1)}, f32[1,6,128,128]{3,2,1,0:T(8,128)S(1)}, u32[]{:S(2)}, u32[]{:S(2)}) collective-permute-start(f32[1,6,128,128]{3,2,1,0:T(8,128)S(1)} %collective-permute-done.x0), channel_id=1, source_target_pairs={{0,2},{1,31},{2,4},{3,1},{4,6},{5,3},{6,8},{7,5},{8,10},{9,7},{10,... | collective-permute-start | bytes 1179656 | tf_op jit(solution)/shard_map/ppermute | solution.py:30
  22.4 8.5 %collective-permute-start.3 = (f32[1,6,128,128]{3,2,1,0:T(8,128)S(1)}, f32[1,6,128,128]{3,2,1,0:T(8,128)S(1)}, u32[]{:S(2)}, u32[]{:S(2)}) collective-permute-start(f32[1,6,128,128]{3,2,1,0:T(8,128)S(1)} %collective-permute-done.1.x1), channel_id=1, source_target_pairs={{0,2},{1,31},{2,4},{3,1},{4,6},{5,3},{6,8},{7,5},{8,10},{9,7},{10,... | collective-permute-start | bytes 1179656 | tf_op jit(solution)/shard_map/ppermute | solution.py:30
  33.8 10.3 %collective-permute-start.9 = (f32[1,6,128,128]{3,2,1,0:T(8,128)S(1)}, f32[1,6,128,128]{3,2,1,0:T(8,128)S(1)}, u32[]{:S(2)}, u32[]{:S(2)}) collective-permute-start(f32[1,6,128,128]{3,2,1,0:T(8,128)S(1)} %get-tuple-element.47), channel_id=1, source_target_pairs={{0,1},{1,0},{2,3},{3,2},{4,5},{5,4},{6,7},{7,6},{8,9},{9,8},{10,11... | collective-permute-start | bytes 1179656 | tf_op jit(solution)/shard_map/ppermute | solution.py:30
  36.1 14.3 %collective-permute-start.7 = (f32[7,128,128]{2,1,0:T(8,128)S(1)}, f32[7,128,128]{2,1,0:T(8,128)S(1)}, u32[]{:S(2)}, u32[]{:S(2)}) collective-permute-start(f32[7,128,128]{2,1,0:T(8,128)S(1)} %get-tuple-element.41), channel_id=1, source_target_pairs={{0,2},{1,3},{2,0},{3,1},{4,6},{5,7},{6,4},{7,5},{8,10},{9,11},{10,... | collective-permute-start | bytes 1376264 | tf_op jit(solution)/shard_map/ppermute | solution.py:30
  37.4 21.2 %collective-permute-start.8 = (f32[7,128,128]{2,1,0:T(8,128)S(1)}, f32[7,128,128]{2,1,0:T(8,128)S(1)}, u32[]{:S(2)}, u32[]{:S(2)}) collective-permute-start(f32[7,128,128]{2,1,0:T(8,128)S(1)} %get-tuple-element.42), channel_id=1, source_target_pairs={{0,30},{1,31},{2,4},{3,5},{4,2},{5,3},{6,8},{7,9},{8,6},{9,7},{10,... | collective-permute-start | bytes 1376264 | tf_op jit(solution)/shard_map/ppermute | solution.py:30
  39.9 23.4 %collective-permute-start.10 = (f32[1,6,128,128]{3,2,1,0:T(8,128)S(1)}, f32[1,6,128,128]{3,2,1,0:T(8,128)S(1)}, u32[]{:S(2)}, u32[]{:S(2)}) collective-permute-start(f32[1,6,128,128]{3,2,1,0:T(8,128)S(1)} %shard_map.60.after.nearer), channel_id=1, source_target_pairs={{0,2},{1,31},{2,4},{3,1},{4,6},{5,3},{6,8},{7,5},{8,10},{9,7},{10,... | collective-permute-start | bytes 1179656 | tf_op jit(solution)/shard_map/ppermute | solution.py:30
  44.1 24.1 %collective-permute-start.11 = (f32[1,6,128,128]{3,2,1,0:T(8,128)S(1)}, f32[1,6,128,128]{3,2,1,0:T(8,128)S(1)}, u32[]{:S(2)}, u32[]{:S(2)}) collective-permute-start(f32[1,6,128,128]{3,2,1,0:T(8,128)S(1)} %collective-permute-done.9.farther), channel_id=1, source_target_pairs={{0,2},{1,31},{2,4},{3,1},{4,6},{5,3},{6,8},{7,5},{8,10},{9,7},{10,... | collective-permute-start | bytes 1179656 | tf_op jit(solution)/shard_map/ppermute | solution.py:30
  59.7 8.4 %collective-permute-start.12 = (f32[256,256]{1,0:T(8,128)S(1)}, f32[256,256]{1,0:T(8,128)S(1)}, u32[]{:S(2)}, u32[]{:S(2)}) collective-permute-start(f32[256,256]{1,0:T(8,128)S(1)} %get-tuple-element.50), channel_id=1, source_target_pairs={{0,1},{1,2},{2,0},{3,31},{4,5},{5,6},{6,4},{7,3},{8,9},{9,10},{10,... | collective-permute-start | bytes 786440 | tf_op jit(solution)/shard_map/ppermute | solution.py:30
  59.8 8.4 %collective-permute-start.13 = (f32[256,256]{1,0:T(8,128)S(1)}, f32[256,256]{1,0:T(8,128)S(1)}, u32[]{:S(2)}, u32[]{:S(2)}) collective-permute-start(f32[256,256]{1,0:T(8,128)S(1)} %get-tuple-element.51), channel_id=1, source_target_pairs={{0,4},{1,3},{2,1},{3,2},{4,8},{5,7},{6,5},{7,6},{8,12},{9,11},{10,... | collective-permute-start | bytes 786440 | tf_op jit(solution)/shard_map/ppermute | solution.py:30
